TPU v7x, 32 devices: a whole 2x2x4 slice. The times are simulated.
32 devices in a mesh: tm: 16 (over z, y, core), band: 2 (over x).
Axes of the slice: x: 2, y: 2, z: 4, core: 2. Of those that a mesh axis runs over, the one named last changes fastest.
Arguments:
- phonon: float32 [32, 256, 256], P('tm', 'band'), may hold values from -4 to 4
- momentum: float32 [32, 256, 256], P('tm', 'band'), may hold values from -6 to 6
- source: float32 [32, 256, 256], P('tm', 'band'), may hold values from -6 to 6
- guess: float32 [32, 256, 256], P('tm', 'band'), may hold values from -4 to 4
- bonds: int32 [2, 256, 256], P(None, 'band'), may hold values 0 or 1
Outputs:
- solution: float32 [32, 256, 256], P('tm', 'band')
- momentum_new: float32 [32, 256, 256], P('tm', 'band')
All inputs are finite; a program needn't handle non-finite values. No bound on the sum of `bonds` on one device may be relied on, other than what follows from the above.
Results may differ from a plain program's by a relative error of at most 0.000064.
Values sent between devices are 32-bit elements; how exact they have to be, the bound alone decides.
No kernel may reach another device: no remote copies, remote signals or barrier semaphores. Data moves between devices by JAX's collectives and lax.ppermute only.
A program may use at most 64 MiB of HBM per device.

v0:
```python
import math

import jax
import jax.numpy as jnp
from jax import lax
from jax.sharding import PartitionSpec as P

ORDER = 24


hop_angle = 0.3
coupling = 0.2
stiffness = 1.0
mass_term = 0.5
relaxation = 0.25
step_size = 0.25
cheb_base = 4.03
cheb_slope = 0.5
half_width = 4.0
deep_width = 4


def extended(value, sides, width):
    for axis, dim in sides:
        size, length = (lax.axis_size(axis), value.shape[dim])
        up = [(i, (i + 1) % size) for i in range(size)]
        down = [(j, i) for i, j in up]
        last = lax.slice_in_dim(value, length - width, length, axis=dim)
        leading = lax.slice_in_dim(value, 0, width, axis=dim)
        before = lax.ppermute(last, axis, up)
        after = lax.ppermute(leading, axis, down)
        value = jnp.concatenate([before, value, after], axis=dim)
    return value


def passed_along(value, axis, by):
    size = lax.axis_size(axis)
    return lax.ppermute(value, axis, [(i, (i + by) % size) for i in range(size)])


def dft_basis(length_total):
    rows = lax.broadcasted_iota(jnp.int32, (length_total, length_total), 0)
    columns = lax.broadcasted_iota(jnp.int32, (length_total, length_total), 1)
    phase = (2 * (rows // 2) + 1) * columns % (2 * length_total)
    angle = phase.astype(jnp.float32) * (math.pi / length_total)
    return math.sqrt(2.0 / length_total) * jnp.where(rows % 2 == 0, jnp.cos(angle), jnp.sin(angle))


def cheb_centre(index, length_total):
    angle = (2 * (index // 2) + 1).astype(jnp.float32) * (math.pi / length_total)
    return cheb_base + cheb_slope * (1.0 - jnp.cos(angle))


def pair_tables(horizontal, vertical, vertical_prev, row_even, column_even):
    horizontal_prev = jnp.roll(horizontal, 1, 1)
    vertical_up = jnp.roll(vertical, 1, 0)
    strengths = (
        jnp.where(column_even, horizontal, horizontal_prev),
        jnp.where(column_even, horizontal_prev, horizontal),
        jnp.where(row_even, vertical, vertical_up),
        jnp.where(row_even, vertical_prev, vertical),
    )
    return tuple(
        ((jnp.cosh(hop_angle * strength), jnp.sinh(hop_angle * strength)) for strength in strengths)
    )


def partner_of(vector, colour, row_even, column_even):
    if colour == 0:
        return jnp.where(column_even, jnp.roll(vector, -1, 2), jnp.roll(vector, 1, 2))
    if colour == 1:
        return jnp.where(column_even, jnp.roll(vector, 1, 2), jnp.roll(vector, -1, 2))
    if colour == 2:
        return jnp.where(row_even, jnp.roll(vector, -1, 1), jnp.roll(vector, 1, 1))
    padded = extended(vector, (("band", 1),), 1)
    return jnp.where(row_even, padded[:, :-2], padded[:, 2:])


def to_spectrum(piece):
    basis = dft_basis(piece.shape[0])
    return jnp.einsum("kl,lrc->krc", basis, piece, precision=lax.Precision.HIGHEST)


def to_slices(piece):
    basis = dft_basis(piece.shape[0])
    return jnp.einsum("kl,krc->lrc", basis, piece, precision=lax.Precision.HIGHEST)


def shards(phonon, momentum, source, guess, bonds):
    slice_count, row_count, col_count = guess.shape
    cycle_size = lax.axis_size("tm")
    position = lax.axis_index("tm")
    grid_shape = (row_count, col_count)
    row_even = lax.broadcasted_iota(jnp.int32, grid_shape, 0) % 2 == 0
    column_even = lax.broadcasted_iota(jnp.int32, grid_shape, 1) % 2 == 0
    edge_bonds = passed_along(bonds[1][-1:], "band", 1)
    vertical_prev = jnp.concatenate([edge_bonds, bonds[1][:-1]], 0)
    tables = pair_tables(
        bonds[0].astype(jnp.float32),
        bonds[1].astype(jnp.float32),
        vertical_prev.astype(jnp.float32),
        row_even,
        column_even,
    )

    def apply_pairs(vector, colours):
        for colour in colours:
            cosh_part, sinh_part = tables[colour]
            vector = cosh_part * vector + sinh_part * partner_of(
                vector, colour, row_even, column_even
            )
        return vector

    phonon_rims = extended(phonon, (("tm", 0),), 1)
    factor_wide = jnp.exp(-coupling * phonon_rims)
    expo = factor_wide[1:-1]
    first_sign = jnp.where(position == 0, -1.0, 1.0).astype(jnp.float32)
    last_sign = jnp.where(position == cycle_size - 1, -1.0, 1.0).astype(jnp.float32)

    def from_prev(piece):
        return passed_along(piece, "tm", 1) * first_sign

    def from_after(piece):
        return passed_along(piece, "tm", -1) * last_sign

    applied = apply_pairs(expo * guess, (0, 1, 2, 3))
    link = guess - jnp.concatenate([from_prev(applied[-1:]), applied[:-1]], 0)
    shifted = jnp.concatenate([link[1:], from_after(link[:1])], 0)
    normal = link - expo * apply_pairs(shifted, (3, 2, 1, 0))
    residual = source - normal
    mixed = to_spectrum(lax.all_to_all(residual, "tm", split_axis=1, concat_axis=0, tiled=True))
    spectrum = lax.all_to_all(mixed, "tm", split_axis=0, concat_axis=1, tiled=True)
    freq_index = position * slice_count + jnp.arange(slice_count, dtype=jnp.int32)
    centre = cheb_centre(freq_index, slice_count * cycle_size)[:, None, None]
    ratio = centre / half_width
    start = (jnp.zeros_like(spectrum), spectrum, spectrum / centre, 1.0 / ratio)

    def sweep_block(counter, carry):
        accum, remaining, direction, weight_now = carry
        stacked = extended(jnp.stack([remaining, direction]), (("band", 2),), deep_width)
        rem_wide = stacked[0]
        dir_wide = stacked[1]
        for inner in range(deep_width):
            offset = deep_width - inner
            middle = dir_wide[:, 1:-1]
            beside_all = (
                dir_wide[:, :-2]
                + dir_wide[:, 2:]
                + jnp.roll(middle, 1, 2)
                + jnp.roll(middle, -1, 2)
            )
            accum = accum + dir_wide[:, offset : offset + row_count]
            rem_wide = rem_wide[:, 1:-1] - (centre * middle - beside_all)
            weight_new = 1.0 / (2.0 * ratio - weight_now)
            dir_wide = weight_new * weight_now * middle + 2.0 * weight_new / half_width * rem_wide
            weight_now = weight_new
        return (accum, rem_wide, dir_wide, weight_now)

    accum = lax.fori_loop(0, ORDER // deep_width, sweep_block, start)[0]
    mixed_back = to_slices(lax.all_to_all(accum, "tm", split_axis=1, concat_axis=0, tiled=True))
    timed = lax.all_to_all(mixed_back, "tm", split_axis=0, concat_axis=1, tiled=True)
    solution = guess + relaxation * timed
    propagated = apply_pairs(expo * solution, (0, 1, 2, 3))
    image = solution - jnp.concatenate([from_prev(propagated[-1:]), propagated[:-1]], 0)
    pulled = apply_pairs(jnp.concatenate([image[1:], from_after(image[:1])], 0), (3, 2, 1, 0))
    fermion_force = -2.0 * coupling * expo * solution * pulled
    boson_force = (
        stiffness * (2.0 * phonon - phonon_rims[:-2] - phonon_rims[2:]) + mass_term * phonon
    )
    momentum_new = momentum - step_size * (boson_force + fermion_force)
    return (solution, momentum_new)


def solution(mesh):
    return jax.shard_map(
        shards,
        mesh=mesh,
        in_specs=(
            P("tm", "band", None),
            P("tm", "band", None),
            P("tm", "band", None),
            P("tm", "band", None),
            P(None, "band", None),
        ),
        out_specs=(P("tm", "band", None), P("tm", "band", None)),
        check_vma=False,
    )
```

profile of v0, /device:TPU:0, one launch (start us, length us, event | category | flops | bytes accessed | tf_op | source)
XLA Modules:
  0.0 157.5 jit_solution(9558485487474373816)
XLA Ops:
  0.6 0.7 slice_bitcast_fusion.4
  1.3 3.0 %collective-permute-start.2 = (s32[1,256]{1,0:T(1,128)S(1)}, s32[1,256]{1,0:T(1,128)S(1)}, u32[]{:S(2)}, u32[]{:S(2)}) collective-permute-start(s32[1,256]{1,0:T(1,128)S(1)} %slice_bitcast_fusion.4), channel_id=1, source_target_pairs={{0,1},{1,0},{2,3},{3,2},{4,5},{5,4},{6,7},{7,6},{8,9},{9,8},{10,11... | collective-permute-start | bytes 3080 | tf_op jit(solution)/shard_map/ppermute | solution.py:38
  4.3 1.0 fusion.157
  5.4 4.4 %collective-permute-start.4 = (f32[1,128,256]{2,1,0:T(8,128)S(1)}, f32[1,128,256]{2,1,0:T(8,128)S(1)}, u32[]{:S(2)}, u32[]{:S(2)}) collective-permute-start(f32[1,128,256]{2,1,0:T(8,128)S(1)} %get-tuple-element.314), channel_id=1, source_target_pairs={{2,0},{4,2},{6,4},{8,6},{10,8},{12,10},{14,12},{16,14},{18,16},{20... | collective-permute-start | bytes 393224 | tf_op jit(solution)/shard_map/ppermute | solution.py:31
  10.9 1.7 %collective-permute-done.3 = f32[1,128,256]{2,1,0:T(8,128)S(1)} collective-permute-done((f32[1,128,256]{2,1,0:T(8,128)S(1)}, f32[1,128,256]{2,1,0:T(8,128)S(1)}, u32[]{:S(2)}, u32[]{:S(2)}) %collective-permute-start.3) | collective-permute-done | bytes 131104 | tf_op jit(solution)/shard_map/ppermute | solution.py:30
  13.7 2.0 %collective-permute-start.6 = (f32[2,1,256]{2,1,0:T(1,128)S(1)}, f32[2,1,256]{2,1,0:T(1,128)S(1)}, u32[]{:S(2)}, u32[]{:S(2)}) collective-permute-start(f32[2,1,256]{2,1,0:T(1,128)S(1)} %get-tuple-element.298), channel_id=1, source_target_pairs={{1,0},{0,1},{3,2},{2,3},{5,4},{4,5},{7,6},{6,7},{9,8},{8,9},{11,10... | collective-permute-start | bytes 6152 | tf_op jit(solution)/shard_map/ppermute | solution.py:31
  15.7 1.6 collective-permute-done.5
  17.5 7.1 %collective-permute-done.7 = f32[1,128,256]{2,1,0:T(8,128)S(1)} collective-permute-done((f32[1,128,256]{2,1,0:T(8,128)S(1)}, f32[1,128,256]{2,1,0:T(8,128)S(1)}, u32[]{:S(2)}, u32[]{:S(2)}) %collective-permute-start.7) | collective-permute-done | bytes 131104 | tf_op jit(solution)/shard_map/ppermute | solution.py:38
  24.8 2.5 %collective-permute-done.8 = f32[1,128,256]{2,1,0:T(8,128)S(1)} collective-permute-done((f32[1,128,256]{2,1,0:T(8,128)S(1)}, f32[1,128,256]{2,1,0:T(8,128)S(1)}, u32[]{:S(2)}, u32[]{:S(2)}) %collective-permute-start.8) | collective-permute-done | bytes 131104 | tf_op jit(solution)/shard_map/ppermute | solution.py:38
  27.3 2.0 %collective-permute-start.9 = (f32[2,1,256]{2,1,0:T(1,128)S(1)}, f32[2,1,256]{2,1,0:T(1,128)S(1)}, u32[]{:S(2)}, u32[]{:S(2)}) collective-permute-start(f32[2,1,256]{2,1,0:T(1,128)S(1)} %get-tuple-element.291), channel_id=1, source_target_pairs={{0,1},{1,0},{2,3},{3,2},{4,5},{5,4},{6,7},{7,6},{8,9},{9,8},{10,11... | collective-permute-start | bytes 6152 | tf_op jit(solution)/shard_map/ppermute | solution.py:30
  29.5 1.5 collective-permute-done.9
  31.0 2.0 %collective-permute-done.10 = f32[2,1,256]{2,1,0:T(1,128)S(1)} collective-permute-done((f32[2,1,256]{2,1,0:T(1,128)S(1)}, f32[2,1,256]{2,1,0:T(1,128)S(1)}, u32[]{:S(2)}, u32[]{:S(2)}) %collective-permute-start.10) | collective-permute-done | bytes 2080 | tf_op jit(solution)/shard_map/ppermute | solution.py:31
  33.9 0.8 copy-done.4
  35.0 0.9 copy.43
  35.9 4.5 %all-to-all-start = ((f32[2,128,256]{2,0,1:T(2,128)}), f32[2,128,256]{2,0,1:T(2,128)S(1)}, u32[]{:S(2)}, u32[]{:S(2)}) async-start(f32[2,128,256]{2,0,1:T(2,128)} %copy.43), calls=%async_computation | async-start | bytes 524288 | tf_op jit(solution)/shard_map/all_to_all | solution.py:131
  40.4 10.0 %all-to-all-done = f32[2,128,256]{2,0,1:T(2,128)S(1)} async-done(((f32[2,128,256]{2,0,1:T(2,128)}), f32[2,128,256]{2,0,1:T(2,128)S(1)}, u32[]{:S(2)}, u32[]{:S(2)}) %all-to-all-start) | async-done | bytes 262176 | tf_op jit(solution)/shard_map/all_to_all | solution.py:131
  50.7 0.5 fusion.90
  51.2 0.9 copy.46
  52.0 3.5 %all-to-all-start.1 = ((f32[32,8,256]{2,1,0:T(8,128)}), f32[32,8,256]{2,1,0:T(8,128)S(1)}, u32[]{:S(2)}, u32[]{:S(2)}) async-start(f32[32,8,256]{2,1,0:T(8,128)} %copy.46), calls=%async_computation.1 | async-start | bytes 524288 | tf_op jit(solution)/shard_map/all_to_all | solution.py:132
  55.7 9.8 %all-to-all-done.1 = f32[32,8,256]{2,1,0:T(8,128)S(1)} async-done(((f32[32,8,256]{2,1,0:T(8,128)}), f32[32,8,256]{2,1,0:T(8,128)S(1)}, u32[]{:S(2)}, u32[]{:S(2)}) %all-to-all-start.1) | async-done | bytes 262176 | tf_op jit(solution)/shard_map/all_to_all | solution.py:132
  65.7 42.2 %while.22 = (s32[]{:T(128)}, f32[2,128,256]{2,1,0:T(8,128)S(1)}, f32[2,128,256]{2,1,0:T(8,128)S(1)}, f32[2,128,256]{2,1,0:T(8,128)S(1)}, f32[2,1,1]{0,2,1:T(1,12...) while((s32[]{:T(128)}, f32[2,128,256]{2,1,0:T(8,128)S(1)}, ...), condition=%wide.region_1.2_spmd.clone.clone.clone, body=%wide.region_0.1_spmd.clone.clone.clone.sunk | while | flops 3704962 | bytes 17105376 | solution.py:159
  66.1 1.7 %collective-permute-start.1 = (f32[2,2,4,256]{3,2,1,0:T(4,128)S(1)}, f32[2,2,4,256]{3,2,1,0:T(4,128)S(1)}, u32[]{:S(2)}, u32[]{:S(2)}) collective-permute-start(f32[2,2,4,256]{3,2,1,0:T(4,128)S(1)} %get-tuple-element.405), channel_id=1, source_target_pairs={{0,1},{1,0},{2,3},{3,2},{4,5},{5,4},{6,7},{7,6},{8,9},{9,8},{10,11... | collective-permute-start | bytes 49160 | tf_op jit(solution)/shard_map/while/body/eval_jaxpr/ppermute | solution.py:30
  68.0 1.5 collective-permute-done
  72.1 1.7 %collective-permute-start = (f32[2,2,4,256]{3,2,1,0:T(4,128)S(1)}, f32[2,2,4,256]{3,2,1,0:T(4,128)S(1)}, u32[]{:S(2)}, u32[]{:S(2)}) collective-permute-start(f32[2,2,4,256]{3,2,1,0:T(4,128)S(1)} %get-tuple-element.404), channel_id=1, source_target_pairs={{1,0},{0,1},{3,2},{2,3},{5,4},{4,5},{7,6},{6,7},{9,8},{8,9},{11,10... | collective-permute-start | bytes 49160 | tf_op jit(solution)/shard_map/while/body/eval_jaxpr/ppermute | solution.py:31
  74.3 1.5 collective-permute-done
  75.9 1.7 %collective-permute-done.1 = f32[2,2,4,256]{3,2,1,0:T(4,128)S(1)} collective-permute-done((f32[2,2,4,256]{3,2,1,0:T(4,128)S(1)}, f32[2,2,4,256]{3,2,1,0:T(4,128)S(1)}, u32[]{:S(2)}, u32[]{:S(2)}) %collective-permute-start.1) | collective-permute-done | bytes 16416 | tf_op jit(solution)/shard_map/while/body/eval_jaxpr/ppermute | solution.py:30
  80.2 1.7 %collective-permute-start.1 = (f32[2,2,4,256]{3,2,1,0:T(4,128)S(1)}, f32[2,2,4,256]{3,2,1,0:T(4,128)S(1)}, u32[]{:S(2)}, u32[]{:S(2)}) collective-permute-start(f32[2,2,4,256]{3,2,1,0:T(4,128)S(1)} %get-tuple-element.405), channel_id=1, source_target_pairs={{0,1},{1,0},{2,3},{3,2},{4,5},{5,4},{6,7},{7,6},{8,9},{9,8},{10,11... | collective-permute-start | bytes 49160 | tf_op jit(solution)/shard_map/while/body/eval_jaxpr/ppermute | solution.py:30
  82.0 1.5 collective-permute-done
  86.1 1.7 %collective-permute-start = (f32[2,2,4,256]{3,2,1,0:T(4,128)S(1)}, f32[2,2,4,256]{3,2,1,0:T(4,128)S(1)}, u32[]{:S(2)}, u32[]{:S(2)}) collective-permute-start(f32[2,2,4,256]{3,2,1,0:T(4,128)S(1)} %get-tuple-element.404), channel_id=1, source_target_pairs={{1,0},{0,1},{3,2},{2,3},{5,4},{4,5},{7,6},{6,7},{9,8},{8,9},{11,10... | collective-permute-start | bytes 49160 | tf_op jit(solution)/shard_map/while/body/eval_jaxpr/ppermute | solution.py:31
  88.4 1.5 collective-permute-done
  89.9 1.7 %collective-permute-done.1 = f32[2,2,4,256]{3,2,1,0:T(4,128)S(1)} collective-permute-done((f32[2,2,4,256]{3,2,1,0:T(4,128)S(1)}, f32[2,2,4,256]{3,2,1,0:T(4,128)S(1)}, u32[]{:S(2)}, u32[]{:S(2)}) %collective-permute-start.1) | collective-permute-done | bytes 16416 | tf_op jit(solution)/shard_map/while/body/eval_jaxpr/ppermute | solution.py:30
  94.3 1.7 %collective-permute-start.1 = (f32[2,2,4,256]{3,2,1,0:T(4,128)S(1)}, f32[2,2,4,256]{3,2,1,0:T(4,128)S(1)}, u32[]{:S(2)}, u32[]{:S(2)}) collective-permute-start(f32[2,2,4,256]{3,2,1,0:T(4,128)S(1)} %get-tuple-element.405), channel_id=1, source_target_pairs={{0,1},{1,0},{2,3},{3,2},{4,5},{5,4},{6,7},{7,6},{8,9},{9,8},{10,11... | collective-permute-start | bytes 49160 | tf_op jit(solution)/shard_map/while/body/eval_jaxpr/ppermute | solution.py:30
  96.1 1.5 collective-permute-done
  100.2 1.7 %collective-permute-start = (f32[2,2,4,256]{3,2,1,0:T(4,128)S(1)}, f32[2,2,4,256]{3,2,1,0:T(4,128)S(1)}, u32[]{:S(2)}, u32[]{:S(2)}) collective-permute-start(f32[2,2,4,256]{3,2,1,0:T(4,128)S(1)} %get-tuple-element.404), channel_id=1, source_target_pairs={{1,0},{0,1},{3,2},{2,3},{5,4},{4,5},{7,6},{6,7},{9,8},{8,9},{11,10... | collective-permute-start | bytes 49160 | tf_op jit(solution)/shard_map/while/body/eval_jaxpr/ppermute | solution.py:31
  102.5 1.5 collective-permute-done
  104.0 1.7 %collective-permute-done.1 = f32[2,2,4,256]{3,2,1,0:T(4,128)S(1)} collective-permute-done((f32[2,2,4,256]{3,2,1,0:T(4,128)S(1)}, f32[2,2,4,256]{3,2,1,0:T(4,128)S(1)}, u32[]{:S(2)}, u32[]{:S(2)}) %collective-permute-start.1) | collective-permute-done | bytes 16416 | tf_op jit(solution)/shard_map/while/body/eval_jaxpr/ppermute | solution.py:30
  108.1 12.7 %all_to_all.63 = f32[2,128,256]{2,0,1:T(2,128)S(1)} all-to-all(f32[2,128,256]{2,0,1:T(2,128)S(1)} %copy.48), channel_id=1, replica_groups=mesh['tm'=16,'band'=2] {'tm'}, dimensions={1} | all-to-all | bytes 524288 | tf_op jit(solution)/shard_map/all_to_all | solution.py:160
  121.0 0.4 fusion.92
  121.6 12.7 %all_to_all.64 = f32[32,8,256]{2,1,0:T(8,128)S(1)} all-to-all(f32[32,8,256]{2,1,0:T(8,128)S(1)} %copy.50), channel_id=1, replica_groups=mesh['tm'=16,'band'=2] {'tm'}, dimensions={0} | all-to-all | bytes 524288 | tf_op jit(solution)/shard_map/all_to_all | solution.py:161
  135.9 1.7 %collective-permute-start.12 = (f32[2,1,256]{2,1,0:T(1,128)S(1)}, f32[2,1,256]{2,1,0:T(1,128)S(1)}, u32[]{:S(2)}, u32[]{:S(2)}) collective-permute-start(f32[2,1,256]{2,1,0:T(1,128)S(1)} %get-tuple-element.266), channel_id=1, source_target_pairs={{1,0},{0,1},{3,2},{2,3},{5,4},{4,5},{7,6},{6,7},{9,8},{8,9},{11,10... | collective-permute-start | bytes 6152 | tf_op jit(solution)/shard_map/ppermute | solution.py:31
  137.5 1.6 collective-permute-done.11
  139.6 7.2 %collective-permute-done.13 = f32[1,128,256]{2,1,0:T(8,128)S(1)} collective-permute-done((f32[1,128,256]{2,1,0:T(8,128)S(1)}, f32[1,128,256]{2,1,0:T(8,128)S(1)}, u32[]{:S(2)}, u32[]{:S(2)}) %collective-permute-start.13) | collective-permute-done | bytes 131104 | tf_op jit(solution)/shard_map/ppermute | solution.py:38
  147.0 2.5 %collective-permute-done.14 = f32[1,128,256]{2,1,0:T(8,128)S(1)} collective-permute-done((f32[1,128,256]{2,1,0:T(8,128)S(1)}, f32[1,128,256]{2,1,0:T(8,128)S(1)}, u32[]{:S(2)}, u32[]{:S(2)}) %collective-permute-start.14) | collective-permute-done | bytes 131104 | tf_op jit(solution)/shard_map/ppermute | solution.py:38
  149.5 1.7 %collective-permute-start.15 = (f32[2,1,256]{2,1,0:T(1,128)S(1)}, f32[2,1,256]{2,1,0:T(1,128)S(1)}, u32[]{:S(2)}, u32[]{:S(2)}) collective-permute-start(f32[2,1,256]{2,1,0:T(1,128)S(1)} %get-tuple-element.259), channel_id=1, source_target_pairs={{0,1},{1,0},{2,3},{3,2},{4,5},{5,4},{6,7},{7,6},{8,9},{9,8},{10,11... | collective-permute-start | bytes 6152 | tf_op jit(solution)/shard_map/ppermute | solution.py:30
  151.6 1.6 collective-permute-done.15
  153.1 1.7 %collective-permute-done.16 = f32[2,1,256]{2,1,0:T(1,128)S(1)} collective-permute-done((f32[2,1,256]{2,1,0:T(1,128)S(1)}, f32[2,1,256]{2,1,0:T(1,128)S(1)}, u32[]{:S(2)}, u32[]{:S(2)}) %collective-permute-start.16) | collective-permute-done | bytes 2080 | tf_op jit(solution)/shard_map/ppermute | solution.py:31
  155.8 0.8 copy-done.5
  156.6 0.9 fusion.35
  (229 shorter events, 25.2 us)
Async XLA Ops:
  1.3 8.5 %copy-start.3 = (s32[2,128,256]{2,1,0:T(8,128)S(1)}, s32[2,128,256]{2,1,0:T(8,128)}, u32[]{:S(2)}) copy-start(s32[2,128,256]{2,1,0:T(8,128)} %param.11) | copy-start | bytes 786436
  1.3 9.1 %collective-permute-start.2 = (s32[1,256]{1,0:T(1,128)S(1)}, s32[1,256]{1,0:T(1,128)S(1)}, u32[]{:S(2)}, u32[]{:S(2)}) collective-permute-start(s32[1,256]{1,0:T(1,128)S(1)} %slice_bitcast_fusion.4), channel_id=1, source_target_pairs={{0,1},{1,0},{2,3},{3,2},{4,5},{5,4},{6,7},{7,6},{8,9},{9,8},{10,11... | collective-permute-start | bytes 3080 | tf_op jit(solution)/shard_map/ppermute | solution.py:38
  5.3 7.2 %collective-permute-start.3 = (f32[1,128,256]{2,1,0:T(8,128)S(1)}, f32[1,128,256]{2,1,0:T(8,128)S(1)}, u32[]{:S(2)}, u32[]{:S(2)}) collective-permute-start(f32[1,128,256]{2,1,0:T(8,128)S(1)} %get-tuple-element.313), channel_id=1, source_target_pairs={{0,2},{2,4},{4,6},{6,8},{8,10},{10,12},{12,14},{14,16},{16,18},{18... | collective-permute-start | bytes 393224 | tf_op jit(solution)/shard_map/ppermute | solution.py:30
  5.4 7.2 %collective-permute-start.4 = (f32[1,128,256]{2,1,0:T(8,128)S(1)}, f32[1,128,256]{2,1,0:T(8,128)S(1)}, u32[]{:S(2)}, u32[]{:S(2)}) collective-permute-start(f32[1,128,256]{2,1,0:T(8,128)S(1)} %get-tuple-element.314), channel_id=1, source_target_pairs={{2,0},{4,2},{6,4},{8,6},{10,8},{12,10},{14,12},{16,14},{18,16},{20... | collective-permute-start | bytes 393224 | tf_op jit(solution)/shard_map/ppermute | solution.py:31
  10.4 2.1 %copy-start = (f32[2,128,256]{2,1,0:T(8,128)S(1)}, f32[2,128,256]{2,1,0:T(8,128)}, u32[]{:S(2)}) copy-start(f32[2,128,256]{2,1,0:T(8,128)} %param.7) | copy-start | bytes 786436
  10.5 2.1 %copy-start.1 = (f32[2,128,256]{2,1,0:T(8,128)S(1)}, f32[2,128,256]{2,1,0:T(8,128)}, u32[]{:S(2)}) copy-start(f32[2,128,256]{2,1,0:T(8,128)} %param.10) | copy-start | bytes 786436
  13.6 3.7 %collective-permute-start.5 = (f32[2,1,256]{2,1,0:T(1,128)S(1)}, f32[2,1,256]{2,1,0:T(1,128)S(1)}, u32[]{:S(2)}, u32[]{:S(2)}) collective-permute-start(f32[2,1,256]{2,1,0:T(1,128)S(1)} %get-tuple-element.297), channel_id=1, source_target_pairs={{0,1},{1,0},{2,3},{3,2},{4,5},{5,4},{6,7},{7,6},{8,9},{9,8},{10,11... | collective-permute-start | bytes 6152 | tf_op jit(solution)/shard_map/ppermute | solution.py:30
  13.7 3.6 %collective-permute-start.6 = (f32[2,1,256]{2,1,0:T(1,128)S(1)}, f32[2,1,256]{2,1,0:T(1,128)S(1)}, u32[]{:S(2)}, u32[]{:S(2)}) collective-permute-start(f32[2,1,256]{2,1,0:T(1,128)S(1)} %get-tuple-element.298), channel_id=1, source_target_pairs={{1,0},{0,1},{3,2},{2,3},{5,4},{4,5},{7,6},{6,7},{9,8},{8,9},{11,10... | collective-permute-start | bytes 6152 | tf_op jit(solution)/shard_map/ppermute | solution.py:31
  17.4 7.2 %collective-permute-start.7 = (f32[1,128,256]{2,1,0:T(8,128)S(1)}, f32[1,128,256]{2,1,0:T(8,128)S(1)}, u32[]{:S(2)}, u32[]{:S(2)}) collective-permute-start(f32[1,128,256]{2,1,0:T(8,128)S(1)} %get-tuple-element.295), channel_id=1, source_target_pairs={{0,2},{2,4},{4,6},{6,8},{8,10},{10,12},{12,14},{14,16},{16,18},{18... | collective-permute-start | bytes 393224 | tf_op jit(solution)/shard_map/ppermute | solution.py:38
  24.7 2.6 %collective-permute-start.8 = (f32[1,128,256]{2,1,0:T(8,128)S(1)}, f32[1,128,256]{2,1,0:T(8,128)S(1)}, u32[]{:S(2)}, u32[]{:S(2)}) collective-permute-start(f32[1,128,256]{2,1,0:T(8,128)S(1)} %get-tuple-element.294), channel_id=1, source_target_pairs={{0,30},{2,0},{4,2},{6,4},{8,6},{10,8},{12,10},{14,12},{16,14},{18,... | collective-permute-start | bytes 393224 | tf_op jit(solution)/shard_map/ppermute | solution.py:38
  27.3 3.7 %collective-permute-start.9 = (f32[2,1,256]{2,1,0:T(1,128)S(1)}, f32[2,1,256]{2,1,0:T(1,128)S(1)}, u32[]{:S(2)}, u32[]{:S(2)}) collective-permute-start(f32[2,1,256]{2,1,0:T(1,128)S(1)} %get-tuple-element.291), channel_id=1, source_target_pairs={{0,1},{1,0},{2,3},{3,2},{4,5},{5,4},{6,7},{7,6},{8,9},{9,8},{10,11... | collective-permute-start | bytes 6152 | tf_op jit(solution)/shard_map/ppermute | solution.py:30
  29.4 3.6 %collective-permute-start.10 = (f32[2,1,256]{2,1,0:T(1,128)S(1)}, f32[2,1,256]{2,1,0:T(1,128)S(1)}, u32[]{:S(2)}, u32[]{:S(2)}) collective-permute-start(f32[2,1,256]{2,1,0:T(1,128)S(1)} %get-tuple-element.292), channel_id=1, source_target_pairs={{1,0},{0,1},{3,2},{2,3},{5,4},{4,5},{7,6},{6,7},{9,8},{8,9},{11,10... | collective-permute-start | bytes 6152 | tf_op jit(solution)/shard_map/ppermute | solution.py:31
  33.8 1.0 copy-start.4
  35.9 14.5 %all-to-all-start = ((f32[2,128,256]{2,0,1:T(2,128)}), f32[2,128,256]{2,0,1:T(2,128)S(1)}, u32[]{:S(2)}, u32[]{:S(2)}) async-start(f32[2,128,256]{2,0,1:T(2,128)} %copy.43), calls=%async_computation | async-start | bytes 524288 | tf_op jit(solution)/shard_map/all_to_all | solution.py:131
  52.0 13.5 %all-to-all-start.1 = ((f32[32,8,256]{2,1,0:T(8,128)}), f32[32,8,256]{2,1,0:T(8,128)S(1)}, u32[]{:S(2)}, u32[]{:S(2)}) async-start(f32[32,8,256]{2,1,0:T(8,128)} %copy.46), calls=%async_computation.1 | async-start | bytes 524288 | tf_op jit(solution)/shard_map/all_to_all | solution.py:132
  65.7 3.8 %collective-permute-start = (f32[2,2,4,256]{3,2,1,0:T(4,128)S(1)}, f32[2,2,4,256]{3,2,1,0:T(4,128)S(1)}, u32[]{:S(2)}, u32[]{:S(2)}) collective-permute-start(f32[2,2,4,256]{3,2,1,0:T(4,128)S(1)} %get-tuple-element.404), channel_id=1, source_target_pairs={{1,0},{0,1},{3,2},{2,3},{5,4},{4,5},{7,6},{6,7},{9,8},{8,9},{11,10... | collective-permute-start | bytes 49160 | tf_op jit(solution)/shard_map/while/body/eval_jaxpr/ppermute | solution.py:31
  66.1 3.7 %collective-permute-start.1 = (f32[2,2,4,256]{3,2,1,0:T(4,128)S(1)}, f32[2,2,4,256]{3,2,1,0:T(4,128)S(1)}, u32[]{:S(2)}, u32[]{:S(2)}) collective-permute-start(f32[2,2,4,256]{3,2,1,0:T(4,128)S(1)} %get-tuple-element.405), channel_id=1, source_target_pairs={{0,1},{1,0},{2,3},{3,2},{4,5},{5,4},{6,7},{7,6},{8,9},{9,8},{10,11... | collective-permute-start | bytes 49160 | tf_op jit(solution)/shard_map/while/body/eval_jaxpr/ppermute | solution.py:30
  72.1 3.8 %collective-permute-start = (f32[2,2,4,256]{3,2,1,0:T(4,128)S(1)}, f32[2,2,4,256]{3,2,1,0:T(4,128)S(1)}, u32[]{:S(2)}, u32[]{:S(2)}) collective-permute-start(f32[2,2,4,256]{3,2,1,0:T(4,128)S(1)} %get-tuple-element.404), channel_id=1, source_target_pairs={{1,0},{0,1},{3,2},{2,3},{5,4},{4,5},{7,6},{6,7},{9,8},{8,9},{11,10... | collective-permute-start | bytes 49160 | tf_op jit(solution)/shard_map/while/body/eval_jaxpr/ppermute | solution.py:31
  73.8 3.7 %collective-permute-start.1 = (f32[2,2,4,256]{3,2,1,0:T(4,128)S(1)}, f32[2,2,4,256]{3,2,1,0:T(4,128)S(1)}, u32[]{:S(2)}, u32[]{:S(2)}) collective-permute-start(f32[2,2,4,256]{3,2,1,0:T(4,128)S(1)} %get-tuple-element.405), channel_id=1, source_target_pairs={{0,1},{1,0},{2,3},{3,2},{4,5},{5,4},{6,7},{7,6},{8,9},{9,8},{10,11... | collective-permute-start | bytes 49160 | tf_op jit(solution)/shard_map/while/body/eval_jaxpr/ppermute | solution.py:30
  79.8 3.8 %collective-permute-start = (f32[2,2,4,256]{3,2,1,0:T(4,128)S(1)}, f32[2,2,4,256]{3,2,1,0:T(4,128)S(1)}, u32[]{:S(2)}, u32[]{:S(2)}) collective-permute-start(f32[2,2,4,256]{3,2,1,0:T(4,128)S(1)} %get-tuple-element.404), channel_id=1, source_target_pairs={{1,0},{0,1},{3,2},{2,3},{5,4},{4,5},{7,6},{6,7},{9,8},{8,9},{11,10... | collective-permute-start | bytes 49160 | tf_op jit(solution)/shard_map/while/body/eval_jaxpr/ppermute | solution.py:31
  80.2 3.7 %collective-permute-start.1 = (f32[2,2,4,256]{3,2,1,0:T(4,128)S(1)}, f32[2,2,4,256]{3,2,1,0:T(4,128)S(1)}, u32[]{:S(2)}, u32[]{:S(2)}) collective-permute-start(f32[2,2,4,256]{3,2,1,0:T(4,128)S(1)} %get-tuple-element.405), channel_id=1, source_target_pairs={{0,1},{1,0},{2,3},{3,2},{4,5},{5,4},{6,7},{7,6},{8,9},{9,8},{10,11... | collective-permute-start | bytes 49160 | tf_op jit(solution)/shard_map/while/body/eval_jaxpr/ppermute | solution.py:30
  86.1 3.8 %collective-permute-start = (f32[2,2,4,256]{3,2,1,0:T(4,128)S(1)}, f32[2,2,4,256]{3,2,1,0:T(4,128)S(1)}, u32[]{:S(2)}, u32[]{:S(2)}) collective-permute-start(f32[2,2,4,256]{3,2,1,0:T(4,128)S(1)} %get-tuple-element.404), channel_id=1, source_target_pairs={{1,0},{0,1},{3,2},{2,3},{5,4},{4,5},{7,6},{6,7},{9,8},{8,9},{11,10... | collective-permute-start | bytes 49160 | tf_op jit(solution)/shard_map/while/body/eval_jaxpr/ppermute | solution.py:31
  87.9 3.7 %collective-permute-start.1 = (f32[2,2,4,256]{3,2,1,0:T(4,128)S(1)}, f32[2,2,4,256]{3,2,1,0:T(4,128)S(1)}, u32[]{:S(2)}, u32[]{:S(2)}) collective-permute-start(f32[2,2,4,256]{3,2,1,0:T(4,128)S(1)} %get-tuple-element.405), channel_id=1, source_target_pairs={{0,1},{1,0},{2,3},{3,2},{4,5},{5,4},{6,7},{7,6},{8,9},{9,8},{10,11... | collective-permute-start | bytes 49160 | tf_op jit(solution)/shard_map/while/body/eval_jaxpr/ppermute | solution.py:30
  93.8 3.8 %collective-permute-start = (f32[2,2,4,256]{3,2,1,0:T(4,128)S(1)}, f32[2,2,4,256]{3,2,1,0:T(4,128)S(1)}, u32[]{:S(2)}, u32[]{:S(2)}) collective-permute-start(f32[2,2,4,256]{3,2,1,0:T(4,128)S(1)} %get-tuple-element.404), channel_id=1, source_target_pairs={{1,0},{0,1},{3,2},{2,3},{5,4},{4,5},{7,6},{6,7},{9,8},{8,9},{11,10... | collective-permute-start | bytes 49160 | tf_op jit(solution)/shard_map/while/body/eval_jaxpr/ppermute | solution.py:31
  94.3 3.7 %collective-permute-start.1 = (f32[2,2,4,256]{3,2,1,0:T(4,128)S(1)}, f32[2,2,4,256]{3,2,1,0:T(4,128)S(1)}, u32[]{:S(2)}, u32[]{:S(2)}) collective-permute-start(f32[2,2,4,256]{3,2,1,0:T(4,128)S(1)} %get-tuple-element.405), channel_id=1, source_target_pairs={{0,1},{1,0},{2,3},{3,2},{4,5},{5,4},{6,7},{7,6},{8,9},{9,8},{10,11... | collective-permute-start | bytes 49160 | tf_op jit(solution)/shard_map/while/body/eval_jaxpr/ppermute | solution.py:30
  100.2 3.8 %collective-permute-start = (f32[2,2,4,256]{3,2,1,0:T(4,128)S(1)}, f32[2,2,4,256]{3,2,1,0:T(4,128)S(1)}, u32[]{:S(2)}, u32[]{:S(2)}) collective-permute-start(f32[2,2,4,256]{3,2,1,0:T(4,128)S(1)} %get-tuple-element.404), channel_id=1, source_target_pairs={{1,0},{0,1},{3,2},{2,3},{5,4},{4,5},{7,6},{6,7},{9,8},{8,9},{11,10... | collective-permute-start | bytes 49160 | tf_op jit(solution)/shard_map/while/body/eval_jaxpr/ppermute | solution.py:31
  101.9 3.7 %collective-permute-start.1 = (f32[2,2,4,256]{3,2,1,0:T(4,128)S(1)}, f32[2,2,4,256]{3,2,1,0:T(4,128)S(1)}, u32[]{:S(2)}, u32[]{:S(2)}) collective-permute-start(f32[2,2,4,256]{3,2,1,0:T(4,128)S(1)} %get-tuple-element.405), channel_id=1, source_target_pairs={{0,1},{1,0},{2,3},{3,2},{4,5},{5,4},{6,7},{7,6},{8,9},{9,8},{10,11... | collective-permute-start | bytes 49160 | tf_op jit(solution)/shard_map/while/body/eval_jaxpr/ppermute | solution.py:30
  134.4 21.3 %copy-start.2 = (f32[2,128,256]{2,1,0:T(8,128)}, f32[2,128,256]{2,1,0:T(8,128)S(1)}, u32[]{:S(2)}) copy-start(f32[2,128,256]{2,1,0:T(8,128)S(1)} %get-tuple-element.207) | copy-start | bytes 786436
  135.4 3.7 %collective-permute-start.11 = (f32[2,1,256]{2,1,0:T(1,128)S(1)}, f32[2,1,256]{2,1,0:T(1,128)S(1)}, u32[]{:S(2)}, u32[]{:S(2)}) collective-permute-start(f32[2,1,256]{2,1,0:T(1,128)S(1)} %get-tuple-element.265), channel_id=1, source_target_pairs={{0,1},{1,0},{2,3},{3,2},{4,5},{5,4},{6,7},{7,6},{8,9},{9,8},{10,11... | collective-permute-start | bytes 6152 | tf_op jit(solution)/shard_map/ppermute | solution.py:30
  135.9 3.6 %collective-permute-start.12 = (f32[2,1,256]{2,1,0:T(1,128)S(1)}, f32[2,1,256]{2,1,0:T(1,128)S(1)}, u32[]{:S(2)}, u32[]{:S(2)}) collective-permute-start(f32[2,1,256]{2,1,0:T(1,128)S(1)} %get-tuple-element.266), channel_id=1, source_target_pairs={{1,0},{0,1},{3,2},{2,3},{5,4},{4,5},{7,6},{6,7},{9,8},{8,9},{11,10... | collective-permute-start | bytes 6152 | tf_op jit(solution)/shard_map/ppermute | solution.py:31
  139.6 7.2 %collective-permute-start.13 = (f32[1,128,256]{2,1,0:T(8,128)S(1)}, f32[1,128,256]{2,1,0:T(8,128)S(1)}, u32[]{:S(2)}, u32[]{:S(2)}) collective-permute-start(f32[1,128,256]{2,1,0:T(8,128)S(1)} %get-tuple-element.263), channel_id=1, source_target_pairs={{0,2},{2,4},{4,6},{6,8},{8,10},{10,12},{12,14},{14,16},{16,18},{18... | collective-permute-start | bytes 393224 | tf_op jit(solution)/shard_map/ppermute | solution.py:38
  146.9 2.6 %collective-permute-start.14 = (f32[1,128,256]{2,1,0:T(8,128)S(1)}, f32[1,128,256]{2,1,0:T(8,128)S(1)}, u32[]{:S(2)}, u32[]{:S(2)}) collective-permute-start(f32[1,128,256]{2,1,0:T(8,128)S(1)} %get-tuple-element.262), channel_id=1, source_target_pairs={{0,30},{2,0},{4,2},{6,4},{8,6},{10,8},{12,10},{14,12},{16,14},{18,... | collective-permute-start | bytes 393224 | tf_op jit(solution)/shard_map/ppermute | solution.py:38
  149.5 3.7 %collective-permute-start.15 = (f32[2,1,256]{2,1,0:T(1,128)S(1)}, f32[2,1,256]{2,1,0:T(1,128)S(1)}, u32[]{:S(2)}, u32[]{:S(2)}) collective-permute-start(f32[2,1,256]{2,1,0:T(1,128)S(1)} %get-tuple-element.259), channel_id=1, source_target_pairs={{0,1},{1,0},{2,3},{3,2},{4,5},{5,4},{6,7},{7,6},{8,9},{9,8},{10,11... | collective-permute-start | bytes 6152 | tf_op jit(solution)/shard_map/ppermute | solution.py:30
  151.2 3.6 %collective-permute-start.16 = (f32[2,1,256]{2,1,0:T(1,128)S(1)}, f32[2,1,256]{2,1,0:T(1,128)S(1)}, u32[]{:S(2)}, u32[]{:S(2)}) collective-permute-start(f32[2,1,256]{2,1,0:T(1,128)S(1)} %get-tuple-element.260), channel_id=1, source_target_pairs={{1,0},{0,1},{3,2},{2,3},{5,4},{4,5},{7,6},{6,7},{9,8},{8,9},{11,10... | collective-permute-start | bytes 6152 | tf_op jit(solution)/shard_map/ppermute | solution.py:31
  155.6 1.0 copy-start.5
where the time goes:
time: 158 us
  waiting for transfers between devices  66.5 us (42%)
  starting transfers between devices  36.7 us (23%)
  blocking collectives  25.4 us (16%)
  local copies, waits for them, and re-layouts  14.2 us (9%)
  other arithmetic  11.9 us (8%)
    ppermute x5, waiting for transfers between devices, passed_along(): lax.ppermute(value, axis, [(i, (i + by) % size) for i in range(size)])  19.3 us
    ppermute x11, starting transfers between devices, extended(): after = lax.ppermute(leading, axis, down)  15 us
    ppermute x11, waiting for transfers between devices, extended(): before = lax.ppermute(last, axis, up)  13.9 us
    ppermute x11, waiting for transfers between devices, extended(): after = lax.ppermute(leading, axis, down)  13.4 us
    all_to_all x1, blocking collectives, shards(): lax.all_to_all(accum, 'tm', split_axis=1, concat_axis=0, tiled=True)  12.7 us
    all_to_all x1, blocking collectives, shards(): lax.all_to_all(mixed_back, 'tm', split_axis=0, concat_axis=1, tiled=True)  12.7 us
    ppermute x11, starting transfers between devices, extended(): before = lax.ppermute(last, axis, up)  10.4 us
    all_to_all x1, waiting for transfers between devices, shards(): lax.all_to_all(residual, 'tm', split_axis=1, concat_axis=0, tiled=True)  9.98 us
  transfers between devices with their start and end apart: 29, of which 27 were waited for; matrix products, arithmetic and copies ran while one was open for 2% of the time, Pallas kernels for 0%

commit v1 on v0

v1 whole, which is shorter than its diff:
```python
import functools
import math

import numpy as np

import jax
import jax.numpy as jnp
from jax import lax
from jax.experimental import pallas as pl
from jax.experimental.pallas import tpu as pltpu
from jax.sharding import PartitionSpec as P

ORDER = 24

hop_angle = 0.3
coupling = 0.2
stiffness = 1.0
mass_term = 0.5
relaxation = 0.25
step_size = 0.25
cheb_base = 4.03
cheb_slope = 0.5
half_width = 4.0

EDGE = 4
HALO = 2 * EDGE
LANES = 128
EXACT = lax.Precision.HIGHEST
AXES = ("tm", "band")


def shifted(value, dt, db):
    tm, band = lax.axis_size("tm"), lax.axis_size("band")
    pairs = [
        (((t + dt) % tm) * band + (b + db) % band, t * band + b)
        for t in range(tm)
        for b in range(band)
    ]
    return lax.ppermute(value, AXES, pairs)


def band_halo(tile, dt):
    if lax.axis_size("band") == 2:
        return shifted(tile, dt, 1)
    after = shifted(tile[..., :EDGE, :], dt, 1)
    before = shifted(tile[..., EDGE:, :], dt, -1)
    return jnp.concatenate([after, before], -2)


def time_basis(slices, at):
    k = np.arange(slices)[:, None]
    phase = (2 * (k // 2) + 1) * np.asarray(at)[None, :] % (2 * slices)
    angle = phase * (math.pi / slices)
    return math.sqrt(2.0 / slices) * np.where(k % 2 == 0, np.cos(angle), np.sin(angle))


def space_basis(length, at):
    mode = np.arange(length)[:, None]
    freq = (mode + 1) // 2
    angle = (freq * np.asarray(at)[None, :] % length) * (2.0 * math.pi / length)
    wave = np.where((mode % 2 == 0) & (mode > 0), np.sin(angle), np.cos(angle))
    norm = np.where((mode == 0) | (2 * freq == length), 1.0, 2.0)
    return np.sqrt(norm / length) * wave


def cheb_t(order, x):
    if order == 0:
        return jnp.ones_like(x)
    if order == 1:
        return x
    if order % 2 == 0:
        half = cheb_t(order // 2, x)
        return 2.0 * half * half - 1.0
    return 2.0 * cheb_t((order + 1) // 2, x) * cheb_t(order // 2, x) - x


def parities(shape):
    row = lax.broadcasted_iota(jnp.int32, shape, 0) % 2 == 0
    col = lax.broadcasted_iota(jnp.int32, shape, 1) % 2 == 0
    return row, col


def turned(value, by, axis):
    return pltpu.roll(value, by % value.shape[axis], axis)


def pair_tables(horizontal, vertical, row_even, col_even):
    h_prev = turned(horizontal, 1, 1)
    v_prev = turned(vertical, 1, 0)
    strengths = (
        jnp.where(col_even, horizontal, h_prev),
        jnp.where(col_even, h_prev, horizontal),
        jnp.where(row_even, vertical, v_prev),
        jnp.where(row_even, v_prev, vertical),
    )
    grow, mix = math.cosh(hop_angle) - 1.0, math.sinh(hop_angle)
    return tuple((1.0 + grow * s, mix * s) for s in strengths)


def apply_pairs(vector, colours, tables, row_even, col_even):
    for colour in colours:
        axis = 1 if colour < 2 else 0
        even = col_even if colour < 2 else row_even
        ahead, behind = turned(vector, -1, axis), turned(vector, 1, axis)
        first, second = (ahead, behind) if colour % 2 == 0 else (behind, ahead)
        cosh_part, sinh_part = tables[colour]
        vector = cosh_part * vector + sinh_part * jnp.where(even, first, second)
    return vector


FORWARD = (0, 1, 2, 3)
BACKWARD = (3, 2, 1, 0)


def wide(main, halo):
    return jnp.concatenate([main, halo], 0)


def last_sign():
    at_end = lax.axis_index("tm") == lax.axis_size("tm") - 1
    return jnp.where(at_end, -1.0, 1.0).astype(jnp.float32)


def setting(phonon, bonds, edges):
    slices, rows, cols = phonon.shape
    parity = parities((rows + HALO, cols))
    horizontal = wide(bonds[0].astype(jnp.float32), edges[2 * slices])
    vertical = wide(bonds[1].astype(jnp.float32), edges[2 * slices + 1])
    tables = pair_tables(horizontal, vertical, *parity)
    expo = [jnp.exp(-coupling * wide(phonon[s], edges[slices + s])) for s in range(slices)]
    return parity, tables, expo


def residual_kernel(phonon, source, guess, bonds, edges, after, after_edge, basis, out):
    slices, rows, cols = guess.shape
    parity, tables, expo = setting(phonon, bonds, edges)
    field = [wide(guess[s], edges[s]) for s in range(slices)]
    field.append(last_sign() * wide(after[0], after_edge[0]))
    pieces = []
    for s in range(slices):
        applied = apply_pairs(expo[s] * field[s], FORWARD, tables, *parity)
        link = field[s + 1] - applied
        back = expo[s] * apply_pairs(link, BACKWARD, tables, *parity)
        own = field[s] if s == 0 else own_link
        pieces.append(source[s] - own[:rows] + back[:rows])
        own_link = link
    pieces.append(applied[:rows])
    stacked = jnp.concatenate(pieces, 0)
    out[...] = lax.dot_general(
        basis[...], stacked, (((1,), (1,)), ((), ())),
        precision=EXACT, preferred_element_type=jnp.float32,
    )


def mode_kernel(count, mixed, times, times_back, rows_in, rows_out, out):
    tm, band, modes, width = mixed.shape
    freqs = times.shape[0] // modes
    length = rows_in.shape[0]
    per = length // band
    slots = width // per

    def dot(a, b):
        return jnp.dot(a, b, precision=EXACT, preferred_element_type=jnp.float32)

    stacked = jnp.concatenate(
        [
            jnp.concatenate(
                [mixed[:, b, :, s * per : (s + 1) * per].reshape(tm * modes, per) for b in range(band)],
                1,
            )
            for s in range(slots)
        ],
        0,
    )
    waves = dot(dot(times[...], stacked), rows_in[...])

    place = lax.axis_index("tm") * band + lax.axis_index("band")
    shape = (modes, length)
    column = place * modes + lax.broadcasted_iota(jnp.int32, shape, 0)
    row = lax.broadcasted_iota(jnp.int32, shape, 1)
    sine_c = jnp.sin(((column + 1) // 2).astype(jnp.float32) * (math.pi / count))
    sine_r = jnp.sin(((row + 1) // 2).astype(jnp.float32) * (math.pi / length))
    depth = sine_c * sine_c + sine_r * sine_r
    top = cheb_t(ORDER, 1.0 - depth * (4.0 / half_width))
    gains = []
    for k in range(freqs):
        if k % 2 == 0:
            lift = cheb_slope * (1.0 - math.cos((k + 1) * math.pi / freqs))
            damp = 1.0 / math.cosh(ORDER * math.acosh((cheb_base + lift) / half_width))
            gain = (1.0 - damp * top) / (4.0 * depth + (cheb_base - 4.0 + lift))
        gains.append(gain)
    waves = waves * jnp.concatenate(gains, 0)

    back = dot(times_back[...], dot(waves, rows_out[...]))
    size = tm * modes
    lane = lax.broadcasted_iota(jnp.int32, (size, LANES), 1)
    for b in range(band):
        rims = back[:size, length + b * LANES : length + (b + 1) * LANES]
        for s in range(slots):
            block = back[s * size : (s + 1) * size]
            out[:, b, :, s * per : (s + 1) * per] = block[:, b * per : (b + 1) * per].reshape(tm, modes, per)
            rims = jnp.where(lane < s * HALO, rims, block[:, length + b * LANES : length + (b + 1) * LANES])
        out[:, b, :, slots * per :] = rims.reshape(tm, modes, LANES)


def force_kernel(phonon, momentum, guess, bonds, edges, after, after_edge, before_ph, after_ph, mixed, basis, sol, mom):
    slices, rows, cols = guess.shape
    parity, tables, expo = setting(phonon, bonds, edges)
    timed = lax.dot_general(
        mixed[...], basis[...], (((0,), (0,)), ((), ())),
        precision=EXACT, preferred_element_type=jnp.float32,
    )
    base = (slices + 1) * rows
    start = [wide(guess[s], edges[s]) for s in range(slices)]
    start.append(last_sign() * wide(after[0], after_edge[0]))
    field = []
    for s in range(slices + 1):
        change = wide(timed[s * rows : (s + 1) * rows], timed[base + s * HALO : base + (s + 1) * HALO])
        field.append(start[s] + relaxation * change)
    for s in range(slices):
        applied = apply_pairs(expo[s] * field[s], FORWARD, tables, *parity)
        image = field[s + 1] - applied
        pulled = apply_pairs(image, BACKWARD, tables, *parity)[:rows]
        own = field[s][:rows]
        sol[s] = own
        fermion = -2.0 * coupling * expo[s][:rows] * own * pulled
        left = before_ph[0] if s == 0 else phonon[s - 1]
        right = after_ph[0] if s == slices - 1 else phonon[s + 1]
        boson = stiffness * (2.0 * phonon[s] - left - right) + mass_term * phonon[s]
        mom[s] = momentum[s] - step_size * (boson + fermion)


def call(kernel, outs, *operands):
    vmem = pl.BlockSpec(memory_space=pltpu.VMEM)
    return pl.pallas_call(
        kernel,
        out_shape=outs,
        in_specs=[vmem] * len(operands),
        out_specs=jax.tree.map(lambda _: vmem, outs),
    )(*operands)


def rims_of(value):
    return jnp.concatenate([value[:, :EDGE], value[:, -EDGE:]], 1)


def shards(phonon, momentum, source, guess, bonds):
    slices, rows, cols = guess.shape
    tm, band = lax.axis_size("tm"), lax.axis_size("band")
    total, length, devices = tm * slices, rows * band, tm * band
    modes = cols // devices
    f32 = functools.partial(np.asarray, dtype=np.float32)

    slot_times = np.concatenate([time_basis(total, slices * np.arange(tm) + s) for s in range(slices + 1)], 1)
    times = f32(np.kron(slot_times, np.eye(modes)))
    rim = np.arange(HALO)
    rim_rows = []
    for b in range(band):
        row = np.where(rim < EDGE, (b + 1) * rows + rim, b * rows + rim - HALO) % length
        rim_rows.append(np.resize(row, LANES))
    rows_in = f32(space_basis(length, np.arange(length)).T)
    rows_out = f32(space_basis(length, np.concatenate([np.arange(length)] + rim_rows)))
    columns = f32(space_basis(cols, np.arange(cols)))

    rims = jnp.concatenate([rims_of(guess), rims_of(phonon), rims_of(bonds).astype(jnp.float32)], 0)
    edges = band_halo(rims, 0)
    after = shifted(guess[:1], 1, 0)
    after_edge = band_halo(rims[:1], 1)

    width = (slices + 1) * rows
    sent = call(
        residual_kernel, jax.ShapeDtypeStruct((cols, width), jnp.float32),
        phonon, source, guess, bonds, edges, after, after_edge, columns,
    )
    mixed = lax.all_to_all(sent.reshape(devices, modes, width), AXES, 0, 0, tiled=True)
    after_ph = shifted(phonon[:1], 1, 0)
    before_ph = shifted(phonon[-1:], -1, 0)
    back = call(
        functools.partial(mode_kernel, cols),
        jax.ShapeDtypeStruct((tm, band, modes, width + LANES), jnp.float32),
        mixed.reshape(tm, band, modes, width), times, np.ascontiguousarray(times.T), rows_in, rows_out,
    )
    mixed = lax.all_to_all(back.reshape(devices, modes, width + LANES), AXES, 0, 0, tiled=True)
    like = jax.ShapeDtypeStruct(guess.shape, jnp.float32)
    return call(
        force_kernel, (like, like),
        phonon, momentum, guess, bonds, edges, after, after_edge, before_ph, after_ph,
        mixed.reshape(cols, width + LANES), columns,
    )


def solution(mesh):
    spec = P("tm", "band", None)
    return jax.shard_map(
        shards,
        mesh=mesh,
        in_specs=(spec, spec, spec, spec, P(None, "band", None)),
        out_specs=(spec, spec),
        check_vma=False,
    )
```

time: 158 us -> 66.4 us (0.42)
  the two profiles are of different devices: /device:TPU:0 before, /device:TPU:1 now
where the time goes in v1:
time: 66.4 us; the launch traced here: 65.9 us
  blocking collectives  19.5 us (29%)
  waiting for transfers between devices  16.3 us (25%)
  Pallas kernels  12.6 us (19%)
  starting transfers between devices  11.5 us (17%)
  local copies, waits for them, and re-layouts  5.22 us (8%)
  between operations  0.68 us (1%)
    all_to_all x1, blocking collectives, shards(): lax.all_to_all(sent.reshape(devices, modes, width), AXES, 0, 0, tiled=True)  19.5 us
    pallas_call x3, Pallas kernels, call(): pl.pallas_call(kernel, out_shape=outs, in_specs=[vmem] * len(operands), o...  12.6 us
    ppermute x5, starting transfers between devices, shifted(): return lax.ppermute(value, AXES, pairs)  8.93 us
    all_to_all x1, waiting for transfers between devices, shards(): lax.all_to_all(back.reshape(devices, modes, width + LANES), AXES, 0, 0, t...  8.24 us
    ppermute x5, waiting for transfers between devices, shifted(): return lax.ppermute(value, AXES, pairs)  8.08 us
    all_to_all x1, starting transfers between devices, shards(): lax.all_to_all(back.reshape(devices, modes, width + LANES), AXES, 0, 0, t...  2.61 us
    slice x3, local copies, waits for them, and re-layouts, rims_of(): return jnp.concatenate([value[:, :EDGE], value[:, -EDGE:]], 1)  2.22 us
    unnamed x14, local copies, waits for them, and re-layouts  2.06 us
  transfers between devices with their start and end apart: 6, of which 4 were waited for; matrix products, arithmetic and copies ran while one was open for 3% of the time, Pallas kernels for 0%

profile of v1, /device:TPU:1, one launch (start us, length us, event | category | flops | bytes accessed | tf_op | source)
XLA Modules:
  0.0 65.9 jit_solution(6526794645150477509)
XLA Ops:
  0.6 0.9 %slice.36 = f32[1,128,256]{2,1,0:T(8,128)S(1)} slice(f32[2,128,256]{2,1,0:T(8,128)} %guess.3), slice={[0:1], [0:128], [0:256]} | slice | bytes 262144 | tf_op jit(solution)/shard_map/slice | solution.py:267
  1.5 0.1 collective-permute-start.1
  1.6 0.7 %fusion.1 = (f32[2,4,256]{2,1,0:T(4,128)S(1)}, f32[2,4,256]{2,1,0:T(4,128)S(1)}) fusion(f32[2,128,256]{2,1,0:T(8,128)} %guess.3), kind=kLoop, calls=%fused_computation.4 | loop fusion | bytes 32768 | tf_op jit(solution)/shard_map/slice | solution.py:244
  2.4 0.7 %fusion.3 = (s32[2,4,256]{2,1,0:T(4,128)S(1)}, s32[2,4,256]{2,1,0:T(4,128)S(1)}) fusion(s32[2,128,256]{2,1,0:T(8,128)} %bonds.3), kind=kLoop, calls=%fused_computation.6 | loop fusion | bytes 32768 | tf_op jit(solution)/shard_map/slice | solution.py:244
  3.1 0.7 %fusion.2 = (f32[2,4,256]{2,1,0:T(4,128)S(1)}, f32[2,4,256]{2,1,0:T(4,128)S(1)}) fusion(f32[2,128,256]{2,1,0:T(8,128)} %phonon.3), kind=kLoop, calls=%fused_computation.5 | loop fusion | bytes 32768 | tf_op jit(solution)/shard_map/slice | solution.py:244
  3.9 2.8 %collective-permute-start = (f32[6,8,256]{2,1,0:T(8,128)S(1)}, f32[6,8,256]{2,1,0:T(8,128)S(1)}, u32[]{:S(2)}, u32[]{:S(2)}) collective-permute-start(f32[6,8,256]{2,1,0:T(8,128)S(1)} %pad_maximum_fusion), channel_id=1, source_target_pairs={{1,0},{0,1},{3,2},{2,3},{5,4},{4,5},{7,6},{6,7},{9,8},{8,9},{11,10... | collective-permute-start | bytes 147464 | tf_op jit(solution)/shard_map/ppermute | solution.py:39
  6.6 4.4 %collective-permute-start.2 = (f32[1,8,256]{2,1,0:T(8,128)S(1)}, f32[1,8,256]{2,1,0:T(8,128)S(1)}, u32[]{:S(2)}, u32[]{:S(2)}) collective-permute-start(f32[1,8,256]{2,1,0:T(8,128)S(1)} %pad_maximum_fusion.1), channel_id=1, source_target_pairs={{3,0},{2,1},{5,2},{4,3},{7,4},{6,5},{9,6},{8,7},{11,8},{10,9},{13,... | collective-permute-start | bytes 24584 | tf_op jit(solution)/shard_map/ppermute | solution.py:39
  11.0 0.8 %collective-permute-done.2.after_edge = f32[1,8,256]{2,1,0:T(8,128)S(1)} collective-permute-done((f32[1,8,256]{2,1,0:T(8,128)S(1)}, f32[1,8,256]{2,1,0:T(8,128)S(1)}, u32[]{:S(2)}, u32[]{:S(2)}) %collective-permute-start.2) | collective-permute-done | bytes 8224 | tf_op jit(solution)/shard_map/ppermute | solution.py:39
  11.8 0.0 copy-start.6
  11.8 0.0 collective-permute-done.edges
  11.8 0.0 copy-start.3
  11.8 0.0 collective-permute-done.1.after
  11.9 0.6 copy-done.6
  12.4 0.0 copy-done.3
  12.5 0.0 copy-start.2
  12.5 0.7 copy-done.2
  13.1 3.7 %shard_map.113 = f32[256,384]{1,0:T(8,128)} custom-call(f32[2,128,256]{2,1,0:T(8,128)} %phonon.3, f32[2,128,256]{2,1,0:T(8,128)} %source.1, f32[2,128,256]{2,1,0:T(8,128)} %guess.3, s32[2,128,256]{2,1,0:T(8,128)} %bonds.3, f32[6,8,256]{2,1,0:T(8,128)} %copy-done.3, f32[1,128,256]{2,1,0:T(8,128)} %copy-done.2, f32[1,8,256]{2,1,0:T(8,128)} %copy-done.6, ...), custom_call_target="tpu_custom_call" | custom-call | tf_op jit(solution)/shard_map/pallas_call | solution.py:235
  16.8 19.5 %all_to_all.10 = f32[32,8,384]{2,1,0:T(8,128)} all-to-all(f32[32,8,384]{2,1,0:T(8,128)} %bitcast.7), channel_id=1, replica_groups=mesh['tm'=16,'band'=2] {'tm','band'}, dimensions={0} | all-to-all | bytes 786432 | tf_op jit(solution)/shard_map/all_to_all | solution.py:275
  36.3 5.2 %shard_map.114 = f32[16,2,8,512]{3,2,1,0:T(8,128)} custom-call(f32[16,2,8,384]{3,2,1,0:T(8,128)} %bitcast.6, f32[256,384]{1,0:T(8,128)} %constant.11.clone.times, f32[384,256]{1,0:T(8,128)} %constant.12.clone.times_back, f32[256,256]{1,0:T(8,128)} %constant.13.clone.rows_in, f32[256,512]{1,0:T(8,128)} %constant.14.clone.rows_out), custom_call_target="tpu_custom_call" | custom-call | tf_op jit(solution)/shard_map/pallas_call | solution.py:235
  41.5 0.0 copy-start
  41.5 2.6 %all-to-all-start.1 = ((f32[32,8,512]{2,1,0:T(8,128)}), f32[32,8,512]{2,1,0:T(8,128)S(1)}, u32[]{:S(2)}, u32[]{:S(2)}) async-start(f32[32,8,512]{2,1,0:T(8,128)} %bitcast.4), calls=%async_computation.1 | async-start | bytes 1048576 | tf_op jit(solution)/shard_map/all_to_all | solution.py:283
  44.1 0.0 copy-done
  44.1 1.7 %collective-permute-start.3 = (f32[1,128,256]{2,1,0:T(8,128)S(1)}, f32[1,128,256]{2,1,0:T(8,128)S(1)}, u32[]{:S(2)}, u32[]{:S(2)}) collective-permute-start(f32[1,128,256]{2,1,0:T(8,128)S(1)} %get-tuple-element.3), channel_id=1, source_target_pairs={{30,0},{31,1},{0,2},{1,3},{2,4},{3,5},{4,6},{5,7},{6,8},{7,9},{8,1... | collective-permute-start | bytes 393224 | tf_op jit(solution)/shard_map/ppermute | solution.py:39
  45.8 0.0 collective-permute-start.4
  45.8 6.6 %collective-permute-done.3.before_ph = f32[1,128,256]{2,1,0:T(8,128)S(1)} collective-permute-done((f32[1,128,256]{2,1,0:T(8,128)S(1)}, f32[1,128,256]{2,1,0:T(8,128)S(1)}, u32[]{:S(2)}, u32[]{:S(2)}) %collective-permute-start.3) | collective-permute-done | bytes 131104 | tf_op jit(solution)/shard_map/ppermute | solution.py:39
  52.5 0.0 copy-start.4
  52.5 0.6 collective-permute-done.4.after_ph
  53.1 0.0 copy-start.5
  53.1 8.2 %all-to-all-done.1 = f32[32,8,512]{2,1,0:T(8,128)S(1)} async-done(((f32[32,8,512]{2,1,0:T(8,128)}), f32[32,8,512]{2,1,0:T(8,128)S(1)}, u32[]{:S(2)}, u32[]{:S(2)}) %all-to-all-start.1) | async-done | bytes 524320 | tf_op jit(solution)/shard_map/all_to_all | solution.py:283
  61.4 0.0 copy-start.1
  61.4 0.0 copy-done.4
  61.4 0.0 copy-done.5
  61.4 0.8 %copy-done.1 = f32[32,8,512]{2,1,0:T(8,128)} copy-done((f32[32,8,512]{2,1,0:T(8,128)}, f32[32,8,512]{2,1,0:T(8,128)S(1)}, u32[]{:S(2)}) %copy-start.1) | copy-done | bytes 524312
  62.2 3.7 %shard_map.115 = (f32[2,128,256]{2,1,0:T(8,128)}, f32[2,128,256]{2,1,0:T(8,128)}) custom-call(f32[2,128,256]{2,1,0:T(8,128)} %phonon.3, f32[2,128,256]{2,1,0:T(8,128)} %momentum.1, f32[2,128,256]{2,1,0:T(8,128)} %guess.3, s32[2,128,256]{2,1,0:T(8,128)} %bonds.3, f32[6,8,256]{2,1,0:T(8,128)} %copy-done.3, f32[1,128,256]{2,1,0:T(8,128)} %copy-done.2, ...), custom_call_target="tpu_custom_call" | custom-call | tf_op jit(solution)/shard_map/pallas_call | solution.py:235
  (4 shorter events, 0.1 us)
Async XLA Ops:
  1.5 10.3 %collective-permute-start.1 = (f32[1,128,256]{2,1,0:T(8,128)S(1)}, f32[1,128,256]{2,1,0:T(8,128)S(1)}, u32[]{:S(2)}, u32[]{:S(2)}) collective-permute-start(f32[1,128,256]{2,1,0:T(8,128)S(1)} %slice.36), channel_id=1, source_target_pairs={{2,0},{3,1},{4,2},{5,3},{6,4},{7,5},{8,6},{9,7},{10,8},{11,9},{12,... | collective-permute-start | bytes 393224 | tf_op jit(solution)/shard_map/ppermute | solution.py:39
  3.9 8.0 %collective-permute-start = (f32[6,8,256]{2,1,0:T(8,128)S(1)}, f32[6,8,256]{2,1,0:T(8,128)S(1)}, u32[]{:S(2)}, u32[]{:S(2)}) collective-permute-start(f32[6,8,256]{2,1,0:T(8,128)S(1)} %pad_maximum_fusion), channel_id=1, source_target_pairs={{1,0},{0,1},{3,2},{2,3},{5,4},{4,5},{7,6},{6,7},{9,8},{8,9},{11,10... | collective-permute-start | bytes 147464 | tf_op jit(solution)/shard_map/ppermute | solution.py:39
  6.6 5.2 %collective-permute-start.2 = (f32[1,8,256]{2,1,0:T(8,128)S(1)}, f32[1,8,256]{2,1,0:T(8,128)S(1)}, u32[]{:S(2)}, u32[]{:S(2)}) collective-permute-start(f32[1,8,256]{2,1,0:T(8,128)S(1)} %pad_maximum_fusion.1), channel_id=1, source_target_pairs={{3,0},{2,1},{5,2},{4,3},{7,4},{6,5},{9,6},{8,7},{11,8},{10,9},{13,... | collective-permute-start | bytes 24584 | tf_op jit(solution)/shard_map/ppermute | solution.py:39
  11.8 0.6 copy-start.6
  11.8 0.6 copy-start.3
  12.5 0.7 copy-start.2
  41.5 2.6 %copy-start = (f32[2,128,256]{2,1,0:T(8,128)S(1)}, f32[2,128,256]{2,1,0:T(8,128)}, u32[]{:S(2)}) copy-start(f32[2,128,256]{2,1,0:T(8,128)} %phonon.3) | copy-start | bytes 786436
  41.5 19.9 %all-to-all-start.1 = ((f32[32,8,512]{2,1,0:T(8,128)}), f32[32,8,512]{2,1,0:T(8,128)S(1)}, u32[]{:S(2)}, u32[]{:S(2)}) async-start(f32[32,8,512]{2,1,0:T(8,128)} %bitcast.4), calls=%async_computation.1 | async-start | bytes 1048576 | tf_op jit(solution)/shard_map/all_to_all | solution.py:283
  44.1 8.3 %collective-permute-start.3 = (f32[1,128,256]{2,1,0:T(8,128)S(1)}, f32[1,128,256]{2,1,0:T(8,128)S(1)}, u32[]{:S(2)}, u32[]{:S(2)}) collective-permute-start(f32[1,128,256]{2,1,0:T(8,128)S(1)} %get-tuple-element.3), channel_id=1, source_target_pairs={{30,0},{31,1},{0,2},{1,3},{2,4},{3,5},{4,6},{5,7},{6,8},{7,9},{8,1... | collective-permute-start | bytes 393224 | tf_op jit(solution)/shard_map/ppermute | solution.py:39
  45.8 7.3 %collective-permute-start.4 = (f32[1,128,256]{2,1,0:T(8,128)S(1)}, f32[1,128,256]{2,1,0:T(8,128)S(1)}, u32[]{:S(2)}, u32[]{:S(2)}) collective-permute-start(f32[1,128,256]{2,1,0:T(8,128)S(1)} %get-tuple-element.2), channel_id=1, source_target_pairs={{2,0},{3,1},{4,2},{5,3},{6,4},{7,5},{8,6},{9,7},{10,8},{11,9},{12,... | collective-permute-start | bytes 393224 | tf_op jit(solution)/shard_map/ppermute | solution.py:39
  52.5 8.9 %copy-start.4 = (f32[1,128,256]{2,1,0:T(8,128)}, f32[1,128,256]{2,1,0:T(8,128)S(1)}, u32[]{:S(2)}) copy-start(f32[1,128,256]{2,1,0:T(8,128)S(1)} %collective-permute-done.3.before_ph) | copy-start | bytes 393220
  53.1 8.2 %copy-start.5 = (f32[1,128,256]{2,1,0:T(8,128)}, f32[1,128,256]{2,1,0:T(8,128)S(1)}, u32[]{:S(2)}) copy-start(f32[1,128,256]{2,1,0:T(8,128)S(1)} %collective-permute-done.4.after_ph) | copy-start | bytes 393220
  61.4 0.8 %copy-start.1 = (f32[32,8,512]{2,1,0:T(8,128)}, f32[32,8,512]{2,1,0:T(8,128)S(1)}, u32[]{:S(2)}) copy-start(f32[32,8,512]{2,1,0:T(8,128)S(1)} %all-to-all-done.1) | copy-start | bytes 1572868

commit v2 on v1

--- a/solution.py
+++ b/solution.py
@@ -237,11 +237,42 @@
         out_shape=outs,
         in_specs=[vmem] * len(operands),
         out_specs=jax.tree.map(lambda _: vmem, outs),
-    )(*operands)
-
-
-def rims_of(value):
-    return jnp.concatenate([value[:, :EDGE], value[:, -EDGE:]], 1)
+    )(*map(onchip, operands))
+
+
+def onchip(value):
+    return pltpu.with_memory_space_constraint(value, pltpu.VMEM)
+
+
+def pack_kernel(guess, *refs):
+    tops, ends, outs = refs[:3], refs[3:6], refs[6:]
+    first, rims, rim = outs
+    first[...] = guess[...]
+    early = lax.broadcasted_iota(jnp.int32, tops[0].shape, 1) < EDGE
+    at = 0
+    for top, end in zip(tops, ends):
+        both = jnp.where(early, top[...], end[...]).astype(jnp.float32)
+        rims[at : at + top.shape[0]] = both
+        if at == 0:
+            rim[...] = both[:1]
+        at += top.shape[0]
+
+
+def pack(phonon, guess, bonds):
+    slices, rows, cols = guess.shape
+    fields = (guess, phonon, bonds)
+    last = rows // HALO - 1
+    whole = lambda shape: pl.BlockSpec(shape, lambda i: (0, 0, 0))
+    tops = [whole((v.shape[0], HALO, cols)) for v in fields]
+    ends = [pl.BlockSpec((v.shape[0], HALO, cols), lambda i: (0, last, 0)) for v in fields]
+    outs = [(1, rows, cols), (2 * slices + 2, HALO, cols), (1, HALO, cols)]
+    return pl.pallas_call(
+        pack_kernel,
+        grid=(1,),
+        out_shape=[pltpu.VMEM(o, jnp.float32) for o in outs],
+        in_specs=[whole((1, rows, cols))] + tops + ends,
+        out_specs=[whole(o) for o in outs],
+    )(guess, *fields, *fields)
 
 
 def shards(phonon, momentum, source, guess, bonds):
@@ -262,10 +293,10 @@
     rows_out = f32(space_basis(length, np.concatenate([np.arange(length)] + rim_rows)))
     columns = f32(space_basis(cols, np.arange(cols)))
 
-    rims = jnp.concatenate([rims_of(guess), rims_of(phonon), rims_of(bonds).astype(jnp.float32)], 0)
+    first, rims, rim = pack(phonon, guess, bonds)
     edges = band_halo(rims, 0)
-    after = shifted(guess[:1], 1, 0)
-    after_edge = band_halo(rims[:1], 1)
+    after = shifted(first, 1, 0)
+    after_edge = band_halo(rim, 1)
 
     width = (slices + 1) * rows
     sent = call(

time: 66.4 us -> 58.7 us (0.88)
  local copies, waits for them, and re-layouts: 5.22 us -> 1.06 us
  Pallas kernels: 12.6 us -> 9.33 us
    pallas_call x3, Pallas kernels: 12.6 us -> 8.25 us  [call(): pl.pallas_call(kernel, out_shape=outs, in_specs=[vmem] * len(operands), o...]
    slice x4 -> x0, local copies, waits for them, and re-layouts: 3.13 us -> none  [the longest x3 2.22 us: rims_of(): return jnp.concatenate([value[:, :EDGE], value[:, -EDGE:]], 1)]
    pallas_call x0 -> x1, Pallas kernels: none -> 1.07 us  [pack(): pl.pallas_call(pack_kernel, grid=(1,), out_shape=[pltpu.VMEM(o, jnp.float...]
    unnamed x14 -> x20, local copies, waits for them, and re-layouts: 2.06 us -> 1.04 us
  transfers between devices with their start and end apart: 6 -> 6, of which waited for: 4 -> 4; matrix products, arithmetic and copies ran while one was open for 3% -> 0% of each run, Pallas kernels for 0% -> 0%
where the time goes in v2:
time: 58.7 us; the launch traced here: 58.4 us
  blocking collectives  19.4 us (33%)
  waiting for transfers between devices  16.3 us (28%)
  starting transfers between devices  11.5 us (20%)
  Pallas kernels  9.33 us (16%)
  local copies, waits for them, and re-layouts  1.06 us (2%)
  between operations  0.76 us (1%)
    all_to_all x1, blocking collectives, shards(): lax.all_to_all(sent.reshape(devices, modes, width), AXES, 0, 0, tiled=True)  19.4 us
    ppermute x5, starting transfers between devices, shifted(): return lax.ppermute(value, AXES, pairs)  8.86 us
    pallas_call x3, Pallas kernels, call(): pl.pallas_call(kernel, out_shape=outs, in_specs=[vmem] * len(operands), o...  8.25 us
    all_to_all x1, waiting for transfers between devices, shards(): lax.all_to_all(back.reshape(devices, modes, width + LANES), AXES, 0, 0, t...  8.24 us
    ppermute x5, waiting for transfers between devices, shifted(): return lax.ppermute(value, AXES, pairs)  8.08 us
    all_to_all x1, starting transfers between devices, shards(): lax.all_to_all(back.reshape(devices, modes, width + LANES), AXES, 0, 0, t...  2.61 us
  transfers between devices with their start and end apart: 6, of which 4 were waited for; matrix products, arithmetic and copies ran while one was open for 0% of the time, Pallas kernels for 0%

profile of v2, /device:TPU:1, one launch (start us, length us, event | category | flops | bytes accessed | tf_op | source)
XLA Modules:
  0.0 58.4 jit_solution(1431461125885011648)
XLA Ops:
  0.6 0.0 copy-start.3
  0.6 0.0 copy-start
  0.7 0.0 copy-start.1
  0.7 0.0 copy-start.2
  0.7 0.0 copy-start.9
  0.7 1.1 %shard_map.113 = (f32[1,128,256]{2,1,0:T(8,128)S(1)}, f32[6,8,256]{2,1,0:T(8,128)S(1)}, f32[1,8,256]{2,1,0:T(8,128)S(1)}) custom-call(f32[2,128,256]{2,1,0:T(8,128)} %guess.5, f32[2,128,256]{2,1,0:T(8,128)} %guess.5, f32[2,128,256]{2,1,0:T(8,128)} %phonon.3, s32[2,128,256]{2,1,0:T(8,128)} %bonds.3, f32[2,128,256]{2,1,0:T(8,128)} %guess.5, ...), custom_call_target="tpu_custom_call" | custom-call | tf_op jit(solution)/shard_map/pallas_call | solution.py:269
  1.8 0.1 collective-permute-start.1
  1.8 2.7 %collective-permute-start = (f32[6,8,256]{2,1,0:T(8,128)S(1)}, f32[6,8,256]{2,1,0:T(8,128)S(1)}, u32[]{:S(2)}, u32[]{:S(2)}) collective-permute-start(f32[6,8,256]{2,1,0:T(8,128)S(1)} %get-tuple-element.5), channel_id=1, source_target_pairs={{1,0},{0,1},{3,2},{2,3},{5,4},{4,5},{7,6},{6,7},{9,8},{8,9},{11,10... | collective-permute-start | bytes 147464 | tf_op jit(solution)/shard_map/ppermute | solution.py:39
  4.5 4.4 %collective-permute-start.2 = (f32[1,8,256]{2,1,0:T(8,128)S(1)}, f32[1,8,256]{2,1,0:T(8,128)S(1)}, u32[]{:S(2)}, u32[]{:S(2)}) collective-permute-start(f32[1,8,256]{2,1,0:T(8,128)S(1)} %get-tuple-element.7), channel_id=1, source_target_pairs={{3,0},{2,1},{5,2},{4,3},{7,4},{6,5},{9,6},{8,7},{11,8},{10,9},{13,... | collective-permute-start | bytes 24584 | tf_op jit(solution)/shard_map/ppermute | solution.py:39
  8.9 0.8 %collective-permute-done.2.after_edge = f32[1,8,256]{2,1,0:T(8,128)S(1)} collective-permute-done((f32[1,8,256]{2,1,0:T(8,128)S(1)}, f32[1,8,256]{2,1,0:T(8,128)S(1)}, u32[]{:S(2)}, u32[]{:S(2)}) %collective-permute-start.2) | collective-permute-done | bytes 8224 | tf_op jit(solution)/shard_map/ppermute | solution.py:39
  9.7 0.0 collective-permute-done.edges
  9.7 0.0 collective-permute-done.1.after
  9.7 0.0 copy-done.3
  9.7 0.0 copy-done
  9.8 0.0 copy-done.1
  9.8 0.0 copy-done.2
  9.8 0.0 copy-done.9
  9.8 0.0 copy-start.5
  9.8 2.3 %shard_map.114 = f32[256,384]{1,0:T(8,128)} custom-call(f32[2,128,256]{2,1,0:T(8,128)S(1)} %copy-done, f32[2,128,256]{2,1,0:T(8,128)S(1)} %copy-done.9, f32[2,128,256]{2,1,0:T(8,128)S(1)} %copy-done.1, s32[2,128,256]{2,1,0:T(8,128)S(1)} %copy-done.2, f32[6,8,256]{2,1,0:T(8,128)S(1)} %collective-permute-done.edges, ...), custom_call_target="tpu_custom_call" | custom-call | tf_op jit(solution)/shard_map/pallas_call | solution.py:235
  12.1 0.0 copy-start.4
  12.1 0.0 copy-start.8
  12.1 19.4 %all_to_all.10 = f32[32,8,384]{2,1,0:T(8,128)S(1)} all-to-all(f32[32,8,384]{2,1,0:T(8,128)} %bitcast.7), channel_id=1, replica_groups=mesh['tm'=16,'band'=2] {'tm','band'}, dimensions={0} | all-to-all | bytes 786432 | tf_op jit(solution)/shard_map/all_to_all | solution.py:306
  31.5 0.0 copy-done.5
  31.6 0.0 copy-done.4
  31.6 0.0 copy-done.8
  31.6 0.0 copy-start.6
  31.6 1.0 %copy-done.6 = f32[384,256]{1,0:T(8,128)S(1)} copy-done((f32[384,256]{1,0:T(8,128)S(1)}, f32[384,256]{1,0:T(8,128)}, u32[]{:S(2)}) %copy-start.6) | copy-done | bytes 393240
  32.6 3.7 %shard_map.115 = f32[16,2,8,512]{3,2,1,0:T(8,128)} custom-call(f32[16,2,8,384]{3,2,1,0:T(8,128)S(1)} %bitcast.5, f32[256,384]{1,0:T(8,128)S(1)} %copy-done.5, f32[384,256]{1,0:T(8,128)S(1)} %copy-done.6, f32[256,256]{1,0:T(8,128)S(1)} %copy-done.8, f32[256,512]{1,0:T(8,128)S(1)} %copy-done.4), custom_call_target="tpu_custom_call" | custom-call | tf_op jit(solution)/shard_map/pallas_call | solution.py:235
  36.3 2.6 %all-to-all-start.1 = ((f32[32,8,512]{2,1,0:T(8,128)}), f32[32,8,512]{2,1,0:T(8,128)S(1)}, u32[]{:S(2)}, u32[]{:S(2)}) async-start(f32[32,8,512]{2,1,0:T(8,128)} %bitcast.6), calls=%async_computation.1 | async-start | bytes 1048576 | tf_op jit(solution)/shard_map/all_to_all | solution.py:314
  38.9 0.0 copy-start.7
  39.0 1.7 %collective-permute-start.3 = (f32[1,128,256]{2,1,0:T(8,128)S(1)}, f32[1,128,256]{2,1,0:T(8,128)S(1)}, u32[]{:S(2)}, u32[]{:S(2)}) collective-permute-start(f32[1,128,256]{2,1,0:T(8,128)S(1)} %get-tuple-element.9), channel_id=1, source_target_pairs={{30,0},{31,1},{0,2},{1,3},{2,4},{3,5},{4,6},{5,7},{6,8},{7,9},{8,1... | collective-permute-start | bytes 393224 | tf_op jit(solution)/shard_map/ppermute | solution.py:39
  40.6 0.0 collective-permute-start.4
  40.6 6.6 %collective-permute-done.3.before_ph = f32[1,128,256]{2,1,0:T(8,128)S(1)} collective-permute-done((f32[1,128,256]{2,1,0:T(8,128)S(1)}, f32[1,128,256]{2,1,0:T(8,128)S(1)}, u32[]{:S(2)}, u32[]{:S(2)}) %collective-permute-start.3) | collective-permute-done | bytes 131104 | tf_op jit(solution)/shard_map/ppermute | solution.py:39
  47.3 0.7 %collective-permute-done.4.after_ph = f32[1,128,256]{2,1,0:T(8,128)S(1)} collective-permute-done((f32[1,128,256]{2,1,0:T(8,128)S(1)}, f32[1,128,256]{2,1,0:T(8,128)S(1)}, u32[]{:S(2)}, u32[]{:S(2)}) %collective-permute-start.4) | collective-permute-done | bytes 131104 | tf_op jit(solution)/shard_map/ppermute | solution.py:39
  47.9 8.2 %all-to-all-done.1 = f32[32,8,512]{2,1,0:T(8,128)S(1)} async-done(((f32[32,8,512]{2,1,0:T(8,128)}), f32[32,8,512]{2,1,0:T(8,128)S(1)}, u32[]{:S(2)}, u32[]{:S(2)}) %all-to-all-start.1) | async-done | bytes 524320 | tf_op jit(solution)/shard_map/all_to_all | solution.py:314
  56.2 0.0 copy-done.7
  56.2 2.2 %shard_map.116 = (f32[2,128,256]{2,1,0:T(8,128)}, f32[2,128,256]{2,1,0:T(8,128)}) custom-call(f32[2,128,256]{2,1,0:T(8,128)S(1)} %copy-done, f32[2,128,256]{2,1,0:T(8,128)S(1)} %copy-done.7, f32[2,128,256]{2,1,0:T(8,128)S(1)} %copy-done.1, s32[2,128,256]{2,1,0:T(8,128)S(1)} %copy-done.2, f32[6,8,256]{2,1,0:T(8,128)S(1)} %collective-permute-done.edges, ...), custom_call_target="tpu_custom_call" | custom-call | tf_op jit(solution)/shard_map/pallas_call | solution.py:235
  (1 shorter events, 0.0 us)
Async XLA Ops:
  0.6 9.1 %copy-start.3 = (f32[256,256]{1,0:T(8,128)S(1)}, f32[256,256]{1,0:T(8,128)}, u32[]{:S(2)}) copy-start(f32[256,256]{1,0:T(8,128)} %constant.10.clone.basis) | copy-start | bytes 786436
  0.6 9.1 %copy-start = (f32[2,128,256]{2,1,0:T(8,128)S(1)}, f32[2,128,256]{2,1,0:T(8,128)}, u32[]{:S(2)}) copy-start(f32[2,128,256]{2,1,0:T(8,128)} %phonon.3) | copy-start | bytes 786436
  0.7 9.1 %copy-start.1 = (f32[2,128,256]{2,1,0:T(8,128)S(1)}, f32[2,128,256]{2,1,0:T(8,128)}, u32[]{:S(2)}) copy-start(f32[2,128,256]{2,1,0:T(8,128)} %guess.5) | copy-start | bytes 786436
  0.7 9.1 %copy-start.2 = (s32[2,128,256]{2,1,0:T(8,128)S(1)}, s32[2,128,256]{2,1,0:T(8,128)}, u32[]{:S(2)}) copy-start(s32[2,128,256]{2,1,0:T(8,128)} %bonds.3) | copy-start | bytes 786436
  0.7 9.1 %copy-start.9 = (f32[2,128,256]{2,1,0:T(8,128)S(1)}, f32[2,128,256]{2,1,0:T(8,128)}, u32[]{:S(2)}) copy-start(f32[2,128,256]{2,1,0:T(8,128)} %source.1) | copy-start | bytes 786436
  1.8 8.0 %collective-permute-start.1 = (f32[1,128,256]{2,1,0:T(8,128)S(1)}, f32[1,128,256]{2,1,0:T(8,128)S(1)}, u32[]{:S(2)}, u32[]{:S(2)}) collective-permute-start(f32[1,128,256]{2,1,0:T(8,128)S(1)} %get-tuple-element.6), channel_id=1, source_target_pairs={{2,0},{3,1},{4,2},{5,3},{6,4},{7,5},{8,6},{9,7},{10,8},{11,9},{12,... | collective-permute-start | bytes 393224 | tf_op jit(solution)/shard_map/ppermute | solution.py:39
  1.8 7.9 %collective-permute-start = (f32[6,8,256]{2,1,0:T(8,128)S(1)}, f32[6,8,256]{2,1,0:T(8,128)S(1)}, u32[]{:S(2)}, u32[]{:S(2)}) collective-permute-start(f32[6,8,256]{2,1,0:T(8,128)S(1)} %get-tuple-element.5), channel_id=1, source_target_pairs={{1,0},{0,1},{3,2},{2,3},{5,4},{4,5},{7,6},{6,7},{9,8},{8,9},{11,10... | collective-permute-start | bytes 147464 | tf_op jit(solution)/shard_map/ppermute | solution.py:39
  4.5 5.2 %collective-permute-start.2 = (f32[1,8,256]{2,1,0:T(8,128)S(1)}, f32[1,8,256]{2,1,0:T(8,128)S(1)}, u32[]{:S(2)}, u32[]{:S(2)}) collective-permute-start(f32[1,8,256]{2,1,0:T(8,128)S(1)} %get-tuple-element.7), channel_id=1, source_target_pairs={{3,0},{2,1},{5,2},{4,3},{7,4},{6,5},{9,6},{8,7},{11,8},{10,9},{13,... | collective-permute-start | bytes 24584 | tf_op jit(solution)/shard_map/ppermute | solution.py:39
  9.8 21.8 %copy-start.5 = (f32[256,384]{1,0:T(8,128)S(1)}, f32[256,384]{1,0:T(8,128)}, u32[]{:S(2)}) copy-start(f32[256,384]{1,0:T(8,128)} %constant.11.clone.times) | copy-start | bytes 1179652
  12.1 19.4 %copy-start.4 = (f32[256,512]{1,0:T(8,128)S(1)}, f32[256,512]{1,0:T(8,128)}, u32[]{:S(2)}) copy-start(f32[256,512]{1,0:T(8,128)} %constant.14.clone.rows_out) | copy-start | bytes 1572868
  12.1 19.4 %copy-start.8 = (f32[256,256]{1,0:T(8,128)S(1)}, f32[256,256]{1,0:T(8,128)}, u32[]{:S(2)}) copy-start(f32[256,256]{1,0:T(8,128)} %constant.13.clone.rows_in) | copy-start | bytes 786436
  31.6 1.0 %copy-start.6 = (f32[384,256]{1,0:T(8,128)S(1)}, f32[384,256]{1,0:T(8,128)}, u32[]{:S(2)}) copy-start(f32[384,256]{1,0:T(8,128)} %constant.12.clone.times_back) | copy-start | bytes 1179652
  36.3 19.9 %all-to-all-start.1 = ((f32[32,8,512]{2,1,0:T(8,128)}), f32[32,8,512]{2,1,0:T(8,128)S(1)}, u32[]{:S(2)}, u32[]{:S(2)}) async-start(f32[32,8,512]{2,1,0:T(8,128)} %bitcast.6), calls=%async_computation.1 | async-start | bytes 1048576 | tf_op jit(solution)/shard_map/all_to_all | solution.py:314
  38.9 17.3 %copy-start.7 = (f32[2,128,256]{2,1,0:T(8,128)S(1)}, f32[2,128,256]{2,1,0:T(8,128)}, u32[]{:S(2)}) copy-start(f32[2,128,256]{2,1,0:T(8,128)} %momentum.1) | copy-start | bytes 786436
  39.0 8.3 %collective-permute-start.3 = (f32[1,128,256]{2,1,0:T(8,128)S(1)}, f32[1,128,256]{2,1,0:T(8,128)S(1)}, u32[]{:S(2)}, u32[]{:S(2)}) collective-permute-start(f32[1,128,256]{2,1,0:T(8,128)S(1)} %get-tuple-element.9), channel_id=1, source_target_pairs={{30,0},{31,1},{0,2},{1,3},{2,4},{3,5},{4,6},{5,7},{6,8},{7,9},{8,1... | collective-permute-start | bytes 393224 | tf_op jit(solution)/shard_map/ppermute | solution.py:39
  40.6 7.3 %collective-permute-start.4 = (f32[1,128,256]{2,1,0:T(8,128)S(1)}, f32[1,128,256]{2,1,0:T(8,128)S(1)}, u32[]{:S(2)}, u32[]{:S(2)}) collective-permute-start(f32[1,128,256]{2,1,0:T(8,128)S(1)} %get-tuple-element.8), channel_id=1, source_target_pairs={{2,0},{3,1},{4,2},{5,3},{6,4},{7,5},{8,6},{9,7},{10,8},{11,9},{12,... | collective-permute-start | bytes 393224 | tf_op jit(solution)/shard_map/ppermute | solution.py:39

commit v3 on v2

v3 whole, which is shorter than its diff:
```python
import functools
import math

import numpy as np

import jax
import jax.numpy as jnp
from jax import lax
from jax.experimental import pallas as pl
from jax.experimental.pallas import tpu as pltpu
from jax.sharding import PartitionSpec as P

ORDER = 24

hop_angle = 0.3
coupling = 0.2
stiffness = 1.0
mass_term = 0.5
relaxation = 0.25
step_size = 0.25
cheb_base = 4.03
cheb_slope = 0.5
half_width = 4.0

EDGE = 4
HALO = 2 * EDGE
NEAR = 2
RIM = 2 * NEAR
AXES = ("tm", "band")
ROWS_BY_COLS = (((1,), (0,)), ((), ()))
ROWS_BY_ROWS = (((1,), (1,)), ((), ()))


def shifted(value, dt, db):
    tm, band = lax.axis_size("tm"), lax.axis_size("band")
    pairs = [
        (((t + dt) % tm) * band + (b + db) % band, t * band + b)
        for t in range(tm)
        for b in range(band)
    ]
    return lax.ppermute(value, AXES, pairs)


def band_halo(tile, dt):
    if lax.axis_size("band") == 2:
        return shifted(tile, dt, 1)
    after = shifted(tile[..., :EDGE, :], dt, 1)
    before = shifted(tile[..., EDGE:, :], dt, -1)
    return jnp.concatenate([after, before], -2)


def time_basis(slices, at):
    k = np.arange(slices)[:, None]
    phase = (2 * (k // 2) + 1) * np.asarray(at)[None, :] % (2 * slices)
    angle = phase * (math.pi / slices)
    return math.sqrt(2.0 / slices) * np.where(k % 2 == 0, np.cos(angle), np.sin(angle))


def space_basis(length, at):
    mode = np.arange(length)[:, None]
    freq = (mode + 1) // 2
    angle = (freq * np.asarray(at)[None, :] % length) * (2.0 * math.pi / length)
    wave = np.where((mode % 2 == 0) & (mode > 0), np.sin(angle), np.cos(angle))
    norm = np.where((mode == 0) | (2 * freq == length), 1.0, 2.0)
    return np.sqrt(norm / length) * wave


def cheb_t(order, x):
    if order == 0:
        return jnp.ones_like(x)
    if order == 1:
        return x
    if order % 2 == 0:
        half = cheb_t(order // 2, x)
        return 2.0 * half * half - 1.0
    return 2.0 * cheb_t((order + 1) // 2, x) * cheb_t(order // 2, x) - x


def parities(shape):
    row = lax.broadcasted_iota(jnp.int32, shape, 0) % 2 == 0
    col = lax.broadcasted_iota(jnp.int32, shape, 1) % 2 == 0
    return row, col


def turned(value, by, axis):
    return pltpu.roll(value, by % value.shape[axis], axis)


def pair_table(strengths, colour, row_even, col_even):
    axis = 1 if colour < 2 else 0
    even = col_even if colour < 2 else row_even
    here, before = strengths[1 - axis], turned(strengths[1 - axis], 1, axis)
    bond = jnp.where(even, here, before) if colour % 2 == 0 else jnp.where(even, before, here)
    return 1.0 + (math.cosh(hop_angle) - 1.0) * bond, math.sinh(hop_angle) * bond


def apply_pairs(vector, colours, tables, row_even, col_even):
    for colour in colours:
        axis = 1 if colour < 2 else 0
        even = col_even if colour < 2 else row_even
        ahead, behind = turned(vector, -1, axis), turned(vector, 1, axis)
        first, second = (ahead, behind) if colour % 2 == 0 else (behind, ahead)
        cosh_part, sinh_part = tables[colour]
        vector = cosh_part * vector + sinh_part * jnp.where(even, first, second)
    return vector


def last_sign():
    at_end = lax.axis_index("tm") == lax.axis_size("tm") - 1
    return jnp.where(at_end, -1.0, 1.0).astype(jnp.float32)


def halves(value):
    high = value.astype(jnp.bfloat16)
    return high, (value - high.astype(jnp.float32)).astype(jnp.bfloat16)


def const_halves(value):
    high = np.asarray(value, np.float32).astype(jnp.bfloat16)
    low = (value - high.astype(np.float64)).astype(np.float32).astype(jnp.bfloat16)
    return np.stack([high, low])


def product(a, b, dims=ROWS_BY_COLS):
    dot = functools.partial(lax.dot_general, dimension_numbers=dims, preferred_element_type=jnp.float32)
    return dot(a[0], b[0]) + (dot(a[0], b[1]) + dot(a[1], b[0]))


def wide(main, halo):
    return jnp.concatenate([main, halo], 0)


def local_kernel(phonon, guess, bonds, expo, tables, inner):
    slices, rows, cols = guess.shape
    parity = parities((rows, cols))
    strengths = (bonds[0].astype(jnp.float32), bonds[1].astype(jnp.float32))
    pairs = [pair_table(strengths, q, *parity) for q in range(3)]
    for q in range(3):
        for part in range(2):
            tables[2 * q + part] = pairs[q][part]
    for s in range(slices):
        expo[s] = jnp.exp(-coupling * phonon[s])
        inner[s] = apply_pairs(expo[s] * guess[s], (0, 1, 2), pairs, *parity)


class Band:
    def __init__(self, bonds, edges, expo, tables, slices):
        _, rows, cols = bonds.shape
        self.rows, self.slices = rows, slices
        self.main, self.strip, self.all = (parities((n, cols)) for n in (rows, HALO, rows + HALO))
        across, down = edges[2 * slices], edges[2 * slices + 1]
        self.pairs = [(tables[2 * q], tables[2 * q + 1]) for q in range(3)]
        self.strip_pairs = [pair_table((across, down), q, *self.strip) for q in range(3)]
        vertical = wide(bonds[1].astype(jnp.float32), down)
        self.wide_pairs = {3: pair_table((None, vertical), 3, *self.all)}
        self.expo = [expo[s] for s in range(slices)]
        self.strip_expo = [jnp.exp(-coupling * edges[slices + s]) for s in range(slices)]

    def inner(self, s, field):
        return apply_pairs(self.expo[s] * field, (0, 1, 2), self.pairs, *self.main)

    def propagated(self, s, inner, strip):
        strip = apply_pairs(self.strip_expo[s] * strip, (0, 1, 2), self.strip_pairs, *self.strip)
        return apply_pairs(wide(inner, strip), (3,), self.wide_pairs, *self.all)

    def pulled(self, field):
        field = apply_pairs(field, (3,), self.wide_pairs, *self.all)[: self.rows]
        return apply_pairs(field, (2, 1, 0), self.pairs, *self.main)


def residual_kernel(source, guess, bonds, edges, after, after_edge, expo, tables, inner, basis, out):
    slices, rows, cols = guess.shape
    band = Band(bonds, edges, expo, tables, slices)
    field = [wide(guess[s], edges[s]) for s in range(slices)]
    field.append(last_sign() * wide(after[0], after_edge[0]))
    pieces = []
    link = field[0]
    for s in range(slices):
        applied = band.propagated(s, inner[s], edges[s])
        following = field[s + 1] - applied
        pieces.append(source[s] - link[:rows] + band.expo[s] * band.pulled(following))
        link = following
    pieces.append(applied[:rows])
    stacked = jnp.concatenate(pieces, 0)
    out[...] = product(basis, halves(stacked), ROWS_BY_ROWS)


def mode_kernel(count, mixed, times, times_back, rows_in, rims, out):
    tm, band, modes, width = mixed.shape
    size = tm * modes
    freqs = times.shape[1] // modes
    length = rows_in.shape[1]
    per = length // band
    slots = width // per
    chunk = slots * modes + 1

    stacked = jnp.concatenate(
        [
            jnp.concatenate(
                [mixed[:, b, :, s * per : (s + 1) * per].reshape(size, per) for b in range(band)], 1
            )
            for s in range(slots)
        ],
        0,
    )
    waves = product(halves(product(times, halves(stacked))), rows_in)

    place = lax.axis_index("tm") * band + lax.axis_index("band")
    shape = (modes, length)
    column = place * modes + lax.broadcasted_iota(jnp.int32, shape, 0)
    row = lax.broadcasted_iota(jnp.int32, shape, 1)
    sine_c = jnp.sin(((column + 1) // 2).astype(jnp.float32) * (math.pi / count))
    sine_r = jnp.sin(((row + 1) // 2).astype(jnp.float32) * (math.pi / length))
    depth = sine_c * sine_c + sine_r * sine_r
    top = cheb_t(ORDER, 1.0 - depth * (4.0 / half_width))
    gains = []
    for k in range(freqs):
        if k % 2 == 0:
            lift = cheb_slope * (1.0 - math.cos((k + 1) * math.pi / freqs))
            damp = 1.0 / math.cosh(ORDER * math.acosh((cheb_base + lift) / half_width))
            gain = (1.0 - damp * top) / (4.0 * depth + (cheb_base - 4.0 + lift))
        gains.append(gain)
    waves = halves(waves * jnp.concatenate(gains, 0))

    back = product(times_back, halves(product(waves, rows_in, ROWS_BY_ROWS)))
    edge = product(halves(product(halves(rims[...]), waves, ROWS_BY_ROWS)), times)
    turns = [
        pltpu.roll(edge[:, s * size : (s + 1) * size], RIM * s * modes, 1, stride=modes, stride_axis=0)
        for s in range(slots)
    ]
    group = lax.broadcasted_iota(jnp.int32, (tm, size), 1) // modes
    slot = group - lax.broadcasted_iota(jnp.int32, (tm, size), 0)
    slot = jnp.where(slot < 0, slot + tm, slot)
    for b in range(band):
        rim = jnp.zeros((tm, size), jnp.float32)
        for s in range(slots):
            for q in range(RIM):
                line = turns[s][b * RIM + q : b * RIM + q + 1]
                rim = jnp.where(slot == (RIM * (s + b) + q) % tm, line, rim)
        for p in range(tm):
            at = (p * band + b) * chunk
            for s in range(slots):
                start = s * size + p * modes
                out[at + s * modes : at + (s + 1) * modes] = back[start : start + modes, b * per : (b + 1) * per]
            out[at + slots * modes : at + chunk] = rim[p : p + 1]


def force_kernel(base, guess, bonds, edges, after, after_edge, expo, tables, mixed, basis, sol, mom, turned_edge):
    slices, rows, cols = guess.shape
    devices = lax.axis_size("tm") * lax.axis_size("band")
    modes = cols // devices
    slots = slices + 1
    chunk = slots * modes + 1
    band = Band(bonds, edges, expo, tables, slices)
    columns = (basis[0], basis[1])

    arrived = [
        jnp.concatenate([mixed[d * chunk + s * modes : d * chunk + (s + 1) * modes] for d in range(devices)], 0)
        for s in range(slots)
    ]
    timed = product(halves(jnp.concatenate(arrived, 1).T), columns)

    rim = mixed[pl.ds(slots * modes, devices, stride=chunk), :]
    lanes = rim.shape[1]
    by = modes * (lax.axis_index("tm") + RIM * lax.axis_index("band"))
    rim = pltpu.roll(rim, lax.rem(2 * lanes - by, lanes), 1)
    turned_edge[...] = rim.T
    groups = lanes // modes
    lines = jnp.concatenate([turned_edge[pl.ds(m, groups, stride=modes), :] for m in range(modes)], 1)
    order = jnp.concatenate(
        [jnp.concatenate([part.reshape(devices, modes, cols)[:, m] for m in range(modes)], 0)[None] for part in columns], 0
    )
    strips = product(halves(lines), order)

    start = [wide(guess[s], edges[s]) for s in range(slices)]
    start.append(last_sign() * wide(after[0], after_edge[0]))
    field = []
    for s in range(slots):
        strip = turned(strips[s * RIM : s * RIM + HALO], -NEAR, 0)
        field.append(start[s] + relaxation * wide(timed[s * rows : (s + 1) * rows], strip))
    for s in range(slices):
        own = field[s][:rows]
        image = field[s + 1] - band.propagated(s, band.inner(s, own), field[s][rows:])
        sol[s] = own
        fermion = -2.0 * coupling * band.expo[s] * own * band.pulled(image)
        mom[s] = base[s] - step_size * fermion


def call(kernel, outs, *operands, flops=0, **kwargs):
    vmem = pl.BlockSpec(memory_space=pltpu.VMEM)
    return pl.pallas_call(
        kernel,
        out_shape=outs,
        in_specs=[vmem] * len(operands),
        out_specs=jax.tree.map(lambda _: vmem, outs),
        cost_estimate=pl.CostEstimate(flops=flops, bytes_accessed=4 << 20, transcendentals=0),
        **kwargs,
    )(*map(onchip, operands))


def onchip(value):
    return pltpu.with_memory_space_constraint(value, pltpu.VMEM)


def pack_kernel(guess, *refs):
    tops, ends, outs = refs[:3], refs[3:6], refs[6:]
    first, rims, rim = outs
    first[...] = guess[...]
    early = lax.broadcasted_iota(jnp.int32, tops[0].shape, 1) < EDGE
    at = 0
    for top, end in zip(tops, ends):
        both = jnp.where(early, top[...], end[...]).astype(jnp.float32)
        rims[at : at + top.shape[0]] = both
        if at == 0:
            rim[...] = both[:1]
        at += top.shape[0]


def pack(phonon, guess, bonds):
    slices, rows, cols = guess.shape
    fields = (guess, phonon, bonds)
    last = rows // HALO - 1
    whole = lambda shape: pl.BlockSpec(shape, lambda i: (0, 0, 0))
    tops = [whole((v.shape[0], HALO, cols)) for v in fields]
    ends = [pl.BlockSpec((v.shape[0], HALO, cols), lambda i: (0, last, 0)) for v in fields]
    outs = [(1, rows, cols), (2 * slices + 2, HALO, cols), (1, HALO, cols)]
    return pl.pallas_call(
        pack_kernel,
        grid=(1,),
        out_shape=[pltpu.VMEM(o, jnp.float32) for o in outs],
        in_specs=[whole((1, rows, cols))] + tops + ends,
        out_specs=[whole(o) for o in outs],
    )(guess, *fields, *fields)


def shards(phonon, momentum, source, guess, bonds):
    slices, rows, cols = guess.shape
    tm, band = lax.axis_size("tm"), lax.axis_size("band")
    total, length, devices = tm * slices, rows * band, tm * band
    modes = cols // devices
    slots = slices + 1

    slot_times = np.concatenate([time_basis(total, slices * np.arange(tm) + s) for s in range(slots)], 1)
    times = np.kron(slot_times, np.eye(modes))
    near = np.concatenate([np.arange(-NEAR, 0), rows + np.arange(NEAR)])
    rim_sites = np.concatenate([(b * rows + near) % length for b in range(band)])
    rims_basis = np.asarray(space_basis(length, rim_sites).T, np.float32)
    rows_in = const_halves(space_basis(length, np.arange(length)).T)
    columns = const_halves(space_basis(cols, np.arange(cols)))

    first, rims, rim = pack(phonon, guess, bonds)
    edges = band_halo(rims, 0)
    after = shifted(first, 1, 0)
    after_edge = band_halo(rim, 1)

    on = lambda *shape: pltpu.VMEM(shape, jnp.float32)
    expo, tables, inner = call(
        local_kernel, (on(slices, rows, cols), on(6, rows, cols), on(slices, rows, cols)),
        phonon, guess, bonds,
    )
    sent = call(
        residual_kernel, jax.ShapeDtypeStruct((cols, slots * rows), jnp.float32),
        source, guess, bonds, edges, after, after_edge, expo, tables, inner, columns,
    )
    mixed = lax.all_to_all(sent.reshape(devices, modes, slots * rows), AXES, 0, 0, tiled=True)
    wave_rows = devices * (slots * modes + 1)
    back = call(
        functools.partial(mode_kernel, cols), jax.ShapeDtypeStruct((wave_rows, rows), jnp.float32),
        mixed.reshape(tm, band, modes, slots * rows),
        const_halves(times), const_halves(np.ascontiguousarray(times.T)), rows_in, rims_basis,
    )
    mixed = lax.all_to_all(back.reshape(devices, 1, -1), AXES, 0, 0, tiled=True)

    after_ph = shifted(phonon[:1], 1, 0)
    before_ph = shifted(phonon[-1:], -1, 0)
    ring = jnp.concatenate([before_ph, phonon, after_ph], 0)
    boson = stiffness * (2.0 * phonon - ring[:-2] - ring[2:]) + mass_term * phonon
    base = momentum - step_size * boson
    like = jax.ShapeDtypeStruct(guess.shape, jnp.float32)
    return call(
        force_kernel, (like, like),
        base, guess, bonds, edges, after, after_edge, expo, tables,
        mixed.reshape(wave_rows, rows), columns,
        scratch_shapes=[pltpu.VMEM((cols // band, devices), jnp.float32)],
    )


def solution(mesh):
    spec = P("tm", "band", None)
    return jax.shard_map(
        shards,
        mesh=mesh,
        in_specs=(spec, spec, spec, spec, P(None, "band", None)),
        out_specs=(spec, spec),
        check_vma=False,
    )
```

time: 58.7 us -> 57.5 us (0.980)
  local copies, waits for them, and re-layouts: 1.06 us -> 5.6 us
  waiting for transfers between devices: 16.3 us -> 13.1 us
  blocking collectives: 19.4 us -> 18 us
  Pallas kernels: 9.33 us -> 8.05 us
    unnamed x20 -> x32, local copies, waits for them, and re-layouts: 1.04 us -> 5.58 us
    ppermute x5, waiting for transfers between devices: 8.08 us -> 6.46 us  [shifted(): return lax.ppermute(value, AXES, pairs)]
    all_to_all x1, waiting for transfers between devices: 8.24 us -> 6.66 us  [shards(): mixed = lax.all_to_all(back.reshape(devices, 1, -1), AXES, 0, 0, tiled=True)]
    all_to_all x1, blocking collectives: 19.4 us -> 18 us  [shards(): lax.all_to_all(sent.reshape(devices, modes, slots * rows), AXES, 0, 0, ti...]
    pallas_call x3 -> x4, Pallas kernels: 8.25 us -> 6.99 us  [call(): pl.pallas_call(kernel, out_shape=outs, in_specs=[vmem] * len(operands), o...]
  transfers between devices with their start and end apart: 6 -> 6, of which waited for: 4 -> 3; matrix products, arithmetic and copies ran while one was open for 0% -> 0% of each run, Pallas kernels for 0% -> 1%
where the time goes in v3:
time: 57.5 us; the launch traced here: 57.1 us
  blocking collectives  18 us (31%)
  waiting for transfers between devices  13.1 us (23%)
  starting transfers between devices  11.5 us (20%)
  Pallas kernels  8.05 us (14%)
  local copies, waits for them, and re-layouts  5.6 us (10%)
  between operations  0.75 us (1%)
    all_to_all x1, blocking collectives, shards(): lax.all_to_all(sent.reshape(devices, modes, slots * rows), AXES, 0, 0, ti...  18 us
    ppermute x5, starting transfers between devices, shifted(): return lax.ppermute(value, AXES, pairs)  8.86 us
    pallas_call x4, Pallas kernels, call(): pl.pallas_call(kernel, out_shape=outs, in_specs=[vmem] * len(operands), o...  6.99 us
    all_to_all x1, waiting for transfers between devices, shards(): mixed = lax.all_to_all(back.reshape(devices, 1, -1), AXES, 0, 0, tiled=True)  6.66 us
    ppermute x5, waiting for transfers between devices, shifted(): return lax.ppermute(value, AXES, pairs)  6.46 us
    unnamed x32, local copies, waits for them, and re-layouts  5.58 us
    all_to_all x1, starting transfers between devices, shards(): mixed = lax.all_to_all(back.reshape(devices, 1, -1), AXES, 0, 0, tiled=True)  2.61 us
  transfers between devices with their start and end apart: 6, of which 3 were waited for; matrix products, arithmetic and copies ran while one was open for 0% of the time, Pallas kernels for 1%

profile of v3, /device:TPU:1, one launch (start us, length us, event | category | flops | bytes accessed | tf_op | source)
XLA Modules:
  0.0 57.1 jit_solution(1226487343421912768)
XLA Ops:
  0.6 0.0 copy-start.2
  0.6 0.0 copy-start
  0.6 0.0 copy-start.1
  0.7 1.1 %shard_map.113 = (f32[1,128,256]{2,1,0:T(8,128)S(1)}, f32[6,8,256]{2,1,0:T(8,128)S(1)}, f32[1,8,256]{2,1,0:T(8,128)S(1)}) custom-call(f32[2,128,256]{2,1,0:T(8,128)} %guess.7, f32[2,128,256]{2,1,0:T(8,128)} %guess.7, f32[2,128,256]{2,1,0:T(8,128)} %phonon.1, s32[2,128,256]{2,1,0:T(8,128)} %bonds.5, f32[2,128,256]{2,1,0:T(8,128)} %guess.7, ...), custom_call_target="tpu_custom_call" | custom-call | tf_op jit(solution)/shard_map/pallas_call | solution.py:327
  1.7 0.1 collective-permute-start.3
  1.8 2.7 %collective-permute-start.2 = (f32[6,8,256]{2,1,0:T(8,128)S(1)}, f32[6,8,256]{2,1,0:T(8,128)S(1)}, u32[]{:S(2)}, u32[]{:S(2)}) collective-permute-start(f32[6,8,256]{2,1,0:T(8,128)S(1)} %get-tuple-element.8), channel_id=1, source_target_pairs={{1,0},{0,1},{3,2},{2,3},{5,4},{4,5},{7,6},{6,7},{9,8},{8,9},{11,10... | collective-permute-start | bytes 147464 | tf_op jit(solution)/shard_map/ppermute | solution.py:41
  4.5 0.0 copy-start.6
  4.5 4.4 %collective-permute-start.4 = (f32[1,8,256]{2,1,0:T(8,128)S(1)}, f32[1,8,256]{2,1,0:T(8,128)S(1)}, u32[]{:S(2)}, u32[]{:S(2)}) collective-permute-start(f32[1,8,256]{2,1,0:T(8,128)S(1)} %get-tuple-element.10), channel_id=1, source_target_pairs={{3,0},{2,1},{5,2},{4,3},{7,4},{6,5},{9,6},{8,7},{11,8},{10,9},{13,... | collective-permute-start | bytes 24584 | tf_op jit(solution)/shard_map/ppermute | solution.py:41
  8.9 0.0 copy-done.2
  8.9 0.0 copy-done
  8.9 0.0 copy-done.1
  8.9 0.6 shard_map.114
  9.5 0.0 copy-start.3
  9.5 0.9 %copy-done.3 = f32[6,128,256]{2,1,0:T(8,128)} copy-done((f32[6,128,256]{2,1,0:T(8,128)}, f32[6,128,256]{2,1,0:T(8,128)S(1)}, u32[]{:S(2)}) %copy-start.3) | copy-done | bytes 786456
  10.4 0.0 copy-start.7
  10.4 0.7 %copy-done.7 = f32[2,128,256]{2,1,0:T(8,128)} copy-done((f32[2,128,256]{2,1,0:T(8,128)}, f32[2,128,256]{2,1,0:T(8,128)S(1)}, u32[]{:S(2)}) %copy-start.7) | copy-done | bytes 262168
  11.1 0.0 collective-permute-done.4.after_edge
  11.1 0.0 collective-permute-done.2.edges
  11.1 0.0 collective-permute-done.3.after
  11.1 0.0 copy-done.6
  11.1 0.0 copy-start.4
  11.1 1.1 %copy-done.4 = f32[6,128,256]{2,1,0:T(8,128)S(1)} copy-done((f32[6,128,256]{2,1,0:T(8,128)S(1)}, f32[6,128,256]{2,1,0:T(8,128)}, u32[]{:S(2)}) %copy-start.4) | copy-done | bytes 786456
  12.2 0.0 copy-start.8
  12.2 0.9 %copy-done.8 = f32[2,128,256]{2,1,0:T(8,128)S(1)} copy-done((f32[2,128,256]{2,1,0:T(8,128)S(1)}, f32[2,128,256]{2,1,0:T(8,128)}, u32[]{:S(2)}) %copy-start.8) | copy-done | bytes 262168
  13.2 0.0 copy-start.12
  13.2 0.9 %copy-done.12 = f32[2,128,256]{2,1,0:T(8,128)S(1)} copy-done((f32[2,128,256]{2,1,0:T(8,128)S(1)}, f32[2,128,256]{2,1,0:T(8,128)}, u32[]{:S(2)}) %copy-start.12) | copy-done | bytes 262168
  14.1 0.0 copy-start.14
  14.1 1.8 %shard_map.115 = f32[256,384]{1,0:T(8,128)} custom-call(f32[2,128,256]{2,1,0:T(8,128)S(1)} %copy-done.12, f32[2,128,256]{2,1,0:T(8,128)S(1)} %copy-done, s32[2,128,256]{2,1,0:T(8,128)S(1)} %copy-done.2, f32[6,8,256]{2,1,0:T(8,128)S(1)} %collective-permute-done.2.edges, f32[1,128,256]{2,1,0:T(8,128)S(1)} %collective-permute-done.3.after, ...), custom_call_target="tpu_custom_call" | custom-call | bytes 4194304 | tf_op jit(solution)/shard_map/pallas_call | solution.py:291
  15.9 0.0 copy-start.10
  15.9 18.0 %all_to_all.10 = f32[32,8,384]{2,1,0:T(8,128)S(1)} all-to-all(f32[32,8,384]{2,1,0:T(8,128)} %bitcast.7), channel_id=1, replica_groups=mesh['tm'=16,'band'=2] {'tm','band'}, dimensions={0} | all-to-all | bytes 786432 | tf_op jit(solution)/shard_map/all_to_all | solution.py:365
  33.9 0.0 copy-done.14
  33.9 0.0 copy-done.10
  33.9 0.0 copy-done.11
  33.9 0.0 copy-start.13
  33.9 0.9 %copy-done.13 = bf16[2,256,256]{2,1,0:T(8,128)(2,1)S(1)} copy-done((bf16[2,256,256]{2,1,0:T(8,128)(2,1)S(1)}, bf16[2,256,256]{2,1,0:T(8,128)(2,1)}, u32[]{:S(2)}) %copy-start.13) | copy-done | bytes 262168
  34.9 2.3 %shard_map.116 = f32[800,128]{1,0:T(8,128)} custom-call(f32[16,2,8,384]{3,2,1,0:T(8,128)S(1)} %bitcast.5, bf16[2,256,384]{2,1,0:T(8,128)(2,1)S(1)} %copy-done.11, bf16[2,384,256]{2,1,0:T(8,128)(2,1)S(1)} %copy-done.10, bf16[2,256,256]{2,1,0:T(8,128)(2,1)S(1)} %copy-done.13, f32[8,256]{1,0:T(8,128)S(1)} %copy-done.14), custom_call_target="tpu_custom_call" | custom-call | bytes 4194304 | tf_op jit(solution)/shard_map/pallas_call | solution.py:291
  37.2 2.6 %all-to-all-start.1 = ((f32[32,1,3200]{2,1,0:T(1,128)}), f32[32,1,3200]{2,1,0:T(1,128)S(1)}, u32[]{:S(2)}, u32[]{:S(2)}) async-start(f32[32,1,3200]{2,1,0:T(1,128)} %bitcast.6), calls=%async_computation.1 | async-start | bytes 819200 | tf_op jit(solution)/shard_map/all_to_all | solution.py:372
  39.8 0.0 copy-start.5
  39.8 1.7 %collective-permute-start = (f32[1,128,256]{2,1,0:T(8,128)S(1)}, f32[1,128,256]{2,1,0:T(8,128)S(1)}, u32[]{:S(2)}, u32[]{:S(2)}) collective-permute-start(f32[1,128,256]{2,1,0:T(8,128)S(1)} %get-tuple-element.14), channel_id=1, source_target_pairs={{30,0},{31,1},{0,2},{1,3},{2,4},{3,5},{4,6},{5,7},{6,8},{7,9},{8,1... | collective-permute-start | bytes 393224 | tf_op jit(solution)/shard_map/ppermute | solution.py:41
  41.5 0.0 collective-permute-start.1
  41.5 6.3 %collective-permute-done = f32[1,128,256]{2,1,0:T(8,128)S(1)} collective-permute-done((f32[1,128,256]{2,1,0:T(8,128)S(1)}, f32[1,128,256]{2,1,0:T(8,128)S(1)}, u32[]{:S(2)}, u32[]{:S(2)}) %collective-permute-start) | collective-permute-done | bytes 131104 | tf_op jit(solution)/shard_map/ppermute | solution.py:41
  47.8 0.1 collective-permute-done.1
  48.0 0.0 copy-done.15
  48.0 0.1 fusion.3.base
  48.0 6.7 %all-to-all-done.1 = f32[32,1,3200]{2,1,0:T(1,128)S(1)} async-done(((f32[32,1,3200]{2,1,0:T(1,128)}), f32[32,1,3200]{2,1,0:T(1,128)S(1)}, u32[]{:S(2)}, u32[]{:S(2)}) %all-to-all-start.1) | async-done | bytes 409632 | tf_op jit(solution)/shard_map/all_to_all | solution.py:372
  54.7 0.0 copy-done.5
  54.7 0.0 copy-done.9
  54.7 2.4 %shard_map.117 = (f32[2,128,256]{2,1,0:T(8,128)}, f32[2,128,256]{2,1,0:T(8,128)}) custom-call(f32[2,128,256]{2,1,0:T(8,128)S(1)} %fusion.3.base, f32[2,128,256]{2,1,0:T(8,128)S(1)} %copy-done, s32[2,128,256]{2,1,0:T(8,128)S(1)} %copy-done.2, f32[6,8,256]{2,1,0:T(8,128)S(1)} %collective-permute-done.2.edges, f32[1,128,256]{2,1,0:T(8,128)S(1)} %collective-permute-done.3.after, ...), custom_call_target="tpu_custom_call" | custom-call | bytes 4194304 | tf_op jit(solution)/shard_map/pallas_call | solution.py:291
  (4 shorter events, 0.0 us)
Async XLA Ops:
  0.6 8.3 %copy-start.2 = (s32[2,128,256]{2,1,0:T(8,128)S(1)}, s32[2,128,256]{2,1,0:T(8,128)}, u32[]{:S(2)}) copy-start(s32[2,128,256]{2,1,0:T(8,128)} %bonds.5) | copy-start | bytes 786436
  0.6 8.3 %copy-start = (f32[2,128,256]{2,1,0:T(8,128)S(1)}, f32[2,128,256]{2,1,0:T(8,128)}, u32[]{:S(2)}) copy-start(f32[2,128,256]{2,1,0:T(8,128)} %guess.7) | copy-start | bytes 786436
  0.6 8.3 %copy-start.1 = (f32[2,128,256]{2,1,0:T(8,128)S(1)}, f32[2,128,256]{2,1,0:T(8,128)}, u32[]{:S(2)}) copy-start(f32[2,128,256]{2,1,0:T(8,128)} %phonon.1) | copy-start | bytes 786436
  1.7 9.4 %collective-permute-start.3 = (f32[1,128,256]{2,1,0:T(8,128)S(1)}, f32[1,128,256]{2,1,0:T(8,128)S(1)}, u32[]{:S(2)}, u32[]{:S(2)}) collective-permute-start(f32[1,128,256]{2,1,0:T(8,128)S(1)} %get-tuple-element.9), channel_id=1, source_target_pairs={{2,0},{3,1},{4,2},{5,3},{6,4},{7,5},{8,6},{9,7},{10,8},{11,9},{12,... | collective-permute-start | bytes 393224 | tf_op jit(solution)/shard_map/ppermute | solution.py:41
  1.8 9.3 %collective-permute-start.2 = (f32[6,8,256]{2,1,0:T(8,128)S(1)}, f32[6,8,256]{2,1,0:T(8,128)S(1)}, u32[]{:S(2)}, u32[]{:S(2)}) collective-permute-start(f32[6,8,256]{2,1,0:T(8,128)S(1)} %get-tuple-element.8), channel_id=1, source_target_pairs={{1,0},{0,1},{3,2},{2,3},{5,4},{4,5},{7,6},{6,7},{9,8},{8,9},{11,10... | collective-permute-start | bytes 147464 | tf_op jit(solution)/shard_map/ppermute | solution.py:41
  4.5 6.6 %copy-start.6 = (bf16[2,256,256]{2,1,0:T(8,128)(2,1)S(1)}, bf16[2,256,256]{2,1,0:T(8,128)(2,1)}, u32[]{:S(2)}) copy-start(bf16[2,256,256]{2,1,0:T(8,128)(2,1)} %constant.16.clone.basis) | copy-start | bytes 786436
  4.5 6.6 %collective-permute-start.4 = (f32[1,8,256]{2,1,0:T(8,128)S(1)}, f32[1,8,256]{2,1,0:T(8,128)S(1)}, u32[]{:S(2)}, u32[]{:S(2)}) collective-permute-start(f32[1,8,256]{2,1,0:T(8,128)S(1)} %get-tuple-element.10), channel_id=1, source_target_pairs={{3,0},{2,1},{5,2},{4,3},{7,4},{6,5},{9,6},{8,7},{11,8},{10,9},{13,... | collective-permute-start | bytes 24584 | tf_op jit(solution)/shard_map/ppermute | solution.py:41
  9.5 0.9 %copy-start.3 = (f32[6,128,256]{2,1,0:T(8,128)}, f32[6,128,256]{2,1,0:T(8,128)S(1)}, u32[]{:S(2)}) copy-start(f32[6,128,256]{2,1,0:T(8,128)S(1)} %get-tuple-element.12.tables) | copy-start | bytes 2359300
  10.4 0.7 %copy-start.7 = (f32[2,128,256]{2,1,0:T(8,128)}, f32[2,128,256]{2,1,0:T(8,128)S(1)}, u32[]{:S(2)}) copy-start(f32[2,128,256]{2,1,0:T(8,128)S(1)} %get-tuple-element.11.expo) | copy-start | bytes 786436
  11.1 1.1 %copy-start.4 = (f32[6,128,256]{2,1,0:T(8,128)S(1)}, f32[6,128,256]{2,1,0:T(8,128)}, u32[]{:S(2)}) copy-start(f32[6,128,256]{2,1,0:T(8,128)} %copy-done.3) | copy-start | bytes 2359300
  12.2 0.9 %copy-start.8 = (f32[2,128,256]{2,1,0:T(8,128)S(1)}, f32[2,128,256]{2,1,0:T(8,128)}, u32[]{:S(2)}) copy-start(f32[2,128,256]{2,1,0:T(8,128)} %copy-done.7) | copy-start | bytes 786436
  13.2 0.9 %copy-start.12 = (f32[2,128,256]{2,1,0:T(8,128)S(1)}, f32[2,128,256]{2,1,0:T(8,128)}, u32[]{:S(2)}) copy-start(f32[2,128,256]{2,1,0:T(8,128)} %source.1) | copy-start | bytes 786436
  14.1 19.8 %copy-start.14 = (f32[8,256]{1,0:T(8,128)S(1)}, f32[8,256]{1,0:T(8,128)}, u32[]{:S(2)}) copy-start(f32[8,256]{1,0:T(8,128)} %constant.20.clone.rims) | copy-start | bytes 24580
  15.9 18.0 %copy-start.10 = (bf16[2,384,256]{2,1,0:T(8,128)(2,1)S(1)}, bf16[2,384,256]{2,1,0:T(8,128)(2,1)}, u32[]{:S(2)}) copy-start(bf16[2,384,256]{2,1,0:T(8,128)(2,1)} %constant.18.clone.times_back) | copy-start | bytes 1179652
  15.9 18.0 %copy-start.11 = (bf16[2,256,384]{2,1,0:T(8,128)(2,1)S(1)}, bf16[2,256,384]{2,1,0:T(8,128)(2,1)}, u32[]{:S(2)}) copy-start(bf16[2,256,384]{2,1,0:T(8,128)(2,1)} %constant.17.clone.times) | copy-start | bytes 1179652
  33.9 1.0 %copy-start.13 = (bf16[2,256,256]{2,1,0:T(8,128)(2,1)S(1)}, bf16[2,256,256]{2,1,0:T(8,128)(2,1)}, u32[]{:S(2)}) copy-start(bf16[2,256,256]{2,1,0:T(8,128)(2,1)} %constant.19.clone.rows_in) | copy-start | bytes 786436
  37.2 10.8 %copy-start.15 = (f32[2,128,256]{2,1,0:T(8,128)S(1)}, f32[2,128,256]{2,1,0:T(8,128)}, u32[]{:S(2)}) copy-start(f32[2,128,256]{2,1,0:T(8,128)} %param.11) | copy-start | bytes 786436
  37.2 17.5 %all-to-all-start.1 = ((f32[32,1,3200]{2,1,0:T(1,128)}), f32[32,1,3200]{2,1,0:T(1,128)S(1)}, u32[]{:S(2)}, u32[]{:S(2)}) async-start(f32[32,1,3200]{2,1,0:T(1,128)} %bitcast.6), calls=%async_computation.1 | async-start | bytes 819200 | tf_op jit(solution)/shard_map/all_to_all | solution.py:372
  39.8 14.9 %copy-start.5 = (f32[6,128,256]{2,1,0:T(8,128)S(1)}, f32[6,128,256]{2,1,0:T(8,128)}, u32[]{:S(2)}) copy-start(f32[6,128,256]{2,1,0:T(8,128)} %copy-done.3) | copy-start | bytes 2359300
  39.8 8.0 %collective-permute-start = (f32[1,128,256]{2,1,0:T(8,128)S(1)}, f32[1,128,256]{2,1,0:T(8,128)S(1)}, u32[]{:S(2)}, u32[]{:S(2)}) collective-permute-start(f32[1,128,256]{2,1,0:T(8,128)S(1)} %get-tuple-element.14), channel_id=1, source_target_pairs={{30,0},{31,1},{0,2},{1,3},{2,4},{3,5},{4,6},{5,7},{6,8},{7,9},{8,1... | collective-permute-start | bytes 393224 | tf_op jit(solution)/shard_map/ppermute | solution.py:41
  41.5 13.2 %copy-start.9 = (f32[2,128,256]{2,1,0:T(8,128)S(1)}, f32[2,128,256]{2,1,0:T(8,128)}, u32[]{:S(2)}) copy-start(f32[2,128,256]{2,1,0:T(8,128)} %copy-done.7) | copy-start | bytes 786436
  41.5 6.5 %collective-permute-start.1 = (f32[1,128,256]{2,1,0:T(8,128)S(1)}, f32[1,128,256]{2,1,0:T(8,128)S(1)}, u32[]{:S(2)}, u32[]{:S(2)}) collective-permute-start(f32[1,128,256]{2,1,0:T(8,128)S(1)} %get-tuple-element.15), channel_id=1, source_target_pairs={{2,0},{3,1},{4,2},{5,3},{6,4},{7,5},{8,6},{9,7},{10,8},{11,9},{12,... | collective-permute-start | bytes 393224 | tf_op jit(solution)/shard_map/ppermute | solution.py:41

commit v4 on v3

--- a/solution.py
+++ b/solution.py
@@ -293,6 +293,7 @@
         out_shape=outs,
         in_specs=[vmem] * len(operands),
         out_specs=jax.tree.map(lambda _: vmem, outs),
+        compiler_params=pltpu.CompilerParams(vmem_limit_bytes=12 << 20),
         cost_estimate=pl.CostEstimate(flops=flops, bytes_accessed=4 << 20, transcendentals=0),
         **kwargs,
     )(*map(onchip, operands))

time: 57.5 us -> 52.5 us (0.913)
  local copies, waits for them, and re-layouts: 5.6 us -> 0.07 us
  blocking collectives: 18 us -> 19.2 us
  Pallas kernels: 8.05 us -> 7.29 us
    unnamed x32 -> x20, local copies, waits for them, and re-layouts: 5.58 us -> 0.05 us
    all_to_all x1, blocking collectives: 18 us -> 19.2 us  [shards(): lax.all_to_all(sent.reshape(devices, modes, slots * rows), AXES, 0, 0, ti...]
    pallas_call x4, Pallas kernels: 6.99 us -> 6.23 us  [call(): pl.pallas_call(kernel, out_shape=outs, in_specs=[vmem] * len(operands), o...]
  transfers between devices with their start and end apart: 6 -> 6, of which waited for: 3 -> 4; matrix products, arithmetic and copies ran while one was open for 0% -> 0% of each run, Pallas kernels for 1% -> 1%
where the time goes in v4:
time: 52.5 us; the launch traced here: 52.2 us
  blocking collectives  19.2 us (37%)
  waiting for transfers between devices  13.3 us (25%)
  starting transfers between devices  11.5 us (22%)
  Pallas kernels  7.29 us (14%)
  between operations  0.76 us (1%)
    all_to_all x1, blocking collectives, shards(): lax.all_to_all(sent.reshape(devices, modes, slots * rows), AXES, 0, 0, ti...  19.2 us
    ppermute x5, starting transfers between devices, shifted(): return lax.ppermute(value, AXES, pairs)  8.86 us
    ppermute x5, waiting for transfers between devices, shifted(): return lax.ppermute(value, AXES, pairs)  6.66 us
    all_to_all x1, waiting for transfers between devices, shards(): mixed = lax.all_to_all(back.reshape(devices, 1, -1), AXES, 0, 0, tiled=True)  6.66 us
    pallas_call x4, Pallas kernels, call(): pl.pallas_call(kernel, out_shape=outs, in_specs=[vmem] * len(operands), o...  6.23 us
    all_to_all x1, starting transfers between devices, shards(): mixed = lax.all_to_all(back.reshape(devices, 1, -1), AXES, 0, 0, tiled=True)  2.61 us
    pallas_call x1, Pallas kernels, pack(): pl.pallas_call(pack_kernel, grid=(1,), out_shape=[pltpu.VMEM(o, jnp.float...  1.06 us
  transfers between devices with their start and end apart: 6, of which 4 were waited for; matrix products, arithmetic and copies ran while one was open for 0% of the time, Pallas kernels for 1%

profile of v4, /device:TPU:1, one launch (start us, length us, event | category | flops | bytes accessed | tf_op | source)
XLA Modules:
  0.0 52.2 jit_solution(9304255285094763658)
XLA Ops:
  0.6 0.0 copy-start.2
  0.6 0.0 copy-start
  0.6 0.0 copy-start.1
  0.7 1.1 %shard_map.113 = (f32[1,128,256]{2,1,0:T(8,128)S(1)}, f32[6,8,256]{2,1,0:T(8,128)S(1)}, f32[1,8,256]{2,1,0:T(8,128)S(1)}) custom-call(f32[2,128,256]{2,1,0:T(8,128)} %guess.7, f32[2,128,256]{2,1,0:T(8,128)} %guess.7, f32[2,128,256]{2,1,0:T(8,128)} %phonon.1, s32[2,128,256]{2,1,0:T(8,128)} %bonds.5, f32[2,128,256]{2,1,0:T(8,128)} %guess.7, ...), custom_call_target="tpu_custom_call" | custom-call | tf_op jit(solution)/shard_map/pallas_call | solution.py:328
  1.7 0.1 collective-permute-start.3
  1.8 2.7 %collective-permute-start.2 = (f32[6,8,256]{2,1,0:T(8,128)S(1)}, f32[6,8,256]{2,1,0:T(8,128)S(1)}, u32[]{:S(2)}, u32[]{:S(2)}) collective-permute-start(f32[6,8,256]{2,1,0:T(8,128)S(1)} %get-tuple-element.8), channel_id=1, source_target_pairs={{1,0},{0,1},{3,2},{2,3},{5,4},{4,5},{7,6},{6,7},{9,8},{8,9},{11,10... | collective-permute-start | bytes 147464 | tf_op jit(solution)/shard_map/ppermute | solution.py:41
  4.5 0.0 copy-start.3
  4.5 0.0 copy-start.6
  4.5 4.4 %collective-permute-start.4 = (f32[1,8,256]{2,1,0:T(8,128)S(1)}, f32[1,8,256]{2,1,0:T(8,128)S(1)}, u32[]{:S(2)}, u32[]{:S(2)}) collective-permute-start(f32[1,8,256]{2,1,0:T(8,128)S(1)} %get-tuple-element.10), channel_id=1, source_target_pairs={{3,0},{2,1},{5,2},{4,3},{7,4},{6,5},{9,6},{8,7},{11,8},{10,9},{13,... | collective-permute-start | bytes 24584 | tf_op jit(solution)/shard_map/ppermute | solution.py:41
  8.9 0.0 copy-done.2
  8.9 0.0 copy-done
  8.9 0.0 copy-done.1
  8.9 0.6 %shard_map.114 = (f32[2,128,256]{2,1,0:T(8,128)S(1)}, f32[6,128,256]{2,1,0:T(8,128)S(1)}, f32[2,128,256]{2,1,0:T(8,128)S(1)}) custom-call(f32[2,128,256]{2,1,0:T(8,128)S(1)} %copy-done.1, f32[2,128,256]{2,1,0:T(8,128)S(1)} %copy-done, s32[2,128,256]{2,1,0:T(8,128)S(1)} %copy-done.2), custom_call_target="tpu_custom_call" | custom-call | bytes 4194304 | tf_op jit(solution)/shard_map/pallas_call | solution.py:291
  9.5 0.2 collective-permute-done.4.after_edge
  9.7 0.0 collective-permute-done.2.edges
  9.7 0.0 collective-permute-done.3.after
  9.7 0.0 copy-done.3
  9.7 0.0 copy-done.6
  9.7 0.0 copy-start.7
  9.7 0.0 copy-start.8
  9.7 1.0 %shard_map.115 = f32[256,384]{1,0:T(8,128)S(1)} custom-call(f32[2,128,256]{2,1,0:T(8,128)S(1)} %copy-done.6, f32[2,128,256]{2,1,0:T(8,128)S(1)} %copy-done, s32[2,128,256]{2,1,0:T(8,128)S(1)} %copy-done.2, f32[6,8,256]{2,1,0:T(8,128)S(1)} %collective-permute-done.2.edges, f32[1,128,256]{2,1,0:T(8,128)S(1)} %collective-permute-done.3.after, ...), custom_call_target="tpu_custom_call" | custom-call | bytes 4194304 | tf_op jit(solution)/shard_map/pallas_call | solution.py:291
  10.7 0.0 copy-start.4
  10.7 0.0 copy-start.5
  10.8 19.2 %all_to_all.10 = f32[32,8,384]{2,1,0:T(8,128)S(1)} all-to-all(f32[32,8,384]{2,1,0:T(8,128)S(1)} %bitcast.6), channel_id=1, replica_groups=mesh['tm'=16,'band'=2] {'tm','band'}, dimensions={0} | all-to-all | bytes 786432 | tf_op jit(solution)/shard_map/all_to_all | solution.py:366
  30.0 0.0 copy-done.7
  30.0 0.0 copy-done.8
  30.0 0.0 copy-done.4
  30.0 0.0 copy-done.5
  30.0 2.3 %shard_map.116 = f32[800,128]{1,0:T(8,128)} custom-call(f32[16,2,8,384]{3,2,1,0:T(8,128)S(1)} %bitcast.5, bf16[2,256,384]{2,1,0:T(8,128)(2,1)S(1)} %copy-done.5, bf16[2,384,256]{2,1,0:T(8,128)(2,1)S(1)} %copy-done.4, bf16[2,256,256]{2,1,0:T(8,128)(2,1)S(1)} %copy-done.7, f32[8,256]{1,0:T(8,128)S(1)} %copy-done.8), custom_call_target="tpu_custom_call" | custom-call | bytes 4194304 | tf_op jit(solution)/shard_map/pallas_call | solution.py:291
  32.3 2.6 %all-to-all-start.1 = ((f32[32,1,3200]{2,1,0:T(1,128)}), f32[32,1,3200]{2,1,0:T(1,128)S(1)}, u32[]{:S(2)}, u32[]{:S(2)}) async-start(f32[32,1,3200]{2,1,0:T(1,128)} %bitcast.2), calls=%async_computation.1 | async-start | bytes 819200 | tf_op jit(solution)/shard_map/all_to_all | solution.py:373
  34.9 0.0 copy-start.9
  34.9 1.7 %collective-permute-start = (f32[1,128,256]{2,1,0:T(8,128)S(1)}, f32[1,128,256]{2,1,0:T(8,128)S(1)}, u32[]{:S(2)}, u32[]{:S(2)}) collective-permute-start(f32[1,128,256]{2,1,0:T(8,128)S(1)} %get-tuple-element.14), channel_id=1, source_target_pairs={{30,0},{31,1},{0,2},{1,3},{2,4},{3,5},{4,6},{5,7},{6,8},{7,9},{8,1... | collective-permute-start | bytes 393224 | tf_op jit(solution)/shard_map/ppermute | solution.py:41
  36.6 0.0 collective-permute-start.1
  36.6 6.3 %collective-permute-done = f32[1,128,256]{2,1,0:T(8,128)S(1)} collective-permute-done((f32[1,128,256]{2,1,0:T(8,128)S(1)}, f32[1,128,256]{2,1,0:T(8,128)S(1)}, u32[]{:S(2)}, u32[]{:S(2)}) %collective-permute-start) | collective-permute-done | bytes 131104 | tf_op jit(solution)/shard_map/ppermute | solution.py:41
  42.9 0.1 collective-permute-done.1
  43.1 0.0 copy-done.9
  43.1 0.1 fusion.3.base
  43.1 6.7 %all-to-all-done.1 = f32[32,1,3200]{2,1,0:T(1,128)S(1)} async-done(((f32[32,1,3200]{2,1,0:T(1,128)}), f32[32,1,3200]{2,1,0:T(1,128)S(1)}, u32[]{:S(2)}, u32[]{:S(2)}) %all-to-all-start.1) | async-done | bytes 409632 | tf_op jit(solution)/shard_map/all_to_all | solution.py:373
  49.8 2.4 %shard_map.117 = (f32[2,128,256]{2,1,0:T(8,128)}, f32[2,128,256]{2,1,0:T(8,128)}) custom-call(f32[2,128,256]{2,1,0:T(8,128)S(1)} %fusion.3.base, f32[2,128,256]{2,1,0:T(8,128)S(1)} %copy-done, s32[2,128,256]{2,1,0:T(8,128)S(1)} %copy-done.2, f32[6,8,256]{2,1,0:T(8,128)S(1)} %collective-permute-done.2.edges, f32[1,128,256]{2,1,0:T(8,128)S(1)} %collective-permute-done.3.after, ...), custom_call_target="tpu_custom_call" | custom-call | bytes 4194304 | tf_op jit(solution)/shard_map/pallas_call | solution.py:291
  (1 shorter events, 0.0 us)
Async XLA Ops:
  0.6 8.3 %copy-start.2 = (s32[2,128,256]{2,1,0:T(8,128)S(1)}, s32[2,128,256]{2,1,0:T(8,128)}, u32[]{:S(2)}) copy-start(s32[2,128,256]{2,1,0:T(8,128)} %bonds.5) | copy-start | bytes 786436
  0.6 8.3 %copy-start = (f32[2,128,256]{2,1,0:T(8,128)S(1)}, f32[2,128,256]{2,1,0:T(8,128)}, u32[]{:S(2)}) copy-start(f32[2,128,256]{2,1,0:T(8,128)} %guess.7) | copy-start | bytes 786436
  0.6 8.3 %copy-start.1 = (f32[2,128,256]{2,1,0:T(8,128)S(1)}, f32[2,128,256]{2,1,0:T(8,128)}, u32[]{:S(2)}) copy-start(f32[2,128,256]{2,1,0:T(8,128)} %phonon.1) | copy-start | bytes 786436
  1.7 8.0 %collective-permute-start.3 = (f32[1,128,256]{2,1,0:T(8,128)S(1)}, f32[1,128,256]{2,1,0:T(8,128)S(1)}, u32[]{:S(2)}, u32[]{:S(2)}) collective-permute-start(f32[1,128,256]{2,1,0:T(8,128)S(1)} %get-tuple-element.9), channel_id=1, source_target_pairs={{2,0},{3,1},{4,2},{5,3},{6,4},{7,5},{8,6},{9,7},{10,8},{11,9},{12,... | collective-permute-start | bytes 393224 | tf_op jit(solution)/shard_map/ppermute | solution.py:41
  1.8 7.9 %collective-permute-start.2 = (f32[6,8,256]{2,1,0:T(8,128)S(1)}, f32[6,8,256]{2,1,0:T(8,128)S(1)}, u32[]{:S(2)}, u32[]{:S(2)}) collective-permute-start(f32[6,8,256]{2,1,0:T(8,128)S(1)} %get-tuple-element.8), channel_id=1, source_target_pairs={{1,0},{0,1},{3,2},{2,3},{5,4},{4,5},{7,6},{6,7},{9,8},{8,9},{11,10... | collective-permute-start | bytes 147464 | tf_op jit(solution)/shard_map/ppermute | solution.py:41
  4.5 5.2 %copy-start.3 = (bf16[2,256,256]{2,1,0:T(8,128)(2,1)S(1)}, bf16[2,256,256]{2,1,0:T(8,128)(2,1)}, u32[]{:S(2)}) copy-start(bf16[2,256,256]{2,1,0:T(8,128)(2,1)} %constant.16.clone.basis) | copy-start | bytes 786436
  4.5 5.2 %copy-start.6 = (f32[2,128,256]{2,1,0:T(8,128)S(1)}, f32[2,128,256]{2,1,0:T(8,128)}, u32[]{:S(2)}) copy-start(f32[2,128,256]{2,1,0:T(8,128)} %source.1) | copy-start | bytes 786436
  4.5 5.2 %collective-permute-start.4 = (f32[1,8,256]{2,1,0:T(8,128)S(1)}, f32[1,8,256]{2,1,0:T(8,128)S(1)}, u32[]{:S(2)}, u32[]{:S(2)}) collective-permute-start(f32[1,8,256]{2,1,0:T(8,128)S(1)} %get-tuple-element.10), channel_id=1, source_target_pairs={{3,0},{2,1},{5,2},{4,3},{7,4},{6,5},{9,6},{8,7},{11,8},{10,9},{13,... | collective-permute-start | bytes 24584 | tf_op jit(solution)/shard_map/ppermute | solution.py:41
  9.7 20.3 %copy-start.7 = (bf16[2,256,256]{2,1,0:T(8,128)(2,1)S(1)}, bf16[2,256,256]{2,1,0:T(8,128)(2,1)}, u32[]{:S(2)}) copy-start(bf16[2,256,256]{2,1,0:T(8,128)(2,1)} %constant.19.clone.rows_in) | copy-start | bytes 786436
  9.7 20.2 %copy-start.8 = (f32[8,256]{1,0:T(8,128)S(1)}, f32[8,256]{1,0:T(8,128)}, u32[]{:S(2)}) copy-start(f32[8,256]{1,0:T(8,128)} %constant.20.clone.rims) | copy-start | bytes 24580
  10.7 19.3 %copy-start.4 = (bf16[2,384,256]{2,1,0:T(8,128)(2,1)S(1)}, bf16[2,384,256]{2,1,0:T(8,128)(2,1)}, u32[]{:S(2)}) copy-start(bf16[2,384,256]{2,1,0:T(8,128)(2,1)} %constant.18.clone.times_back) | copy-start | bytes 1179652
  10.7 19.2 %copy-start.5 = (bf16[2,256,384]{2,1,0:T(8,128)(2,1)S(1)}, bf16[2,256,384]{2,1,0:T(8,128)(2,1)}, u32[]{:S(2)}) copy-start(bf16[2,256,384]{2,1,0:T(8,128)(2,1)} %constant.17.clone.times) | copy-start | bytes 1179652
  32.3 17.5 %all-to-all-start.1 = ((f32[32,1,3200]{2,1,0:T(1,128)}), f32[32,1,3200]{2,1,0:T(1,128)S(1)}, u32[]{:S(2)}, u32[]{:S(2)}) async-start(f32[32,1,3200]{2,1,0:T(1,128)} %bitcast.2), calls=%async_computation.1 | async-start | bytes 819200 | tf_op jit(solution)/shard_map/all_to_all | solution.py:373
  34.9 8.2 %copy-start.9 = (f32[2,128,256]{2,1,0:T(8,128)S(1)}, f32[2,128,256]{2,1,0:T(8,128)}, u32[]{:S(2)}) copy-start(f32[2,128,256]{2,1,0:T(8,128)} %param.11) | copy-start | bytes 786436
  34.9 8.0 %collective-permute-start = (f32[1,128,256]{2,1,0:T(8,128)S(1)}, f32[1,128,256]{2,1,0:T(8,128)S(1)}, u32[]{:S(2)}, u32[]{:S(2)}) collective-permute-start(f32[1,128,256]{2,1,0:T(8,128)S(1)} %get-tuple-element.14), channel_id=1, source_target_pairs={{30,0},{31,1},{0,2},{1,3},{2,4},{3,5},{4,6},{5,7},{6,8},{7,9},{8,1... | collective-permute-start | bytes 393224 | tf_op jit(solution)/shard_map/ppermute | solution.py:41
  36.6 6.5 %collective-permute-start.1 = (f32[1,128,256]{2,1,0:T(8,128)S(1)}, f32[1,128,256]{2,1,0:T(8,128)S(1)}, u32[]{:S(2)}, u32[]{:S(2)}) collective-permute-start(f32[1,128,256]{2,1,0:T(8,128)S(1)} %get-tuple-element.15), channel_id=1, source_target_pairs={{2,0},{3,1},{4,2},{5,3},{6,4},{7,5},{8,6},{9,7},{10,8},{11,9},{12,... | collective-permute-start | bytes 393224 | tf_op jit(solution)/shard_map/ppermute | solution.py:41

commit v5 on v4

--- a/solution.py
+++ b/solution.py
@@ -9,6 +9,7 @@
 from jax.experimental import pallas as pl
 from jax.experimental.pallas import tpu as pltpu
 from jax.sharding import PartitionSpec as P
+
 
 ORDER = 24
 
@@ -24,6 +25,8 @@
 
 EDGE = 4
 HALO = 2 * EDGE
+SUBLANES = 8
+LANES = 128
 NEAR = 2
 RIM = 2 * NEAR
 AXES = ("tm", "band")
@@ -76,33 +79,85 @@
     return 2.0 * cheb_t((order + 1) // 2, x) * cheb_t(order // 2, x) - x
 
 
-def parities(shape):
-    row = lax.broadcasted_iota(jnp.int32, shape, 0) % 2 == 0
-    col = lax.broadcasted_iota(jnp.int32, shape, 1) % 2 == 0
-    return row, col
-
-
-def turned(value, by, axis):
-    return pltpu.roll(value, by % value.shape[axis], axis)
-
-
-def pair_table(strengths, colour, row_even, col_even):
-    axis = 1 if colour < 2 else 0
-    even = col_even if colour < 2 else row_even
-    here, before = strengths[1 - axis], turned(strengths[1 - axis], 1, axis)
-    bond = jnp.where(even, here, before) if colour % 2 == 0 else jnp.where(even, before, here)
-    return 1.0 + (math.cosh(hop_angle) - 1.0) * bond, math.sinh(hop_angle) * bond
-
-
-def apply_pairs(vector, colours, tables, row_even, col_even):
+def blocks(value):
+    rows, cols = value.shape
+    return [value[:, i : i + LANES].reshape(rows // SUBLANES, SUBLANES, LANES) for i in range(0, cols, LANES)]
+
+
+def joined(parts):
+    return jnp.concatenate([part.reshape(-1, LANES) for part in parts], 1)
+
+
+def each(function, *lists):
+    return [function(*items) for items in zip(*lists)]
+
+
+def taken(part, index):
+    numbers = lax.GatherDimensionNumbers(
+        offset_dims=(),
+        collapsed_slice_dims=(2,),
+        start_index_map=(2,),
+        operand_batching_dims=(0, 1),
+        start_indices_batching_dims=(0, 1),
+    )
+    return lax.gather(
+        part, index[..., None], numbers, (1, 1, 1), mode=lax.GatherScatterMode.PROMISE_IN_BOUNDS
+    )
+
+
+def along_columns(parts, colour):
+    place = lax.broadcasted_iota(jnp.int32, parts[0].shape, 2)
+    if colour == 0:
+        return each(lambda part: taken(part, place ^ 1), parts)
+    before, after = parts[-1:] + parts[:-1], parts[1:] + parts[:1]
+    if len(parts) == 2:
+        outer = (place == 0) | (place == LANES - 1)
+        parts = each(lambda mine, other: jnp.where(outer, other, mine), parts, after)
+    else:
+        parts = each(
+            lambda mine, low, high: jnp.where(place == LANES - 1, low, jnp.where(place == 0, high, mine)),
+            parts, before, after,
+        )
+    index = ((((place + LANES - 1) & (LANES - 1)) ^ 1) + 1) & (LANES - 1)
+    return each(lambda part: taken(part, index), parts)
+
+
+def along_rows(parts, colour):
+    place = lax.broadcasted_iota(jnp.int32, parts[0].shape, 1)
+    even = (place & 1) == 0
+
+    def partner(part):
+        up, down = pltpu.roll(part, SUBLANES - 1, 1), pltpu.roll(part, 1, 1)
+        if colour == 2:
+            return jnp.where(even, up, down)
+        inside = jnp.where(even, down, up)
+        if part.shape[0] == 1:
+            return inside
+        low = jnp.concatenate([down[-1:], down[:-1]], 0)
+        high = jnp.concatenate([up[1:], up[:1]], 0)
+        return jnp.where(place == 0, low, jnp.where(place == SUBLANES - 1, high, inside))
+
+    return each(partner, parts)
+
+
+def partners(parts, colour):
+    return along_columns(parts, colour) if colour < 2 else along_rows(parts, colour)
+
+
+def pair_table(strengths, colour):
+    parts = strengths[colour // 2]
+    odd = lax.broadcasted_iota(jnp.int32, parts[0].shape, 2 if colour < 2 else 1) & 1
+    holder = odd == colour % 2
+    bonds = each(lambda mine, other: jnp.where(holder, mine, other), parts, partners(parts, colour))
+    cosh_part = each(lambda bond: 1.0 + (math.cosh(hop_angle) - 1.0) * bond, bonds)
+    return cosh_part, each(lambda bond: math.sinh(hop_angle) * bond, bonds)
+
+
+def apply_pairs(parts, colours, tables):
     for colour in colours:
-        axis = 1 if colour < 2 else 0
-        even = col_even if colour < 2 else row_even
-        ahead, behind = turned(vector, -1, axis), turned(vector, 1, axis)
-        first, second = (ahead, behind) if colour % 2 == 0 else (behind, ahead)
-        cosh_part, sinh_part = tables[colour]
-        vector = cosh_part * vector + sinh_part * jnp.where(even, first, second)
-    return vector
+        mix = lambda mine, other, cosh_part, sinh_part: cosh_part * mine + sinh_part * other
+        parts = each(mix, parts, partners(parts, colour), *tables[colour])
+    return parts
 
 
 def last_sign():
@@ -126,69 +181,87 @@
     return dot(a[0], b[0]) + (dot(a[0], b[1]) + dot(a[1], b[0]))
 
 
+def times(a, b):
+    return each(lax.mul, a, b)
+
+
 def wide(main, halo):
-    return jnp.concatenate([main, halo], 0)
+    return each(lambda rows, rim: jnp.concatenate([rows, rim], 0), main, halo)
 
 
 def local_kernel(phonon, guess, bonds, expo, tables, inner):
-    slices, rows, cols = guess.shape
-    parity = parities((rows, cols))
-    strengths = (bonds[0].astype(jnp.float32), bonds[1].astype(jnp.float32))
-    pairs = [pair_table(strengths, q, *parity) for q in range(3)]
+    slices = guess.shape[0]
+    strengths = [blocks(bonds[d].astype(jnp.float32)) for d in range(2)]
+    pairs = [pair_table(strengths, q) for q in range(3)]
     for q in range(3):
         for part in range(2):
-            tables[2 * q + part] = pairs[q][part]
+            tables[2 * q + part] = joined(pairs[q][part])
     for s in range(slices):
-        expo[s] = jnp.exp(-coupling * phonon[s])
-        inner[s] = apply_pairs(expo[s] * guess[s], (0, 1, 2), pairs, *parity)
+        grown = jnp.exp(-coupling * phonon[s])
+        expo[s] = grown
+        inner[s] = joined(apply_pairs(blocks(grown * guess[s]), (0, 1, 2), pairs))
 
 
 class Band:
     def __init__(self, bonds, edges, expo, tables, slices):
-        _, rows, cols = bonds.shape
-        self.rows, self.slices = rows, slices
-        self.main, self.strip, self.all = (parities((n, cols)) for n in (rows, HALO, rows + HALO))
-        across, down = edges[2 * slices], edges[2 * slices + 1]
-        self.pairs = [(tables[2 * q], tables[2 * q + 1]) for q in range(3)]
-        self.strip_pairs = [pair_table((across, down), q, *self.strip) for q in range(3)]
-        vertical = wide(bonds[1].astype(jnp.float32), down)
-        self.wide_pairs = {3: pair_table((None, vertical), 3, *self.all)}
-        self.expo = [expo[s] for s in range(slices)]
-        self.strip_expo = [jnp.exp(-coupling * edges[slices + s]) for s in range(slices)]
+        self.tiles = bonds.shape[1] // SUBLANES
+        across, down = blocks(edges[2 * slices]), blocks(edges[2 * slices + 1])
+        self.pairs = [[blocks(tables[2 * q + part]) for part in range(2)] for q in range(3)]
+        self.strip_pairs = [pair_table((across, down), q) for q in range(3)]
+        vertical = wide(blocks(bonds[1].astype(jnp.float32)), down)
+        self.wide_pairs = {3: pair_table((None, vertical), 3)}
+        self.expo = [blocks(expo[s]) for s in range(slices)]
+        self.strip_expo = [blocks(jnp.exp(-coupling * edges[slices + s])) for s in range(slices)]
+
+    def own(self, parts):
+        return each(lambda part: part[: self.tiles], parts)
+
+    def rim(self, parts):
+        return each(lambda part: part[self.tiles :], parts)
 
     def inner(self, s, field):
-        return apply_pairs(self.expo[s] * field, (0, 1, 2), self.pairs, *self.main)
+        return apply_pairs(times(self.expo[s], field), (0, 1, 2), self.pairs)
 
     def propagated(self, s, inner, strip):
-        strip = apply_pairs(self.strip_expo[s] * strip, (0, 1, 2), self.strip_pairs, *self.strip)
-        return apply_pairs(wide(inner, strip), (3,), self.wide_pairs, *self.all)
+        strip = apply_pairs(times(self.strip_expo[s], strip), (0, 1, 2), self.strip_pairs)
+        return apply_pairs(wide(inner, strip), (3,), self.wide_pairs)
 
     def pulled(self, field):
-        field = apply_pairs(field, (3,), self.wide_pairs, *self.all)[: self.rows]
-        return apply_pairs(field, (2, 1, 0), self.pairs, *self.main)
+        field = self.own(apply_pairs(field, (3,), self.wide_pairs))
+        return apply_pairs(field, (2, 1, 0), self.pairs)
+
+
+def with_following(guess, edges, after, after_edge):
+    fields = [wide(blocks(guess[s]), blocks(edges[s])) for s in range(guess.shape[0])]
+    sign = last_sign()
+    fields.append(each(lambda part: sign * part, wide(blocks(after[0]), blocks(after_edge[0]))))
+    return fields
 
 
 def residual_kernel(source, guess, bonds, edges, after, after_edge, expo, tables, inner, basis, out):
-    slices, rows, cols = guess.shape
+    slices, rows, _ = guess.shape
     band = Band(bonds, edges, expo, tables, slices)
-    field = [wide(guess[s], edges[s]) for s in range(slices)]
-    field.append(last_sign() * wide(after[0], after_edge[0]))
+    field = with_following(guess, edges, after, after_edge)
     pieces = []
     link = field[0]
     for s in range(slices):
-        applied = band.propagated(s, inner[s], edges[s])
-        following = field[s + 1] - applied
-        pieces.append(source[s] - link[:rows] + band.expo[s] * band.pulled(following))
+        applied = band.propagated(s, blocks(inner[s]), blocks(edges[s]))
+        following = each(lax.sub, field[s + 1], applied)
+        back = joined(times(band.expo[s], band.pulled(following)))
+        pieces.append(source[s] - joined(band.own(link)) + back)
         link = following
-    pieces.append(applied[:rows])
-    stacked = jnp.concatenate(pieces, 0)
-    out[...] = product(basis, halves(stacked), ROWS_BY_ROWS)
-
-
-def mode_kernel(count, mixed, times, times_back, rows_in, rims, out):
+    pieces.insert(1, joined(band.own(applied)))
+    places = [0, slices] + list(range(1, slices))
+    for group in (slice(0, 2), slice(2, None)):
+        waves = product(basis, halves(jnp.concatenate(pieces[group], 0)), ROWS_BY_ROWS)
+        for i, s in enumerate(places[group]):
+            out[:, s * rows : (s + 1) * rows] = waves[:, i * rows : (i + 1) * rows]
+
+
+def mode_kernel(count, mixed, slices_in, slices_out, rows_in, rims, out):
     tm, band, modes, width = mixed.shape
     size = tm * modes
-    freqs = times.shape[1] // modes
+    freqs = slices_in.shape[1] // modes
     length = rows_in.shape[1]
     per = length // band
     slots = width // per
@@ -203,7 +276,7 @@
         ],
         0,
     )
-    waves = product(halves(product(times, halves(stacked))), rows_in)
+    waves = product(halves(product(slices_in, halves(stacked))), rows_in)
 
     place = lax.axis_index("tm") * band + lax.axis_index("band")
     shape = (modes, length)
@@ -222,8 +295,8 @@
         gains.append(gain)
     waves = halves(waves * jnp.concatenate(gains, 0))
 
-    back = product(times_back, halves(product(waves, rows_in, ROWS_BY_ROWS)))
-    edge = product(halves(product(halves(rims[...]), waves, ROWS_BY_ROWS)), times)
+    back = product(slices_out, halves(product(waves, rows_in, ROWS_BY_ROWS)))
+    edge = product(halves(product(halves(rims[...]), waves, ROWS_BY_ROWS)), slices_in)
     turns = [
         pltpu.roll(edge[:, s * size : (s + 1) * size], RIM * s * modes, 1, stride=modes, stride_axis=0)
         for s in range(slots)
@@ -245,20 +318,14 @@
             out[at + slots * modes : at + chunk] = rim[p : p + 1]
 
 
-def force_kernel(base, guess, bonds, edges, after, after_edge, expo, tables, mixed, basis, sol, mom, turned_edge):
-    slices, rows, cols = guess.shape
+def force_kernel(base, guess, bonds, edges, after, after_edge, expo, tables, mixed, basis, order, sol, mom, turned_edge):
+    slices, _, cols = guess.shape
     devices = lax.axis_size("tm") * lax.axis_size("band")
     modes = cols // devices
     slots = slices + 1
     chunk = slots * modes + 1
     band = Band(bonds, edges, expo, tables, slices)
     columns = (basis[0], basis[1])
-
-    arrived = [
-        jnp.concatenate([mixed[d * chunk + s * modes : d * chunk + (s + 1) * modes] for d in range(devices)], 0)
-        for s in range(slots)
-    ]
-    timed = product(halves(jnp.concatenate(arrived, 1).T), columns)
 
     rim = mixed[pl.ds(slots * modes, devices, stride=chunk), :]
     lanes = rim.shape[1]
@@ -267,22 +334,22 @@
     turned_edge[...] = rim.T
     groups = lanes // modes
     lines = jnp.concatenate([turned_edge[pl.ds(m, groups, stride=modes), :] for m in range(modes)], 1)
-    order = jnp.concatenate(
-        [jnp.concatenate([part.reshape(devices, modes, cols)[:, m] for m in range(modes)], 0)[None] for part in columns], 0
-    )
     strips = product(halves(lines), order)
 
-    start = [wide(guess[s], edges[s]) for s in range(slices)]
-    start.append(last_sign() * wide(after[0], after_edge[0]))
+    start = with_following(guess, edges, after, after_edge)
     field = []
     for s in range(slots):
-        strip = turned(strips[s * RIM : s * RIM + HALO], -NEAR, 0)
-        field.append(start[s] + relaxation * wide(timed[s * rows : (s + 1) * rows], strip))
+        arrived = [mixed[d * chunk + s * modes : d * chunk + (s + 1) * modes] for d in range(devices)]
+        timed = product(halves(jnp.concatenate(arrived, 0).T), columns)
+        strip = pltpu.roll(strips[s * RIM : s * RIM + HALO], HALO - NEAR, 0)
+        change = wide(blocks(timed), blocks(strip))
+        field.append(each(lambda old, new: old + relaxation * new, start[s], change))
     for s in range(slices):
-        own = field[s][:rows]
-        image = field[s + 1] - band.propagated(s, band.inner(s, own), field[s][rows:])
-        sol[s] = own
-        fermion = -2.0 * coupling * band.expo[s] * own * band.pulled(image)
+        own = band.own(field[s])
+        ahead = band.propagated(s, band.inner(s, own), band.rim(field[s]))
+        pulled = band.pulled(each(lax.sub, field[s + 1], ahead))
+        sol[s] = joined(own)
+        fermion = (-2.0 * coupling) * joined(times(times(band.expo[s], own), pulled))
         mom[s] = base[s] - step_size * fermion
 
 
@@ -342,7 +409,7 @@
     slots = slices + 1
 
     slot_times = np.concatenate([time_basis(total, slices * np.arange(tm) + s) for s in range(slots)], 1)
-    times = np.kron(slot_times, np.eye(modes))
+    slices_in = np.kron(slot_times, np.eye(modes))
     near = np.concatenate([np.arange(-NEAR, 0), rows + np.arange(NEAR)])
     rim_sites = np.concatenate([(b * rows + near) % length for b in range(band)])
     rims_basis = np.asarray(space_basis(length, rim_sites).T, np.float32)
@@ -366,9 +433,9 @@
     mixed = lax.all_to_all(sent.reshape(devices, modes, slots * rows), AXES, 0, 0, tiled=True)
     wave_rows = devices * (slots * modes + 1)
     back = call(
-        functools.partial(mode_kernel, cols), jax.ShapeDtypeStruct((wave_rows, rows), jnp.float32),
+        functools.partial(mode_kernel, cols), on(wave_rows, rows),
         mixed.reshape(tm, band, modes, slots * rows),
-        const_halves(times), const_halves(np.ascontiguousarray(times.T)), rows_in, rims_basis,
+        const_halves(slices_in), const_halves(np.ascontiguousarray(slices_in.T)), rows_in, rims_basis,
     )
     mixed = lax.all_to_all(back.reshape(devices, 1, -1), AXES, 0, 0, tiled=True)
 
@@ -382,6 +449,7 @@
         force_kernel, (like, like),
         base, guess, bonds, edges, after, after_edge, expo, tables,
         mixed.reshape(wave_rows, rows), columns,
+        np.ascontiguousarray(columns.reshape(2, devices, modes, cols).swapaxes(1, 2).reshape(2, cols, cols)),
         scratch_shapes=[pltpu.VMEM((cols // band, devices), jnp.float32)],
     )
 

time: 52.5 us -> 52 us (level)
  Pallas kernels: 7.29 us -> 6.7 us
    pallas_call x4, Pallas kernels: 6.23 us -> 5.64 us  [call(): pl.pallas_call(kernel, out_shape=outs, in_specs=[vmem] * len(operands), o...]
where the time goes in v5:
time: 52 us; the launch traced here: 51.8 us
  blocking collectives  19.2 us (37%)
  waiting for transfers between devices  13.5 us (26%)
  starting transfers between devices  11.5 us (22%)
  Pallas kernels  6.7 us (13%)
  between operations  0.77 us (1%)
    all_to_all x1, blocking collectives, shards(): lax.all_to_all(sent.reshape(devices, modes, slots * rows), AXES, 0, 0, ti...  19.2 us
    ppermute x5, starting transfers between devices, shifted(): return lax.ppermute(value, AXES, pairs)  8.86 us
    ppermute x5, waiting for transfers between devices, shifted(): return lax.ppermute(value, AXES, pairs)  6.81 us
    all_to_all x1, waiting for transfers between devices, shards(): mixed = lax.all_to_all(back.reshape(devices, 1, -1), AXES, 0, 0, tiled=True)  6.66 us
    pallas_call x4, Pallas kernels, call(): pl.pallas_call(kernel, out_shape=outs, in_specs=[vmem] * len(operands), o...  5.64 us
    all_to_all x1, starting transfers between devices, shards(): mixed = lax.all_to_all(back.reshape(devices, 1, -1), AXES, 0, 0, tiled=True)  2.61 us
    pallas_call x1, Pallas kernels, pack(): pl.pallas_call(pack_kernel, grid=(1,), out_shape=[pltpu.VMEM(o, jnp.float...  1.06 us
  transfers between devices with their start and end apart: 6, of which 4 were waited for; matrix products, arithmetic and copies ran while one was open for 0% of the time, Pallas kernels for 1%

profile of v5, /device:TPU:1, one launch (start us, length us, event | category | flops | bytes accessed | tf_op | source)
XLA Modules:
  0.0 51.8 jit_solution(17455341492806829696)
XLA Ops:
  0.6 0.0 copy-start.1
  0.6 0.0 copy-start
  0.6 0.0 copy-start.2
  0.7 1.1 %shard_map.122 = (f32[1,128,256]{2,1,0:T(8,128)S(1)}, f32[6,8,256]{2,1,0:T(8,128)S(1)}, f32[1,8,256]{2,1,0:T(8,128)S(1)}) custom-call(f32[2,128,256]{2,1,0:T(8,128)} %guess.7, f32[2,128,256]{2,1,0:T(8,128)} %guess.7, f32[2,128,256]{2,1,0:T(8,128)} %phonon.1, s32[2,128,256]{2,1,0:T(8,128)} %bonds.5, f32[2,128,256]{2,1,0:T(8,128)} %guess.7, ...), custom_call_target="tpu_custom_call" | custom-call | tf_op jit(solution)/shard_map/pallas_call | solution.py:395
  1.7 0.1 collective-permute-start.3
  1.8 2.7 %collective-permute-start.2 = (f32[6,8,256]{2,1,0:T(8,128)S(1)}, f32[6,8,256]{2,1,0:T(8,128)S(1)}, u32[]{:S(2)}, u32[]{:S(2)}) collective-permute-start(f32[6,8,256]{2,1,0:T(8,128)S(1)} %get-tuple-element.8), channel_id=1, source_target_pairs={{1,0},{0,1},{3,2},{2,3},{5,4},{4,5},{7,6},{6,7},{9,8},{8,9},{11,10... | collective-permute-start | bytes 147464 | tf_op jit(solution)/shard_map/ppermute | solution.py:44
  4.5 0.0 copy-start.3
  4.5 0.0 copy-start.6
  4.5 4.4 %collective-permute-start.4 = (f32[1,8,256]{2,1,0:T(8,128)S(1)}, f32[1,8,256]{2,1,0:T(8,128)S(1)}, u32[]{:S(2)}, u32[]{:S(2)}) collective-permute-start(f32[1,8,256]{2,1,0:T(8,128)S(1)} %get-tuple-element.10), channel_id=1, source_target_pairs={{3,0},{2,1},{5,2},{4,3},{7,4},{6,5},{9,6},{8,7},{11,8},{10,9},{13,... | collective-permute-start | bytes 24584 | tf_op jit(solution)/shard_map/ppermute | solution.py:44
  8.9 0.0 copy-done.1
  8.9 0.0 copy-done
  8.9 0.0 copy-done.2
  8.9 0.4 shard_map.123
  9.3 0.4 collective-permute-done.4.after_edge
  9.7 0.0 collective-permute-done.2.edges
  9.7 0.0 collective-permute-done.3.after
  9.7 0.0 copy-done.3
  9.7 0.0 copy-done.6
  9.7 0.0 copy-start.8
  9.7 0.0 copy-start.9
  9.7 0.9 %shard_map.124 = f32[256,384]{1,0:T(8,128)S(1)} custom-call(f32[2,128,256]{2,1,0:T(8,128)S(1)} %copy-done.6, f32[2,128,256]{2,1,0:T(8,128)S(1)} %copy-done, s32[2,128,256]{2,1,0:T(8,128)S(1)} %copy-done.1, f32[6,8,256]{2,1,0:T(8,128)S(1)} %collective-permute-done.2.edges, f32[1,128,256]{2,1,0:T(8,128)S(1)} %collective-permute-done.3.after, ...), custom_call_target="tpu_custom_call" | custom-call | bytes 4194304 | tf_op jit(solution)/shard_map/pallas_call | solution.py:358
  10.7 0.0 copy-start.4
  10.7 0.0 copy-start.5
  10.7 19.2 %all_to_all.10 = f32[32,8,384]{2,1,0:T(8,128)S(1)} all-to-all(f32[32,8,384]{2,1,0:T(8,128)S(1)} %bitcast.6), channel_id=1, replica_groups=mesh['tm'=16,'band'=2] {'tm','band'}, dimensions={0} | all-to-all | bytes 786432 | tf_op jit(solution)/shard_map/all_to_all | solution.py:433
  29.9 0.0 copy-done.8
  29.9 0.0 copy-done.9
  29.9 0.0 copy-done.4
  29.9 0.0 copy-done.5
  29.9 2.3 %shard_map.125 = f32[800,128]{1,0:T(8,128)} custom-call(f32[16,2,8,384]{3,2,1,0:T(8,128)S(1)} %bitcast.5, bf16[2,256,384]{2,1,0:T(8,128)(2,1)S(1)} %copy-done.5, bf16[2,384,256]{2,1,0:T(8,128)(2,1)S(1)} %copy-done.4, bf16[2,256,256]{2,1,0:T(8,128)(2,1)S(1)} %copy-done.8, f32[8,256]{1,0:T(8,128)S(1)} %copy-done.9), custom_call_target="tpu_custom_call" | custom-call | bytes 4194304 | tf_op jit(solution)/shard_map/pallas_call | solution.py:358
  32.2 2.6 %all-to-all-start.1 = ((f32[32,1,3200]{2,1,0:T(1,128)}), f32[32,1,3200]{2,1,0:T(1,128)S(1)}, u32[]{:S(2)}, u32[]{:S(2)}) async-start(f32[32,1,3200]{2,1,0:T(1,128)} %bitcast.2), calls=%async_computation.1 | async-start | bytes 819200 | tf_op jit(solution)/shard_map/all_to_all | solution.py:440
  34.8 0.0 copy-start.10
  34.9 1.7 %collective-permute-start = (f32[1,128,256]{2,1,0:T(8,128)S(1)}, f32[1,128,256]{2,1,0:T(8,128)S(1)}, u32[]{:S(2)}, u32[]{:S(2)}) collective-permute-start(f32[1,128,256]{2,1,0:T(8,128)S(1)} %get-tuple-element.14), channel_id=1, source_target_pairs={{30,0},{31,1},{0,2},{1,3},{2,4},{3,5},{4,6},{5,7},{6,8},{7,9},{8,1... | collective-permute-start | bytes 393224 | tf_op jit(solution)/shard_map/ppermute | solution.py:44
  36.5 0.0 copy-start.7
  36.5 0.0 collective-permute-start.1
  36.5 6.3 %collective-permute-done = f32[1,128,256]{2,1,0:T(8,128)S(1)} collective-permute-done((f32[1,128,256]{2,1,0:T(8,128)S(1)}, f32[1,128,256]{2,1,0:T(8,128)S(1)}, u32[]{:S(2)}, u32[]{:S(2)}) %collective-permute-start) | collective-permute-done | bytes 131104 | tf_op jit(solution)/shard_map/ppermute | solution.py:44
  42.8 0.1 collective-permute-done.1
  43.0 0.0 copy-done.10
  43.0 0.1 fusion.3.base
  43.1 6.7 %all-to-all-done.1 = f32[32,1,3200]{2,1,0:T(1,128)S(1)} async-done(((f32[32,1,3200]{2,1,0:T(1,128)}), f32[32,1,3200]{2,1,0:T(1,128)S(1)}, u32[]{:S(2)}, u32[]{:S(2)}) %all-to-all-start.1) | async-done | bytes 409632 | tf_op jit(solution)/shard_map/all_to_all | solution.py:440
  49.7 0.0 copy-done.7
  49.7 2.0 %shard_map.126 = (f32[2,128,256]{2,1,0:T(8,128)}, f32[2,128,256]{2,1,0:T(8,128)}) custom-call(f32[2,128,256]{2,1,0:T(8,128)S(1)} %fusion.3.base, f32[2,128,256]{2,1,0:T(8,128)S(1)} %copy-done, s32[2,128,256]{2,1,0:T(8,128)S(1)} %copy-done.1, f32[6,8,256]{2,1,0:T(8,128)S(1)} %collective-permute-done.2.edges, f32[1,128,256]{2,1,0:T(8,128)S(1)} %collective-permute-done.3.after, ...), custom_call_target="tpu_custom_call" | custom-call | bytes 4194304 | tf_op jit(solution)/shard_map/pallas_call | solution.py:358
  (1 shorter events, 0.0 us)
Async XLA Ops:
  0.6 8.3 %copy-start.1 = (s32[2,128,256]{2,1,0:T(8,128)S(1)}, s32[2,128,256]{2,1,0:T(8,128)}, u32[]{:S(2)}) copy-start(s32[2,128,256]{2,1,0:T(8,128)} %bonds.5) | copy-start | bytes 786436
  0.6 8.3 %copy-start = (f32[2,128,256]{2,1,0:T(8,128)S(1)}, f32[2,128,256]{2,1,0:T(8,128)}, u32[]{:S(2)}) copy-start(f32[2,128,256]{2,1,0:T(8,128)} %guess.7) | copy-start | bytes 786436
  0.6 8.3 %copy-start.2 = (f32[2,128,256]{2,1,0:T(8,128)S(1)}, f32[2,128,256]{2,1,0:T(8,128)}, u32[]{:S(2)}) copy-start(f32[2,128,256]{2,1,0:T(8,128)} %phonon.1) | copy-start | bytes 786436
  1.7 8.0 %collective-permute-start.3 = (f32[1,128,256]{2,1,0:T(8,128)S(1)}, f32[1,128,256]{2,1,0:T(8,128)S(1)}, u32[]{:S(2)}, u32[]{:S(2)}) collective-permute-start(f32[1,128,256]{2,1,0:T(8,128)S(1)} %get-tuple-element.9), channel_id=1, source_target_pairs={{2,0},{3,1},{4,2},{5,3},{6,4},{7,5},{8,6},{9,7},{10,8},{11,9},{12,... | collective-permute-start | bytes 393224 | tf_op jit(solution)/shard_map/ppermute | solution.py:44
  1.8 7.9 %collective-permute-start.2 = (f32[6,8,256]{2,1,0:T(8,128)S(1)}, f32[6,8,256]{2,1,0:T(8,128)S(1)}, u32[]{:S(2)}, u32[]{:S(2)}) collective-permute-start(f32[6,8,256]{2,1,0:T(8,128)S(1)} %get-tuple-element.8), channel_id=1, source_target_pairs={{1,0},{0,1},{3,2},{2,3},{5,4},{4,5},{7,6},{6,7},{9,8},{8,9},{11,10... | collective-permute-start | bytes 147464 | tf_op jit(solution)/shard_map/ppermute | solution.py:44
  4.5 5.2 %copy-start.3 = (bf16[2,256,256]{2,1,0:T(8,128)(2,1)S(1)}, bf16[2,256,256]{2,1,0:T(8,128)(2,1)}, u32[]{:S(2)}) copy-start(bf16[2,256,256]{2,1,0:T(8,128)(2,1)} %constant.18.clone.basis) | copy-start | bytes 786436
  4.5 5.2 %copy-start.6 = (f32[2,128,256]{2,1,0:T(8,128)S(1)}, f32[2,128,256]{2,1,0:T(8,128)}, u32[]{:S(2)}) copy-start(f32[2,128,256]{2,1,0:T(8,128)} %source.1) | copy-start | bytes 786436
  4.5 5.2 %collective-permute-start.4 = (f32[1,8,256]{2,1,0:T(8,128)S(1)}, f32[1,8,256]{2,1,0:T(8,128)S(1)}, u32[]{:S(2)}, u32[]{:S(2)}) collective-permute-start(f32[1,8,256]{2,1,0:T(8,128)S(1)} %get-tuple-element.10), channel_id=1, source_target_pairs={{3,0},{2,1},{5,2},{4,3},{7,4},{6,5},{9,6},{8,7},{11,8},{10,9},{13,... | collective-permute-start | bytes 24584 | tf_op jit(solution)/shard_map/ppermute | solution.py:44
  9.7 20.2 %copy-start.8 = (bf16[2,256,256]{2,1,0:T(8,128)(2,1)S(1)}, bf16[2,256,256]{2,1,0:T(8,128)(2,1)}, u32[]{:S(2)}) copy-start(bf16[2,256,256]{2,1,0:T(8,128)(2,1)} %constant.21.clone.rows_in) | copy-start | bytes 786436
  9.7 20.2 %copy-start.9 = (f32[8,256]{1,0:T(8,128)S(1)}, f32[8,256]{1,0:T(8,128)}, u32[]{:S(2)}) copy-start(f32[8,256]{1,0:T(8,128)} %constant.22.clone.rims) | copy-start | bytes 24580
  10.7 19.3 %copy-start.4 = (bf16[2,384,256]{2,1,0:T(8,128)(2,1)S(1)}, bf16[2,384,256]{2,1,0:T(8,128)(2,1)}, u32[]{:S(2)}) copy-start(bf16[2,384,256]{2,1,0:T(8,128)(2,1)} %constant.20.clone.slices_out) | copy-start | bytes 1179652
  10.7 19.2 %copy-start.5 = (bf16[2,256,384]{2,1,0:T(8,128)(2,1)S(1)}, bf16[2,256,384]{2,1,0:T(8,128)(2,1)}, u32[]{:S(2)}) copy-start(bf16[2,256,384]{2,1,0:T(8,128)(2,1)} %constant.19.clone.slices_in) | copy-start | bytes 1179652
  32.2 17.5 %all-to-all-start.1 = ((f32[32,1,3200]{2,1,0:T(1,128)}), f32[32,1,3200]{2,1,0:T(1,128)S(1)}, u32[]{:S(2)}, u32[]{:S(2)}) async-start(f32[32,1,3200]{2,1,0:T(1,128)} %bitcast.2), calls=%async_computation.1 | async-start | bytes 819200 | tf_op jit(solution)/shard_map/all_to_all | solution.py:440
  34.8 8.2 %copy-start.10 = (f32[2,128,256]{2,1,0:T(8,128)S(1)}, f32[2,128,256]{2,1,0:T(8,128)}, u32[]{:S(2)}) copy-start(f32[2,128,256]{2,1,0:T(8,128)} %param.12) | copy-start | bytes 786436
  34.9 8.0 %collective-permute-start = (f32[1,128,256]{2,1,0:T(8,128)S(1)}, f32[1,128,256]{2,1,0:T(8,128)S(1)}, u32[]{:S(2)}, u32[]{:S(2)}) collective-permute-start(f32[1,128,256]{2,1,0:T(8,128)S(1)} %get-tuple-element.14), channel_id=1, source_target_pairs={{30,0},{31,1},{0,2},{1,3},{2,4},{3,5},{4,6},{5,7},{6,8},{7,9},{8,1... | collective-permute-start | bytes 393224 | tf_op jit(solution)/shard_map/ppermute | solution.py:44
  36.5 13.2 %copy-start.7 = (bf16[2,256,256]{2,1,0:T(8,128)(2,1)S(1)}, bf16[2,256,256]{2,1,0:T(8,128)(2,1)}, u32[]{:S(2)}) copy-start(bf16[2,256,256]{2,1,0:T(8,128)(2,1)} %constant.23.clone.order) | copy-start | bytes 786436
  36.5 6.4 %collective-permute-start.1 = (f32[1,128,256]{2,1,0:T(8,128)S(1)}, f32[1,128,256]{2,1,0:T(8,128)S(1)}, u32[]{:S(2)}, u32[]{:S(2)}) collective-permute-start(f32[1,128,256]{2,1,0:T(8,128)S(1)} %get-tuple-element.15), channel_id=1, source_target_pairs={{2,0},{3,1},{4,2},{5,3},{6,4},{7,5},{8,6},{9,7},{10,8},{11,9},{12,... | collective-permute-start | bytes 393224 | tf_op jit(solution)/shard_map/ppermute | solution.py:44

commit v6 on v5

--- a/solution.py
+++ b/solution.py
@@ -371,9 +371,10 @@
 
 
 def pack_kernel(guess, *refs):
-    tops, ends, outs = refs[:3], refs[3:6], refs[6:]
-    first, rims, rim = outs
+    last_ph, tops, ends, outs = refs[0], refs[1:4], refs[4:7], refs[7:]
+    first, last, rims, rim = outs
     first[...] = guess[...]
+    last[...] = last_ph[...]
     early = lax.broadcasted_iota(jnp.int32, tops[0].shape, 1) < EDGE
     at = 0
     for top, end in zip(tops, ends):
@@ -391,14 +392,15 @@
     whole = lambda shape: pl.BlockSpec(shape, lambda i: (0, 0, 0))
     tops = [whole((v.shape[0], HALO, cols)) for v in fields]
     ends = [pl.BlockSpec((v.shape[0], HALO, cols), lambda i: (0, last, 0)) for v in fields]
-    outs = [(1, rows, cols), (2 * slices + 2, HALO, cols), (1, HALO, cols)]
+    outs = [(1, rows, cols), (1, rows, cols), (2 * slices + 2, HALO, cols), (1, HALO, cols)]
+    final = pl.BlockSpec((1, rows, cols), lambda i: (slices - 1, 0, 0))
     return pl.pallas_call(
         pack_kernel,
         grid=(1,),
         out_shape=[pltpu.VMEM(o, jnp.float32) for o in outs],
-        in_specs=[whole((1, rows, cols))] + tops + ends,
+        in_specs=[whole((1, rows, cols)), final] + tops + ends,
         out_specs=[whole(o) for o in outs],
-    )(guess, *fields, *fields)
+    )(guess, phonon, *fields, *fields)
 
 
 def shards(phonon, momentum, source, guess, bonds):
@@ -416,7 +418,7 @@
     rows_in = const_halves(space_basis(length, np.arange(length)).T)
     columns = const_halves(space_basis(cols, np.arange(cols)))
 
-    first, rims, rim = pack(phonon, guess, bonds)
+    first, last, rims, rim = pack(phonon, guess, bonds)
     edges = band_halo(rims, 0)
     after = shifted(first, 1, 0)
     after_edge = band_halo(rim, 1)
@@ -440,7 +442,7 @@
     mixed = lax.all_to_all(back.reshape(devices, 1, -1), AXES, 0, 0, tiled=True)
 
     after_ph = shifted(phonon[:1], 1, 0)
-    before_ph = shifted(phonon[-1:], -1, 0)
+    before_ph = shifted(last, -1, 0)
     ring = jnp.concatenate([before_ph, phonon, after_ph], 0)
     boson = stiffness * (2.0 * phonon - ring[:-2] - ring[2:]) + mass_term * phonon
     base = momentum - step_size * boson

time: 52 us -> 52.1 us (level)
  no operation moved by 1% of the time
where the time goes in v6:
time: 52.1 us; the launch traced here: 51.8 us
  blocking collectives  19.2 us (37%)
  waiting for transfers between devices  13.4 us (26%)
  starting transfers between devices  11.6 us (22%)
  Pallas kernels  6.75 us (13%)
  between operations  0.77 us (1%)
    all_to_all x1, blocking collectives, shards(): lax.all_to_all(sent.reshape(devices, modes, slots * rows), AXES, 0, 0, ti...  19.2 us
    ppermute x5, starting transfers between devices, shifted(): return lax.ppermute(value, AXES, pairs)  8.97 us
    ppermute x5, waiting for transfers between devices, shifted(): return lax.ppermute(value, AXES, pairs)  6.7 us
    all_to_all x1, waiting for transfers between devices, shards(): mixed = lax.all_to_all(back.reshape(devices, 1, -1), AXES, 0, 0, tiled=True)  6.67 us
    pallas_call x4, Pallas kernels, call(): pl.pallas_call(kernel, out_shape=outs, in_specs=[vmem] * len(operands), o...  5.64 us
    all_to_all x1, starting transfers between devices, shards(): mixed = lax.all_to_all(back.reshape(devices, 1, -1), AXES, 0, 0, tiled=True)  2.61 us
    pallas_call x1, Pallas kernels, pack(): pl.pallas_call(pack_kernel, grid=(1,), out_shape=[pltpu.VMEM(o, jnp.float...  1.1 us
  transfers between devices with their start and end apart: 6, of which 4 were waited for; matrix products, arithmetic and copies ran while one was open for 0% of the time, Pallas kernels for 1%

profile of v6, /device:TPU:1, one launch (start us, length us, event | category | flops | bytes accessed | tf_op | source)
XLA Modules:
  0.0 51.8 jit_solution(1328778552620456590)
XLA Ops:
  0.6 0.0 copy-start.2
  0.6 0.0 copy-start
  0.6 0.0 copy-start.1
  0.7 1.1 %shard_map.122 = (f32[1,128,256]{2,1,0:T(8,128)S(1)}, f32[1,128,256]{2,1,0:T(8,128)S(1)}, f32[6,8,256]{2,1,0:T(8,128)S(1)}, f32[1,8,256]{2,1,0:T(8,128)S(1)}) custom-call(f32[2,128,256]{2,1,0:T(8,128)} %guess.7, f32[2,128,256]{2,1,0:T(8,128)} %phonon.1, f32[2,128,256]{2,1,0:T(8,128)} %guess.7, f32[2,128,256]{2,1,0:T(8,128)} %phonon.1, s32[2,128,256]{2,1,0:T(8,128)} %bonds.5, ...), custom_call_target="tpu_custom_call" | custom-call | tf_op jit(solution)/shard_map/pallas_call | solution.py:397
  1.8 0.1 collective-permute-start.3
  1.8 2.7 %collective-permute-start.2 = (f32[6,8,256]{2,1,0:T(8,128)S(1)}, f32[6,8,256]{2,1,0:T(8,128)S(1)}, u32[]{:S(2)}, u32[]{:S(2)}) collective-permute-start(f32[6,8,256]{2,1,0:T(8,128)S(1)} %get-tuple-element.10), channel_id=1, source_target_pairs={{1,0},{0,1},{3,2},{2,3},{5,4},{4,5},{7,6},{6,7},{9,8},{8,9},{11,10... | collective-permute-start | bytes 147464 | tf_op jit(solution)/shard_map/ppermute | solution.py:44
  4.5 0.0 copy-start.3
  4.5 0.0 copy-start.6
  4.5 4.4 %collective-permute-start.4 = (f32[1,8,256]{2,1,0:T(8,128)S(1)}, f32[1,8,256]{2,1,0:T(8,128)S(1)}, u32[]{:S(2)}, u32[]{:S(2)}) collective-permute-start(f32[1,8,256]{2,1,0:T(8,128)S(1)} %get-tuple-element.12), channel_id=1, source_target_pairs={{3,0},{2,1},{5,2},{4,3},{7,4},{6,5},{9,6},{8,7},{11,8},{10,9},{13,... | collective-permute-start | bytes 24584 | tf_op jit(solution)/shard_map/ppermute | solution.py:44
  8.9 0.0 copy-done.2
  8.9 0.0 copy-done
  9.0 0.0 copy-done.1
  9.0 0.4 shard_map.123
  9.4 0.4 collective-permute-done.4.after_edge
  9.7 0.0 collective-permute-done.2.edges
  9.7 0.0 collective-permute-done.3.after
  9.7 0.0 copy-done.3
  9.8 0.0 copy-done.6
  9.8 0.0 copy-start.8
  9.8 0.0 copy-start.9
  9.8 0.9 %shard_map.124 = f32[256,384]{1,0:T(8,128)S(1)} custom-call(f32[2,128,256]{2,1,0:T(8,128)S(1)} %copy-done.6, f32[2,128,256]{2,1,0:T(8,128)S(1)} %copy-done, s32[2,128,256]{2,1,0:T(8,128)S(1)} %copy-done.2, f32[6,8,256]{2,1,0:T(8,128)S(1)} %collective-permute-done.2.edges, f32[1,128,256]{2,1,0:T(8,128)S(1)} %collective-permute-done.3.after, ...), custom_call_target="tpu_custom_call" | custom-call | bytes 4194304 | tf_op jit(solution)/shard_map/pallas_call | solution.py:358
  10.7 0.0 copy-start.4
  10.7 0.0 copy-start.5
  10.7 19.2 %all_to_all.10 = f32[32,8,384]{2,1,0:T(8,128)S(1)} all-to-all(f32[32,8,384]{2,1,0:T(8,128)S(1)} %bitcast.6), channel_id=1, replica_groups=mesh['tm'=16,'band'=2] {'tm','band'}, dimensions={0} | all-to-all | bytes 786432 | tf_op jit(solution)/shard_map/all_to_all | solution.py:435
  29.9 0.0 copy-done.8
  29.9 0.0 copy-done.9
  29.9 0.0 copy-done.4
  29.9 0.0 copy-done.5
  29.9 2.3 %shard_map.125 = f32[800,128]{1,0:T(8,128)} custom-call(f32[16,2,8,384]{3,2,1,0:T(8,128)S(1)} %bitcast.5, bf16[2,256,384]{2,1,0:T(8,128)(2,1)S(1)} %copy-done.5, bf16[2,384,256]{2,1,0:T(8,128)(2,1)S(1)} %copy-done.4, bf16[2,256,256]{2,1,0:T(8,128)(2,1)S(1)} %copy-done.8, f32[8,256]{1,0:T(8,128)S(1)} %copy-done.9), custom_call_target="tpu_custom_call" | custom-call | bytes 4194304 | tf_op jit(solution)/shard_map/pallas_call | solution.py:358
  32.2 2.6 %all-to-all-start.1 = ((f32[32,1,3200]{2,1,0:T(1,128)}), f32[32,1,3200]{2,1,0:T(1,128)S(1)}, u32[]{:S(2)}, u32[]{:S(2)}) async-start(f32[32,1,3200]{2,1,0:T(1,128)} %bitcast.2), calls=%async_computation.1 | async-start | bytes 819200 | tf_op jit(solution)/shard_map/all_to_all | solution.py:442
  34.9 0.0 copy-start.10
  34.9 0.3 collective-permute-start.1
  35.2 0.0 copy-start.7
  35.2 1.5 %collective-permute-start = (f32[1,128,256]{2,1,0:T(8,128)S(1)}, f32[1,128,256]{2,1,0:T(8,128)S(1)}, u32[]{:S(2)}, u32[]{:S(2)}) collective-permute-start(f32[1,128,256]{2,1,0:T(8,128)S(1)} %get-tuple-element.9), channel_id=1, source_target_pairs={{30,0},{31,1},{0,2},{1,3},{2,4},{3,5},{4,6},{5,7},{6,8},{7,9},{8,1... | collective-permute-start | bytes 393224 | tf_op jit(solution)/shard_map/ppermute | solution.py:44
  36.7 5.9 %collective-permute-done.1 = f32[1,128,256]{2,1,0:T(8,128)S(1)} collective-permute-done((f32[1,128,256]{2,1,0:T(8,128)S(1)}, f32[1,128,256]{2,1,0:T(8,128)S(1)}, u32[]{:S(2)}, u32[]{:S(2)}) %collective-permute-start.1) | collective-permute-done | bytes 131104 | tf_op jit(solution)/shard_map/ppermute | solution.py:44
  42.6 0.5 collective-permute-done
  43.0 0.0 copy-done.10
  43.0 0.1 fusion.3.base
  43.1 6.7 %all-to-all-done.1 = f32[32,1,3200]{2,1,0:T(1,128)S(1)} async-done(((f32[32,1,3200]{2,1,0:T(1,128)}), f32[32,1,3200]{2,1,0:T(1,128)S(1)}, u32[]{:S(2)}, u32[]{:S(2)}) %all-to-all-start.1) | async-done | bytes 409632 | tf_op jit(solution)/shard_map/all_to_all | solution.py:442
  49.8 0.0 copy-done.7
  49.8 2.0 %shard_map.126 = (f32[2,128,256]{2,1,0:T(8,128)}, f32[2,128,256]{2,1,0:T(8,128)}) custom-call(f32[2,128,256]{2,1,0:T(8,128)S(1)} %fusion.3.base, f32[2,128,256]{2,1,0:T(8,128)S(1)} %copy-done, s32[2,128,256]{2,1,0:T(8,128)S(1)} %copy-done.2, f32[6,8,256]{2,1,0:T(8,128)S(1)} %collective-permute-done.2.edges, f32[1,128,256]{2,1,0:T(8,128)S(1)} %collective-permute-done.3.after, ...), custom_call_target="tpu_custom_call" | custom-call | bytes 4194304 | tf_op jit(solution)/shard_map/pallas_call | solution.py:358
  (1 shorter events, 0.0 us)
Async XLA Ops:
  0.6 8.3 %copy-start.2 = (s32[2,128,256]{2,1,0:T(8,128)S(1)}, s32[2,128,256]{2,1,0:T(8,128)}, u32[]{:S(2)}) copy-start(s32[2,128,256]{2,1,0:T(8,128)} %bonds.5) | copy-start | bytes 786436
  0.6 8.3 %copy-start = (f32[2,128,256]{2,1,0:T(8,128)S(1)}, f32[2,128,256]{2,1,0:T(8,128)}, u32[]{:S(2)}) copy-start(f32[2,128,256]{2,1,0:T(8,128)} %guess.7) | copy-start | bytes 786436
  0.6 8.3 %copy-start.1 = (f32[2,128,256]{2,1,0:T(8,128)S(1)}, f32[2,128,256]{2,1,0:T(8,128)}, u32[]{:S(2)}) copy-start(f32[2,128,256]{2,1,0:T(8,128)} %phonon.1) | copy-start | bytes 786436
  1.8 8.0 %collective-permute-start.3 = (f32[1,128,256]{2,1,0:T(8,128)S(1)}, f32[1,128,256]{2,1,0:T(8,128)S(1)}, u32[]{:S(2)}, u32[]{:S(2)}) collective-permute-start(f32[1,128,256]{2,1,0:T(8,128)S(1)} %get-tuple-element.11), channel_id=1, source_target_pairs={{2,0},{3,1},{4,2},{5,3},{6,4},{7,5},{8,6},{9,7},{10,8},{11,9},{12,... | collective-permute-start | bytes 393224 | tf_op jit(solution)/shard_map/ppermute | solution.py:44
  1.8 7.9 %collective-permute-start.2 = (f32[6,8,256]{2,1,0:T(8,128)S(1)}, f32[6,8,256]{2,1,0:T(8,128)S(1)}, u32[]{:S(2)}, u32[]{:S(2)}) collective-permute-start(f32[6,8,256]{2,1,0:T(8,128)S(1)} %get-tuple-element.10), channel_id=1, source_target_pairs={{1,0},{0,1},{3,2},{2,3},{5,4},{4,5},{7,6},{6,7},{9,8},{8,9},{11,10... | collective-permute-start | bytes 147464 | tf_op jit(solution)/shard_map/ppermute | solution.py:44
  4.5 5.2 %copy-start.3 = (bf16[2,256,256]{2,1,0:T(8,128)(2,1)S(1)}, bf16[2,256,256]{2,1,0:T(8,128)(2,1)}, u32[]{:S(2)}) copy-start(bf16[2,256,256]{2,1,0:T(8,128)(2,1)} %constant.18.clone.basis) | copy-start | bytes 786436
  4.5 5.2 %copy-start.6 = (f32[2,128,256]{2,1,0:T(8,128)S(1)}, f32[2,128,256]{2,1,0:T(8,128)}, u32[]{:S(2)}) copy-start(f32[2,128,256]{2,1,0:T(8,128)} %source.1) | copy-start | bytes 786436
  4.5 5.2 %collective-permute-start.4 = (f32[1,8,256]{2,1,0:T(8,128)S(1)}, f32[1,8,256]{2,1,0:T(8,128)S(1)}, u32[]{:S(2)}, u32[]{:S(2)}) collective-permute-start(f32[1,8,256]{2,1,0:T(8,128)S(1)} %get-tuple-element.12), channel_id=1, source_target_pairs={{3,0},{2,1},{5,2},{4,3},{7,4},{6,5},{9,6},{8,7},{11,8},{10,9},{13,... | collective-permute-start | bytes 24584 | tf_op jit(solution)/shard_map/ppermute | solution.py:44
  9.8 20.2 %copy-start.8 = (bf16[2,256,256]{2,1,0:T(8,128)(2,1)S(1)}, bf16[2,256,256]{2,1,0:T(8,128)(2,1)}, u32[]{:S(2)}) copy-start(bf16[2,256,256]{2,1,0:T(8,128)(2,1)} %constant.21.clone.rows_in) | copy-start | bytes 786436
  9.8 20.2 %copy-start.9 = (f32[8,256]{1,0:T(8,128)S(1)}, f32[8,256]{1,0:T(8,128)}, u32[]{:S(2)}) copy-start(f32[8,256]{1,0:T(8,128)} %constant.22.clone.rims) | copy-start | bytes 24580
  10.7 19.2 %copy-start.4 = (bf16[2,384,256]{2,1,0:T(8,128)(2,1)S(1)}, bf16[2,384,256]{2,1,0:T(8,128)(2,1)}, u32[]{:S(2)}) copy-start(bf16[2,384,256]{2,1,0:T(8,128)(2,1)} %constant.20.clone.slices_out) | copy-start | bytes 1179652
  10.7 19.2 %copy-start.5 = (bf16[2,256,384]{2,1,0:T(8,128)(2,1)S(1)}, bf16[2,256,384]{2,1,0:T(8,128)(2,1)}, u32[]{:S(2)}) copy-start(bf16[2,256,384]{2,1,0:T(8,128)(2,1)} %constant.19.clone.slices_in) | copy-start | bytes 1179652
  32.2 17.5 %all-to-all-start.1 = ((f32[32,1,3200]{2,1,0:T(1,128)}), f32[32,1,3200]{2,1,0:T(1,128)S(1)}, u32[]{:S(2)}, u32[]{:S(2)}) async-start(f32[32,1,3200]{2,1,0:T(1,128)} %bitcast.2), calls=%async_computation.1 | async-start | bytes 819200 | tf_op jit(solution)/shard_map/all_to_all | solution.py:442
  34.9 8.2 %copy-start.10 = (f32[2,128,256]{2,1,0:T(8,128)S(1)}, f32[2,128,256]{2,1,0:T(8,128)}, u32[]{:S(2)}) copy-start(f32[2,128,256]{2,1,0:T(8,128)} %param.12) | copy-start | bytes 786436
  34.9 7.7 %collective-permute-start.1 = (f32[1,128,256]{2,1,0:T(8,128)S(1)}, f32[1,128,256]{2,1,0:T(8,128)S(1)}, u32[]{:S(2)}, u32[]{:S(2)}) collective-permute-start(f32[1,128,256]{2,1,0:T(8,128)S(1)} %slice.12), channel_id=1, source_target_pairs={{2,0},{3,1},{4,2},{5,3},{6,4},{7,5},{8,6},{9,7},{10,8},{11,9},{12,... | collective-permute-start | bytes 393224 | tf_op jit(solution)/shard_map/ppermute | solution.py:44
  35.2 14.6 %copy-start.7 = (bf16[2,256,256]{2,1,0:T(8,128)(2,1)S(1)}, bf16[2,256,256]{2,1,0:T(8,128)(2,1)}, u32[]{:S(2)}) copy-start(bf16[2,256,256]{2,1,0:T(8,128)(2,1)} %constant.23.clone.order) | copy-start | bytes 786436
  35.2 7.8 %collective-permute-start = (f32[1,128,256]{2,1,0:T(8,128)S(1)}, f32[1,128,256]{2,1,0:T(8,128)S(1)}, u32[]{:S(2)}, u32[]{:S(2)}) collective-permute-start(f32[1,128,256]{2,1,0:T(8,128)S(1)} %get-tuple-element.9), channel_id=1, source_target_pairs={{30,0},{31,1},{0,2},{1,3},{2,4},{3,5},{4,6},{5,7},{6,8},{7,9},{8,1... | collective-permute-start | bytes 393224 | tf_op jit(solution)/shard_map/ppermute | solution.py:44

commit v7 on v6

--- a/solution.py
+++ b/solution.py
@@ -178,7 +178,16 @@
 
 def product(a, b, dims=ROWS_BY_COLS):
     dot = functools.partial(lax.dot_general, dimension_numbers=dims, preferred_element_type=jnp.float32)
-    return dot(a[0], b[0]) + (dot(a[0], b[1]) + dot(a[1], b[0]))
+    high, low = a[0], a[1]
+    rows = high.shape[0]
+    cuts = [0, rows // 2 // (2 * SUBLANES) * (2 * SUBLANES), rows]
+    parts = []
+    for start, stop in zip(cuts, cuts[1:]):
+        if start < stop:
+            both = dot(jnp.concatenate([high[start:stop], low[start:stop]], 0), b[0])
+            small = both[stop - start :] + dot(high[start:stop], b[1])
+            parts.append(both[: stop - start] + small)
+    return jnp.concatenate(parts, 0)
 
 
 def times(a, b):
@@ -258,7 +267,7 @@
             out[:, s * rows : (s + 1) * rows] = waves[:, i * rows : (i + 1) * rows]
 
 
-def mode_kernel(count, mixed, slices_in, slices_out, rows_in, rims, out):
+def mode_kernel(count, mixed, slices_in, slices_out, rows_in, rows_out, out):
     tm, band, modes, width = mixed.shape
     size = tm * modes
     freqs = slices_in.shape[1] // modes
@@ -295,8 +304,9 @@
         gains.append(gain)
     waves = halves(waves * jnp.concatenate(gains, 0))
 
-    back = product(slices_out, halves(product(waves, rows_in, ROWS_BY_ROWS)))
-    edge = product(halves(product(halves(rims[...]), waves, ROWS_BY_ROWS)), slices_in)
+    lines = halves(product(rows_out, waves, ROWS_BY_ROWS))
+    back = product(slices_out, [part[:length] for part in lines], ROWS_BY_ROWS)
+    edge = product([part[length:] for part in lines], slices_out, ROWS_BY_ROWS)[: RIM * band]
     turns = [
         pltpu.roll(edge[:, s * size : (s + 1) * size], RIM * s * modes, 1, stride=modes, stride_axis=0)
         for s in range(slots)
@@ -318,14 +328,13 @@
             out[at + slots * modes : at + chunk] = rim[p : p + 1]
 
 
-def force_kernel(base, guess, bonds, edges, after, after_edge, expo, tables, mixed, basis, order, sol, mom, turned_edge):
-    slices, _, cols = guess.shape
+def force_kernel(base, guess, bonds, edges, after, after_edge, expo, tables, mixed, order, sol, mom, turned_edge):
+    slices, rows, cols = guess.shape
     devices = lax.axis_size("tm") * lax.axis_size("band")
     modes = cols // devices
     slots = slices + 1
     chunk = slots * modes + 1
     band = Band(bonds, edges, expo, tables, slices)
-    columns = (basis[0], basis[1])
 
     rim = mixed[pl.ds(slots * modes, devices, stride=chunk), :]
     lanes = rim.shape[1]
@@ -334,15 +343,18 @@
     turned_edge[...] = rim.T
     groups = lanes // modes
     lines = jnp.concatenate([turned_edge[pl.ds(m, groups, stride=modes), :] for m in range(modes)], 1)
-    strips = product(halves(lines), order)
+    arrived = [
+        jnp.concatenate([mixed[pl.ds(s * modes + m, devices, stride=chunk), :] for m in range(modes)], 0).T
+        for s in range(slots)
+    ]
+    timed = product(halves(jnp.concatenate(arrived + [lines], 0)), order)
+    strips = timed[slots * rows :]
 
     start = with_following(guess, edges, after, after_edge)
     field = []
     for s in range(slots):
-        arrived = [mixed[d * chunk + s * modes : d * chunk + (s + 1) * modes] for d in range(devices)]
-        timed = product(halves(jnp.concatenate(arrived, 0).T), columns)
         strip = pltpu.roll(strips[s * RIM : s * RIM + HALO], HALO - NEAR, 0)
-        change = wide(blocks(timed), blocks(strip))
+        change = wide(blocks(timed[s * rows : (s + 1) * rows]), blocks(strip))
         field.append(each(lambda old, new: old + relaxation * new, start[s], change))
     for s in range(slices):
         own = band.own(field[s])
@@ -414,7 +426,8 @@
     slices_in = np.kron(slot_times, np.eye(modes))
     near = np.concatenate([np.arange(-NEAR, 0), rows + np.arange(NEAR)])
     rim_sites = np.concatenate([(b * rows + near) % length for b in range(band)])
-    rims_basis = np.asarray(space_basis(length, rim_sites).T, np.float32)
+    spare = np.zeros(-len(rim_sites) % (2 * SUBLANES), rim_sites.dtype)
+    rows_out = const_halves(space_basis(length, np.concatenate([np.arange(length), rim_sites, spare])).T)
     rows_in = const_halves(space_basis(length, np.arange(length)).T)
     columns = const_halves(space_basis(cols, np.arange(cols)))
 
@@ -437,7 +450,7 @@
     back = call(
         functools.partial(mode_kernel, cols), on(wave_rows, rows),
         mixed.reshape(tm, band, modes, slots * rows),
-        const_halves(slices_in), const_halves(np.ascontiguousarray(slices_in.T)), rows_in, rims_basis,
+        const_halves(slices_in), const_halves(np.ascontiguousarray(slices_in.T)), rows_in, rows_out,
     )
     mixed = lax.all_to_all(back.reshape(devices, 1, -1), AXES, 0, 0, tiled=True)
 
@@ -450,7 +463,7 @@
     return call(
         force_kernel, (like, like),
         base, guess, bonds, edges, after, after_edge, expo, tables,
-        mixed.reshape(wave_rows, rows), columns,
+        mixed.reshape(wave_rows, rows),
         np.ascontiguousarray(columns.reshape(2, devices, modes, cols).swapaxes(1, 2).reshape(2, cols, cols)),
         scratch_shapes=[pltpu.VMEM((cols // band, devices), jnp.float32)],
     )

time: 52.1 us -> 51.7 us (level)
  no operation moved by 1% of the time
where the time goes in v7:
time: 51.7 us; the launch traced here: 51.5 us
  blocking collectives  19.2 us (37%)
  waiting for transfers between devices  13.4 us (26%)
  starting transfers between devices  11.6 us (22%)
  Pallas kernels  6.41 us (12%)
  between operations  0.77 us (1%)
    all_to_all x1, blocking collectives, shards(): lax.all_to_all(sent.reshape(devices, modes, slots * rows), AXES, 0, 0, ti...  19.2 us
    ppermute x5, starting transfers between devices, shifted(): return lax.ppermute(value, AXES, pairs)  8.97 us
    ppermute x5, waiting for transfers between devices, shifted(): return lax.ppermute(value, AXES, pairs)  6.69 us
    all_to_all x1, waiting for transfers between devices, shards(): mixed = lax.all_to_all(back.reshape(devices, 1, -1), AXES, 0, 0, tiled=True)  6.67 us
    pallas_call x4, Pallas kernels, call(): pl.pallas_call(kernel, out_shape=outs, in_specs=[vmem] * len(operands), o...  5.3 us
    all_to_all x1, starting transfers between devices, shards(): mixed = lax.all_to_all(back.reshape(devices, 1, -1), AXES, 0, 0, tiled=True)  2.61 us
    pallas_call x1, Pallas kernels, pack(): pl.pallas_call(pack_kernel, grid=(1,), out_shape=[pltpu.VMEM(o, jnp.float...  1.1 us
  transfers between devices with their start and end apart: 6, of which 4 were waited for; matrix products, arithmetic and copies ran while one was open for 0% of the time, Pallas kernels for 1%

profile of v7, /device:TPU:1, one launch (start us, length us, event | category | flops | bytes accessed | tf_op | source)
XLA Modules:
  0.0 51.5 jit_solution(651812458319383887)
XLA Ops:
  0.6 0.0 copy-start.2
  0.6 0.0 copy-start
  0.6 0.0 copy-start.1
  0.7 1.1 %shard_map.122 = (f32[1,128,256]{2,1,0:T(8,128)S(1)}, f32[1,128,256]{2,1,0:T(8,128)S(1)}, f32[6,8,256]{2,1,0:T(8,128)S(1)}, f32[1,8,256]{2,1,0:T(8,128)S(1)}) custom-call(f32[2,128,256]{2,1,0:T(8,128)} %guess.7, f32[2,128,256]{2,1,0:T(8,128)} %phonon.1, f32[2,128,256]{2,1,0:T(8,128)} %guess.7, f32[2,128,256]{2,1,0:T(8,128)} %phonon.1, s32[2,128,256]{2,1,0:T(8,128)} %bonds.5, ...), custom_call_target="tpu_custom_call" | custom-call | tf_op jit(solution)/shard_map/pallas_call | solution.py:409
  1.8 0.1 collective-permute-start.3
  1.8 2.7 %collective-permute-start.2 = (f32[6,8,256]{2,1,0:T(8,128)S(1)}, f32[6,8,256]{2,1,0:T(8,128)S(1)}, u32[]{:S(2)}, u32[]{:S(2)}) collective-permute-start(f32[6,8,256]{2,1,0:T(8,128)S(1)} %get-tuple-element.10), channel_id=1, source_target_pairs={{1,0},{0,1},{3,2},{2,3},{5,4},{4,5},{7,6},{6,7},{9,8},{8,9},{11,10... | collective-permute-start | bytes 147464 | tf_op jit(solution)/shard_map/ppermute | solution.py:44
  4.5 0.0 copy-start.6
  4.5 0.0 copy-start.7
  4.5 4.4 %collective-permute-start.4 = (f32[1,8,256]{2,1,0:T(8,128)S(1)}, f32[1,8,256]{2,1,0:T(8,128)S(1)}, u32[]{:S(2)}, u32[]{:S(2)}) collective-permute-start(f32[1,8,256]{2,1,0:T(8,128)S(1)} %get-tuple-element.12), channel_id=1, source_target_pairs={{3,0},{2,1},{5,2},{4,3},{7,4},{6,5},{9,6},{8,7},{11,8},{10,9},{13,... | collective-permute-start | bytes 24584 | tf_op jit(solution)/shard_map/ppermute | solution.py:44
  8.9 0.0 copy-done.2
  8.9 0.0 copy-done
  9.0 0.0 copy-done.1
  9.0 0.4 shard_map.123
  9.4 0.4 collective-permute-done.4.after_edge
  9.7 0.0 collective-permute-done.2.edges
  9.7 0.0 collective-permute-done.3.after
  9.7 0.0 copy-done.6
  9.8 0.0 copy-done.7
  9.8 0.0 copy-start.5
  9.8 0.0 copy-start.9
  9.8 0.9 %shard_map.124 = f32[256,384]{1,0:T(8,128)S(1)} custom-call(f32[2,128,256]{2,1,0:T(8,128)S(1)} %copy-done.6, f32[2,128,256]{2,1,0:T(8,128)S(1)} %copy-done, s32[2,128,256]{2,1,0:T(8,128)S(1)} %copy-done.2, f32[6,8,256]{2,1,0:T(8,128)S(1)} %collective-permute-done.2.edges, f32[1,128,256]{2,1,0:T(8,128)S(1)} %collective-permute-done.3.after, ...), custom_call_target="tpu_custom_call" | custom-call | bytes 4194304 | tf_op jit(solution)/shard_map/pallas_call | solution.py:370
  10.7 0.0 copy-start.3
  10.7 0.0 copy-start.4
  10.7 19.2 %all_to_all.10 = f32[32,8,384]{2,1,0:T(8,128)S(1)} all-to-all(f32[32,8,384]{2,1,0:T(8,128)S(1)} %bitcast.6), channel_id=1, replica_groups=mesh['tm'=16,'band'=2] {'tm','band'}, dimensions={0} | all-to-all | bytes 786432 | tf_op jit(solution)/shard_map/all_to_all | solution.py:448
  30.0 0.0 copy-done.5
  30.0 0.0 copy-done.9
  30.0 0.0 copy-done.3
  30.0 0.0 copy-done.4
  30.0 2.1 %shard_map.125 = f32[800,128]{1,0:T(8,128)} custom-call(f32[16,2,8,384]{3,2,1,0:T(8,128)S(1)} %bitcast.5, bf16[2,256,384]{2,1,0:T(8,128)(2,1)S(1)} %copy-done.4, bf16[2,384,256]{2,1,0:T(8,128)(2,1)S(1)} %copy-done.3, bf16[2,256,256]{2,1,0:T(8,128)(2,1)S(1)} %copy-done.9, bf16[2,272,256]{2,1,0:T(8,128)(2,1)S(1)} %copy-done.5), custom_call_target="tpu_custom_call" | custom-call | bytes 4194304 | tf_op jit(solution)/shard_map/pallas_call | solution.py:370
  32.0 2.6 %all-to-all-start.1 = ((f32[32,1,3200]{2,1,0:T(1,128)}), f32[32,1,3200]{2,1,0:T(1,128)S(1)}, u32[]{:S(2)}, u32[]{:S(2)}) async-start(f32[32,1,3200]{2,1,0:T(1,128)} %bitcast.2), calls=%async_computation.1 | async-start | bytes 819200 | tf_op jit(solution)/shard_map/all_to_all | solution.py:455
  34.7 0.0 copy-start.10
  34.7 0.3 collective-permute-start.1
  35.0 0.0 copy-start.8
  35.0 1.5 %collective-permute-start = (f32[1,128,256]{2,1,0:T(8,128)S(1)}, f32[1,128,256]{2,1,0:T(8,128)S(1)}, u32[]{:S(2)}, u32[]{:S(2)}) collective-permute-start(f32[1,128,256]{2,1,0:T(8,128)S(1)} %get-tuple-element.9), channel_id=1, source_target_pairs={{30,0},{31,1},{0,2},{1,3},{2,4},{3,5},{4,6},{5,7},{6,8},{7,9},{8,1... | collective-permute-start | bytes 393224 | tf_op jit(solution)/shard_map/ppermute | solution.py:44
  36.5 5.9 %collective-permute-done.1 = f32[1,128,256]{2,1,0:T(8,128)S(1)} collective-permute-done((f32[1,128,256]{2,1,0:T(8,128)S(1)}, f32[1,128,256]{2,1,0:T(8,128)S(1)}, u32[]{:S(2)}, u32[]{:S(2)}) %collective-permute-start.1) | collective-permute-done | bytes 131104 | tf_op jit(solution)/shard_map/ppermute | solution.py:44
  42.4 0.5 collective-permute-done
  42.8 0.0 copy-done.10
  42.8 0.1 fusion.3.base
  42.9 6.7 %all-to-all-done.1 = f32[32,1,3200]{2,1,0:T(1,128)S(1)} async-done(((f32[32,1,3200]{2,1,0:T(1,128)}), f32[32,1,3200]{2,1,0:T(1,128)S(1)}, u32[]{:S(2)}, u32[]{:S(2)}) %all-to-all-start.1) | async-done | bytes 409632 | tf_op jit(solution)/shard_map/all_to_all | solution.py:455
  49.6 0.0 copy-done.8
  49.6 1.9 %shard_map.126 = (f32[2,128,256]{2,1,0:T(8,128)}, f32[2,128,256]{2,1,0:T(8,128)}) custom-call(f32[2,128,256]{2,1,0:T(8,128)S(1)} %fusion.3.base, f32[2,128,256]{2,1,0:T(8,128)S(1)} %copy-done, s32[2,128,256]{2,1,0:T(8,128)S(1)} %copy-done.2, f32[6,8,256]{2,1,0:T(8,128)S(1)} %collective-permute-done.2.edges, f32[1,128,256]{2,1,0:T(8,128)S(1)} %collective-permute-done.3.after, ...), custom_call_target="tpu_custom_call" | custom-call | bytes 4194304 | tf_op jit(solution)/shard_map/pallas_call | solution.py:370
  (1 shorter events, 0.0 us)
Async XLA Ops:
  0.6 8.3 %copy-start.2 = (s32[2,128,256]{2,1,0:T(8,128)S(1)}, s32[2,128,256]{2,1,0:T(8,128)}, u32[]{:S(2)}) copy-start(s32[2,128,256]{2,1,0:T(8,128)} %bonds.5) | copy-start | bytes 786436
  0.6 8.3 %copy-start = (f32[2,128,256]{2,1,0:T(8,128)S(1)}, f32[2,128,256]{2,1,0:T(8,128)}, u32[]{:S(2)}) copy-start(f32[2,128,256]{2,1,0:T(8,128)} %guess.7) | copy-start | bytes 786436
  0.6 8.3 %copy-start.1 = (f32[2,128,256]{2,1,0:T(8,128)S(1)}, f32[2,128,256]{2,1,0:T(8,128)}, u32[]{:S(2)}) copy-start(f32[2,128,256]{2,1,0:T(8,128)} %phonon.1) | copy-start | bytes 786436
  1.8 8.0 %collective-permute-start.3 = (f32[1,128,256]{2,1,0:T(8,128)S(1)}, f32[1,128,256]{2,1,0:T(8,128)S(1)}, u32[]{:S(2)}, u32[]{:S(2)}) collective-permute-start(f32[1,128,256]{2,1,0:T(8,128)S(1)} %get-tuple-element.11), channel_id=1, source_target_pairs={{2,0},{3,1},{4,2},{5,3},{6,4},{7,5},{8,6},{9,7},{10,8},{11,9},{12,... | collective-permute-start | bytes 393224 | tf_op jit(solution)/shard_map/ppermute | solution.py:44
  1.8 7.9 %collective-permute-start.2 = (f32[6,8,256]{2,1,0:T(8,128)S(1)}, f32[6,8,256]{2,1,0:T(8,128)S(1)}, u32[]{:S(2)}, u32[]{:S(2)}) collective-permute-start(f32[6,8,256]{2,1,0:T(8,128)S(1)} %get-tuple-element.10), channel_id=1, source_target_pairs={{1,0},{0,1},{3,2},{2,3},{5,4},{4,5},{7,6},{6,7},{9,8},{8,9},{11,10... | collective-permute-start | bytes 147464 | tf_op jit(solution)/shard_map/ppermute | solution.py:44
  4.5 5.2 %copy-start.6 = (f32[2,128,256]{2,1,0:T(8,128)S(1)}, f32[2,128,256]{2,1,0:T(8,128)}, u32[]{:S(2)}) copy-start(f32[2,128,256]{2,1,0:T(8,128)} %source.1) | copy-start | bytes 786436
  4.5 5.2 %copy-start.7 = (bf16[2,256,256]{2,1,0:T(8,128)(2,1)S(1)}, bf16[2,256,256]{2,1,0:T(8,128)(2,1)}, u32[]{:S(2)}) copy-start(bf16[2,256,256]{2,1,0:T(8,128)(2,1)} %constant.18.clone.basis) | copy-start | bytes 786436
  4.5 5.2 %collective-permute-start.4 = (f32[1,8,256]{2,1,0:T(8,128)S(1)}, f32[1,8,256]{2,1,0:T(8,128)S(1)}, u32[]{:S(2)}, u32[]{:S(2)}) collective-permute-start(f32[1,8,256]{2,1,0:T(8,128)S(1)} %get-tuple-element.12), channel_id=1, source_target_pairs={{3,0},{2,1},{5,2},{4,3},{7,4},{6,5},{9,6},{8,7},{11,8},{10,9},{13,... | collective-permute-start | bytes 24584 | tf_op jit(solution)/shard_map/ppermute | solution.py:44
  9.8 20.2 %copy-start.5 = (bf16[2,272,256]{2,1,0:T(8,128)(2,1)S(1)}, bf16[2,272,256]{2,1,0:T(8,128)(2,1)}, u32[]{:S(2)}) copy-start(bf16[2,272,256]{2,1,0:T(8,128)(2,1)} %constant.22.clone.rows_out) | copy-start | bytes 835588
  9.8 20.2 %copy-start.9 = (bf16[2,256,256]{2,1,0:T(8,128)(2,1)S(1)}, bf16[2,256,256]{2,1,0:T(8,128)(2,1)}, u32[]{:S(2)}) copy-start(bf16[2,256,256]{2,1,0:T(8,128)(2,1)} %constant.21.clone.rows_in) | copy-start | bytes 786436
  10.7 19.2 %copy-start.3 = (bf16[2,384,256]{2,1,0:T(8,128)(2,1)S(1)}, bf16[2,384,256]{2,1,0:T(8,128)(2,1)}, u32[]{:S(2)}) copy-start(bf16[2,384,256]{2,1,0:T(8,128)(2,1)} %constant.20.clone.slices_out) | copy-start | bytes 1179652
  10.7 19.2 %copy-start.4 = (bf16[2,256,384]{2,1,0:T(8,128)(2,1)S(1)}, bf16[2,256,384]{2,1,0:T(8,128)(2,1)}, u32[]{:S(2)}) copy-start(bf16[2,256,384]{2,1,0:T(8,128)(2,1)} %constant.19.clone.slices_in) | copy-start | bytes 1179652
  32.0 17.5 %all-to-all-start.1 = ((f32[32,1,3200]{2,1,0:T(1,128)}), f32[32,1,3200]{2,1,0:T(1,128)S(1)}, u32[]{:S(2)}, u32[]{:S(2)}) async-start(f32[32,1,3200]{2,1,0:T(1,128)} %bitcast.2), calls=%async_computation.1 | async-start | bytes 819200 | tf_op jit(solution)/shard_map/all_to_all | solution.py:455
  34.7 8.2 %copy-start.10 = (f32[2,128,256]{2,1,0:T(8,128)S(1)}, f32[2,128,256]{2,1,0:T(8,128)}, u32[]{:S(2)}) copy-start(f32[2,128,256]{2,1,0:T(8,128)} %param.12) | copy-start | bytes 786436
  34.7 7.7 %collective-permute-start.1 = (f32[1,128,256]{2,1,0:T(8,128)S(1)}, f32[1,128,256]{2,1,0:T(8,128)S(1)}, u32[]{:S(2)}, u32[]{:S(2)}) collective-permute-start(f32[1,128,256]{2,1,0:T(8,128)S(1)} %slice.12), channel_id=1, source_target_pairs={{2,0},{3,1},{4,2},{5,3},{6,4},{7,5},{8,6},{9,7},{10,8},{11,9},{12,... | collective-permute-start | bytes 393224 | tf_op jit(solution)/shard_map/ppermute | solution.py:44
  35.0 14.6 %copy-start.8 = (bf16[2,256,256]{2,1,0:T(8,128)(2,1)S(1)}, bf16[2,256,256]{2,1,0:T(8,128)(2,1)}, u32[]{:S(2)}) copy-start(bf16[2,256,256]{2,1,0:T(8,128)(2,1)} %constant.23.clone.order) | copy-start | bytes 786436
  35.0 7.8 %collective-permute-start = (f32[1,128,256]{2,1,0:T(8,128)S(1)}, f32[1,128,256]{2,1,0:T(8,128)S(1)}, u32[]{:S(2)}, u32[]{:S(2)}) collective-permute-start(f32[1,128,256]{2,1,0:T(8,128)S(1)} %get-tuple-element.9), channel_id=1, source_target_pairs={{30,0},{31,1},{0,2},{1,3},{2,4},{3,5},{4,6},{5,7},{6,8},{7,9},{8,1... | collective-permute-start | bytes 393224 | tf_op jit(solution)/shard_map/ppermute | solution.py:44

commit v8 on v7

--- a/solution.py
+++ b/solution.py
@@ -30,6 +30,7 @@
 NEAR = 2
 RIM = 2 * NEAR
 AXES = ("tm", "band")
+EXCHANGE = ("band", "tm")
 ROWS_BY_COLS = (((1,), (0,)), ((), ()))
 ROWS_BY_ROWS = (((1,), (1,)), ((), ()))
 
@@ -176,11 +177,11 @@
     return np.stack([high, low])
 
 
-def product(a, b, dims=ROWS_BY_COLS):
+def product(a, b, dims=ROWS_BY_COLS, cuts=None):
     dot = functools.partial(lax.dot_general, dimension_numbers=dims, preferred_element_type=jnp.float32)
     high, low = a[0], a[1]
     rows = high.shape[0]
-    cuts = [0, rows // 2 // (2 * SUBLANES) * (2 * SUBLANES), rows]
+    cuts = cuts or [0, rows // 2 // (2 * SUBLANES) * (2 * SUBLANES), rows]
     parts = []
     for start, stop in zip(cuts, cuts[1:]):
         if start < stop:
@@ -248,7 +249,7 @@
 
 
 def residual_kernel(source, guess, bonds, edges, after, after_edge, expo, tables, inner, basis, out):
-    slices, rows, _ = guess.shape
+    slices, rows, cols = guess.shape
     band = Band(bonds, edges, expo, tables, slices)
     field = with_following(guess, edges, after, after_edge)
     pieces = []
@@ -262,13 +263,13 @@
     pieces.insert(1, joined(band.own(applied)))
     places = [0, slices] + list(range(1, slices))
     for group in (slice(0, 2), slice(2, None)):
-        waves = product(basis, halves(jnp.concatenate(pieces[group], 0)), ROWS_BY_ROWS)
+        waves = product(basis, halves(jnp.concatenate(pieces[group], 0)), ROWS_BY_ROWS, cuts=[0, cols])
         for i, s in enumerate(places[group]):
             out[:, s * rows : (s + 1) * rows] = waves[:, i * rows : (i + 1) * rows]
 
 
 def mode_kernel(count, mixed, slices_in, slices_out, rows_in, rows_out, out):
-    tm, band, modes, width = mixed.shape
+    band, tm, modes, width = mixed.shape
     size = tm * modes
     freqs = slices_in.shape[1] // modes
     length = rows_in.shape[1]
@@ -279,7 +280,7 @@
     stacked = jnp.concatenate(
         [
             jnp.concatenate(
-                [mixed[:, b, :, s * per : (s + 1) * per].reshape(size, per) for b in range(band)], 1
+                [mixed[b, :, :, s * per : (s + 1) * per].reshape(size, per) for b in range(band)], 1
             )
             for s in range(slots)
         ],
@@ -287,7 +288,7 @@
     )
     waves = product(halves(product(slices_in, halves(stacked))), rows_in)
 
-    place = lax.axis_index("tm") * band + lax.axis_index("band")
+    place = lax.axis_index("band") * tm + lax.axis_index("tm")
     shape = (modes, length)
     column = place * modes + lax.broadcasted_iota(jnp.int32, shape, 0)
     row = lax.broadcasted_iota(jnp.int32, shape, 1)
@@ -321,7 +322,7 @@
                 line = turns[s][b * RIM + q : b * RIM + q + 1]
                 rim = jnp.where(slot == (RIM * (s + b) + q) % tm, line, rim)
         for p in range(tm):
-            at = (p * band + b) * chunk
+            at = (b * tm + p) * chunk
             for s in range(slots):
                 start = s * size + p * modes
                 out[at + s * modes : at + (s + 1) * modes] = back[start : start + modes, b * per : (b + 1) * per]
@@ -347,8 +348,9 @@
         jnp.concatenate([mixed[pl.ds(s * modes + m, devices, stride=chunk), :] for m in range(modes)], 0).T
         for s in range(slots)
     ]
-    timed = product(halves(jnp.concatenate(arrived + [lines], 0)), order)
-    strips = timed[slots * rows :]
+    first = lines.shape[0]
+    timed = product(halves(jnp.concatenate([lines] + arrived, 0)), order, cuts=[0] + [first + s * rows for s in range(1, slots + 1)])
+    strips, timed = timed[:first], timed[first:]
 
     start = with_following(guess, edges, after, after_edge)
     field = []
@@ -445,14 +447,14 @@
         residual_kernel, jax.ShapeDtypeStruct((cols, slots * rows), jnp.float32),
         source, guess, bonds, edges, after, after_edge, expo, tables, inner, columns,
     )
-    mixed = lax.all_to_all(sent.reshape(devices, modes, slots * rows), AXES, 0, 0, tiled=True)
+    mixed = lax.all_to_all(sent.reshape(devices, modes, slots * rows), EXCHANGE, 0, 0, tiled=True)
     wave_rows = devices * (slots * modes + 1)
     back = call(
         functools.partial(mode_kernel, cols), on(wave_rows, rows),
-        mixed.reshape(tm, band, modes, slots * rows),
+        mixed.reshape(band, tm, modes, slots * rows),
         const_halves(slices_in), const_halves(np.ascontiguousarray(slices_in.T)), rows_in, rows_out,
     )
-    mixed = lax.all_to_all(back.reshape(devices, 1, -1), AXES, 0, 0, tiled=True)
+    mixed = lax.all_to_all(back.reshape(devices, 1, -1), EXCHANGE, 0, 0, tiled=True)
 
     after_ph = shifted(phonon[:1], 1, 0)
     before_ph = shifted(last, -1, 0)

time: 51.7 us -> 51.2 us (level)
  waiting for transfers between devices: 13.4 us -> 12.8 us
  blocking collectives: 19.2 us -> 18.6 us
    ppermute x5, waiting for transfers between devices: 6.69 us -> 5.36 us  [shifted(): return lax.ppermute(value, AXES, pairs)]
    all_to_all x1, waiting for transfers between devices: 6.67 us -> 7.48 us  [shards(): lax.all_to_all(back.reshape(devices, 1, -1), EXCHANGE, 0, 0, tiled=True)]
    all_to_all x1, blocking collectives: 19.2 us -> 18.6 us  [shards(): lax.all_to_all(sent.reshape(devices, modes, slots * rows), EXCHANGE, 0, 0...]
where the time goes in v8:
time: 51.2 us; the launch traced here: 50.7 us
  blocking collectives  18.6 us (36%)
  waiting for transfers between devices  12.8 us (25%)
  starting transfers between devices  11.9 us (23%)
  Pallas kernels  6.39 us (12%)
  between operations  0.77 us (2%)
    all_to_all x1, blocking collectives, shards(): lax.all_to_all(sent.reshape(devices, modes, slots * rows), EXCHANGE, 0, 0...  18.6 us
    ppermute x5, starting transfers between devices, shifted(): return lax.ppermute(value, AXES, pairs)  8.97 us
    all_to_all x1, waiting for transfers between devices, shards(): lax.all_to_all(back.reshape(devices, 1, -1), EXCHANGE, 0, 0, tiled=True)  7.48 us
    ppermute x5, waiting for transfers between devices, shifted(): return lax.ppermute(value, AXES, pairs)  5.36 us
    pallas_call x4, Pallas kernels, call(): pl.pallas_call(kernel, out_shape=outs, in_specs=[vmem] * len(operands), o...  5.28 us
    all_to_all x1, starting transfers between devices, shards(): lax.all_to_all(back.reshape(devices, 1, -1), EXCHANGE, 0, 0, tiled=True)  2.97 us
    pallas_call x1, Pallas kernels, pack(): pl.pallas_call(pack_kernel, grid=(1,), out_shape=[pltpu.VMEM(o, jnp.float...  1.1 us
  transfers between devices with their start and end apart: 6, of which 4 were waited for; matrix products, arithmetic and copies ran while one was open for 0% of the time, Pallas kernels for 1%

profile of v8, /device:TPU:1, one launch (start us, length us, event | category | flops | bytes accessed | tf_op | source)
XLA Modules:
  0.0 50.7 jit_solution(11412968191016674574)
XLA Ops:
  0.6 0.0 copy-start.2
  0.6 0.0 copy-start
  0.6 0.0 copy-start.1
  0.7 1.1 %shard_map.122 = (f32[1,128,256]{2,1,0:T(8,128)S(1)}, f32[1,128,256]{2,1,0:T(8,128)S(1)}, f32[6,8,256]{2,1,0:T(8,128)S(1)}, f32[1,8,256]{2,1,0:T(8,128)S(1)}) custom-call(f32[2,128,256]{2,1,0:T(8,128)} %guess.7, f32[2,128,256]{2,1,0:T(8,128)} %phonon.1, f32[2,128,256]{2,1,0:T(8,128)} %guess.7, f32[2,128,256]{2,1,0:T(8,128)} %phonon.1, s32[2,128,256]{2,1,0:T(8,128)} %bonds.5, ...), custom_call_target="tpu_custom_call" | custom-call | tf_op jit(solution)/shard_map/pallas_call | solution.py:411
  1.8 0.1 collective-permute-start.3
  1.8 2.7 %collective-permute-start.2 = (f32[6,8,256]{2,1,0:T(8,128)S(1)}, f32[6,8,256]{2,1,0:T(8,128)S(1)}, u32[]{:S(2)}, u32[]{:S(2)}) collective-permute-start(f32[6,8,256]{2,1,0:T(8,128)S(1)} %get-tuple-element.10), channel_id=1, source_target_pairs={{1,0},{0,1},{3,2},{2,3},{5,4},{4,5},{7,6},{6,7},{9,8},{8,9},{11,10... | collective-permute-start | bytes 147464 | tf_op jit(solution)/shard_map/ppermute | solution.py:45
  4.5 0.0 copy-start.6
  4.5 0.0 copy-start.7
  4.5 4.4 %collective-permute-start.4 = (f32[1,8,256]{2,1,0:T(8,128)S(1)}, f32[1,8,256]{2,1,0:T(8,128)S(1)}, u32[]{:S(2)}, u32[]{:S(2)}) collective-permute-start(f32[1,8,256]{2,1,0:T(8,128)S(1)} %get-tuple-element.12), channel_id=1, source_target_pairs={{3,0},{2,1},{5,2},{4,3},{7,4},{6,5},{9,6},{8,7},{11,8},{10,9},{13,... | collective-permute-start | bytes 24584 | tf_op jit(solution)/shard_map/ppermute | solution.py:45
  8.9 0.0 copy-done.2
  8.9 0.0 copy-done
  9.0 0.0 copy-done.1
  9.0 0.4 shard_map.123
  9.4 0.4 collective-permute-done.4.after_edge
  9.7 0.0 collective-permute-done.2.edges
  9.7 0.0 collective-permute-done.3.after
  9.7 0.0 copy-done.6
  9.8 0.0 copy-done.7
  9.8 0.0 copy-start.5
  9.8 0.0 copy-start.9
  9.8 0.9 %shard_map.124 = f32[256,384]{1,0:T(8,128)S(1)} custom-call(f32[2,128,256]{2,1,0:T(8,128)S(1)} %copy-done.6, f32[2,128,256]{2,1,0:T(8,128)S(1)} %copy-done, s32[2,128,256]{2,1,0:T(8,128)S(1)} %copy-done.2, f32[6,8,256]{2,1,0:T(8,128)S(1)} %collective-permute-done.2.edges, f32[1,128,256]{2,1,0:T(8,128)S(1)} %collective-permute-done.3.after, ...), custom_call_target="tpu_custom_call" | custom-call | bytes 4194304 | tf_op jit(solution)/shard_map/pallas_call | solution.py:372
  10.7 0.0 copy-start.3
  10.7 0.0 copy-start.4
  10.7 18.6 %all_to_all.10 = f32[32,8,384]{2,1,0:T(8,128)S(1)} all-to-all(f32[32,8,384]{2,1,0:T(8,128)S(1)} %bitcast.6), channel_id=1, replica_groups=mesh['tm'=16,'band'=2] {'band','tm'}, dimensions={0} | all-to-all | bytes 786432 | tf_op jit(solution)/shard_map/all_to_all | solution.py:450
  29.3 0.0 copy-done.5
  29.3 0.0 copy-done.9
  29.3 0.0 copy-done.3
  29.3 0.0 copy-done.4
  29.3 2.1 %shard_map.125 = f32[800,128]{1,0:T(8,128)} custom-call(f32[2,16,8,384]{3,2,1,0:T(8,128)S(1)} %bitcast.5, bf16[2,256,384]{2,1,0:T(8,128)(2,1)S(1)} %copy-done.4, bf16[2,384,256]{2,1,0:T(8,128)(2,1)S(1)} %copy-done.3, bf16[2,256,256]{2,1,0:T(8,128)(2,1)S(1)} %copy-done.9, bf16[2,272,256]{2,1,0:T(8,128)(2,1)S(1)} %copy-done.5), custom_call_target="tpu_custom_call" | custom-call | bytes 4194304 | tf_op jit(solution)/shard_map/pallas_call | solution.py:372
  31.4 3.0 %all-to-all-start.1 = ((f32[32,1,3200]{2,1,0:T(1,128)}), f32[32,1,3200]{2,1,0:T(1,128)S(1)}, u32[]{:S(2)}, u32[]{:S(2)}) async-start(f32[32,1,3200]{2,1,0:T(1,128)} %bitcast.2), calls=%async_computation.1 | async-start | bytes 819200 | tf_op jit(solution)/shard_map/all_to_all | solution.py:457
  34.4 0.0 copy-start.10
  34.4 0.5 collective-permute-start.1
  34.9 0.0 copy-start.8
  34.9 1.3 %collective-permute-start = (f32[1,128,256]{2,1,0:T(8,128)S(1)}, f32[1,128,256]{2,1,0:T(8,128)S(1)}, u32[]{:S(2)}, u32[]{:S(2)}) collective-permute-start(f32[1,128,256]{2,1,0:T(8,128)S(1)} %get-tuple-element.9), channel_id=1, source_target_pairs={{30,0},{31,1},{0,2},{1,3},{2,4},{3,5},{4,6},{5,7},{6,8},{7,9},{8,1... | collective-permute-start | bytes 393224 | tf_op jit(solution)/shard_map/ppermute | solution.py:45
  36.2 4.9 %collective-permute-done.1 = f32[1,128,256]{2,1,0:T(8,128)S(1)} collective-permute-done((f32[1,128,256]{2,1,0:T(8,128)S(1)}, f32[1,128,256]{2,1,0:T(8,128)S(1)}, u32[]{:S(2)}, u32[]{:S(2)}) %collective-permute-start.1) | collective-permute-done | bytes 131104 | tf_op jit(solution)/shard_map/ppermute | solution.py:45
  41.1 0.1 collective-permute-done
  41.2 0.0 copy-done.10
  41.2 0.1 fusion.3.base
  41.3 7.5 %all-to-all-done.1 = f32[32,1,3200]{2,1,0:T(1,128)S(1)} async-done(((f32[32,1,3200]{2,1,0:T(1,128)}), f32[32,1,3200]{2,1,0:T(1,128)S(1)}, u32[]{:S(2)}, u32[]{:S(2)}) %all-to-all-start.1) | async-done | bytes 409632 | tf_op jit(solution)/shard_map/all_to_all | solution.py:457
  48.8 0.0 copy-done.8
  48.8 1.9 %shard_map.126 = (f32[2,128,256]{2,1,0:T(8,128)}, f32[2,128,256]{2,1,0:T(8,128)}) custom-call(f32[2,128,256]{2,1,0:T(8,128)S(1)} %fusion.3.base, f32[2,128,256]{2,1,0:T(8,128)S(1)} %copy-done, s32[2,128,256]{2,1,0:T(8,128)S(1)} %copy-done.2, f32[6,8,256]{2,1,0:T(8,128)S(1)} %collective-permute-done.2.edges, f32[1,128,256]{2,1,0:T(8,128)S(1)} %collective-permute-done.3.after, ...), custom_call_target="tpu_custom_call" | custom-call | bytes 4194304 | tf_op jit(solution)/shard_map/pallas_call | solution.py:372
  (1 shorter events, 0.0 us)
Async XLA Ops:
  0.6 8.3 %copy-start.2 = (s32[2,128,256]{2,1,0:T(8,128)S(1)}, s32[2,128,256]{2,1,0:T(8,128)}, u32[]{:S(2)}) copy-start(s32[2,128,256]{2,1,0:T(8,128)} %bonds.5) | copy-start | bytes 786436
  0.6 8.3 %copy-start = (f32[2,128,256]{2,1,0:T(8,128)S(1)}, f32[2,128,256]{2,1,0:T(8,128)}, u32[]{:S(2)}) copy-start(f32[2,128,256]{2,1,0:T(8,128)} %guess.7) | copy-start | bytes 786436
  0.6 8.3 %copy-start.1 = (f32[2,128,256]{2,1,0:T(8,128)S(1)}, f32[2,128,256]{2,1,0:T(8,128)}, u32[]{:S(2)}) copy-start(f32[2,128,256]{2,1,0:T(8,128)} %phonon.1) | copy-start | bytes 786436
  1.8 8.0 %collective-permute-start.3 = (f32[1,128,256]{2,1,0:T(8,128)S(1)}, f32[1,128,256]{2,1,0:T(8,128)S(1)}, u32[]{:S(2)}, u32[]{:S(2)}) collective-permute-start(f32[1,128,256]{2,1,0:T(8,128)S(1)} %get-tuple-element.11), channel_id=1, source_target_pairs={{2,0},{3,1},{4,2},{5,3},{6,4},{7,5},{8,6},{9,7},{10,8},{11,9},{12,... | collective-permute-start | bytes 393224 | tf_op jit(solution)/shard_map/ppermute | solution.py:45
  1.8 7.9 %collective-permute-start.2 = (f32[6,8,256]{2,1,0:T(8,128)S(1)}, f32[6,8,256]{2,1,0:T(8,128)S(1)}, u32[]{:S(2)}, u32[]{:S(2)}) collective-permute-start(f32[6,8,256]{2,1,0:T(8,128)S(1)} %get-tuple-element.10), channel_id=1, source_target_pairs={{1,0},{0,1},{3,2},{2,3},{5,4},{4,5},{7,6},{6,7},{9,8},{8,9},{11,10... | collective-permute-start | bytes 147464 | tf_op jit(solution)/shard_map/ppermute | solution.py:45
  4.5 5.2 %copy-start.6 = (f32[2,128,256]{2,1,0:T(8,128)S(1)}, f32[2,128,256]{2,1,0:T(8,128)}, u32[]{:S(2)}) copy-start(f32[2,128,256]{2,1,0:T(8,128)} %source.1) | copy-start | bytes 786436
  4.5 5.2 %copy-start.7 = (bf16[2,256,256]{2,1,0:T(8,128)(2,1)S(1)}, bf16[2,256,256]{2,1,0:T(8,128)(2,1)}, u32[]{:S(2)}) copy-start(bf16[2,256,256]{2,1,0:T(8,128)(2,1)} %constant.18.clone.basis) | copy-start | bytes 786436
  4.5 5.2 %collective-permute-start.4 = (f32[1,8,256]{2,1,0:T(8,128)S(1)}, f32[1,8,256]{2,1,0:T(8,128)S(1)}, u32[]{:S(2)}, u32[]{:S(2)}) collective-permute-start(f32[1,8,256]{2,1,0:T(8,128)S(1)} %get-tuple-element.12), channel_id=1, source_target_pairs={{3,0},{2,1},{5,2},{4,3},{7,4},{6,5},{9,6},{8,7},{11,8},{10,9},{13,... | collective-permute-start | bytes 24584 | tf_op jit(solution)/shard_map/ppermute | solution.py:45
  9.8 19.6 %copy-start.5 = (bf16[2,272,256]{2,1,0:T(8,128)(2,1)S(1)}, bf16[2,272,256]{2,1,0:T(8,128)(2,1)}, u32[]{:S(2)}) copy-start(bf16[2,272,256]{2,1,0:T(8,128)(2,1)} %constant.22.clone.rows_out) | copy-start | bytes 835588
  9.8 19.5 %copy-start.9 = (bf16[2,256,256]{2,1,0:T(8,128)(2,1)S(1)}, bf16[2,256,256]{2,1,0:T(8,128)(2,1)}, u32[]{:S(2)}) copy-start(bf16[2,256,256]{2,1,0:T(8,128)(2,1)} %constant.21.clone.rows_in) | copy-start | bytes 786436
  10.7 18.6 %copy-start.3 = (bf16[2,384,256]{2,1,0:T(8,128)(2,1)S(1)}, bf16[2,384,256]{2,1,0:T(8,128)(2,1)}, u32[]{:S(2)}) copy-start(bf16[2,384,256]{2,1,0:T(8,128)(2,1)} %constant.20.clone.slices_out) | copy-start | bytes 1179652
  10.7 18.6 %copy-start.4 = (bf16[2,256,384]{2,1,0:T(8,128)(2,1)S(1)}, bf16[2,256,384]{2,1,0:T(8,128)(2,1)}, u32[]{:S(2)}) copy-start(bf16[2,256,384]{2,1,0:T(8,128)(2,1)} %constant.19.clone.slices_in) | copy-start | bytes 1179652
  31.4 17.4 %all-to-all-start.1 = ((f32[32,1,3200]{2,1,0:T(1,128)}), f32[32,1,3200]{2,1,0:T(1,128)S(1)}, u32[]{:S(2)}, u32[]{:S(2)}) async-start(f32[32,1,3200]{2,1,0:T(1,128)} %bitcast.2), calls=%async_computation.1 | async-start | bytes 819200 | tf_op jit(solution)/shard_map/all_to_all | solution.py:457
  34.4 6.8 %copy-start.10 = (f32[2,128,256]{2,1,0:T(8,128)S(1)}, f32[2,128,256]{2,1,0:T(8,128)}, u32[]{:S(2)}) copy-start(f32[2,128,256]{2,1,0:T(8,128)} %param.12) | copy-start | bytes 786436
  34.4 6.7 %collective-permute-start.1 = (f32[1,128,256]{2,1,0:T(8,128)S(1)}, f32[1,128,256]{2,1,0:T(8,128)S(1)}, u32[]{:S(2)}, u32[]{:S(2)}) collective-permute-start(f32[1,128,256]{2,1,0:T(8,128)S(1)} %slice.12), channel_id=1, source_target_pairs={{2,0},{3,1},{4,2},{5,3},{6,4},{7,5},{8,6},{9,7},{10,8},{11,9},{12,... | collective-permute-start | bytes 393224 | tf_op jit(solution)/shard_map/ppermute | solution.py:45
  34.9 13.9 %copy-start.8 = (bf16[2,256,256]{2,1,0:T(8,128)(2,1)S(1)}, bf16[2,256,256]{2,1,0:T(8,128)(2,1)}, u32[]{:S(2)}) copy-start(bf16[2,256,256]{2,1,0:T(8,128)(2,1)} %constant.23.clone.order) | copy-start | bytes 786436
  34.9 6.3 %collective-permute-start = (f32[1,128,256]{2,1,0:T(8,128)S(1)}, f32[1,128,256]{2,1,0:T(8,128)S(1)}, u32[]{:S(2)}, u32[]{:S(2)}) collective-permute-start(f32[1,128,256]{2,1,0:T(8,128)S(1)} %get-tuple-element.9), channel_id=1, source_target_pairs={{30,0},{31,1},{0,2},{1,3},{2,4},{3,5},{4,6},{5,7},{6,8},{7,9},{8,1... | collective-permute-start | bytes 393224 | tf_op jit(solution)/shard_map/ppermute | solution.py:45

commit v9 on v8

--- a/solution.py
+++ b/solution.py
@@ -322,7 +322,7 @@
                 line = turns[s][b * RIM + q : b * RIM + q + 1]
                 rim = jnp.where(slot == (RIM * (s + b) + q) % tm, line, rim)
         for p in range(tm):
-            at = (b * tm + p) * chunk
+            at = (p * band + b) * chunk
             for s in range(slots):
                 start = s * size + p * modes
                 out[at + s * modes : at + (s + 1) * modes] = back[start : start + modes, b * per : (b + 1) * per]
@@ -454,7 +454,7 @@
         mixed.reshape(band, tm, modes, slots * rows),
         const_halves(slices_in), const_halves(np.ascontiguousarray(slices_in.T)), rows_in, rows_out,
     )
-    mixed = lax.all_to_all(back.reshape(devices, 1, -1), EXCHANGE, 0, 0, tiled=True)
+    mixed = lax.all_to_all(back.reshape(devices, 1, -1), AXES, 0, 0, tiled=True)
 
     after_ph = shifted(phonon[:1], 1, 0)
     before_ph = shifted(last, -1, 0)
@@ -466,7 +466,7 @@
         force_kernel, (like, like),
         base, guess, bonds, edges, after, after_edge, expo, tables,
         mixed.reshape(wave_rows, rows),
-        np.ascontiguousarray(columns.reshape(2, devices, modes, cols).swapaxes(1, 2).reshape(2, cols, cols)),
+        np.ascontiguousarray(columns.reshape(2, band, tm, modes, cols).swapaxes(1, 2).reshape(2, devices, modes, cols).swapaxes(1, 2).reshape(2, cols, cols)),
         scratch_shapes=[pltpu.VMEM((cols // band, devices), jnp.float32)],
     )
 

time: 51.2 us -> 51.6 us (level)
  waiting for transfers between devices: 12.8 us -> 13.5 us
    ppermute x5, waiting for transfers between devices: 5.36 us -> 6.69 us  [shifted(): return lax.ppermute(value, AXES, pairs)]
    all_to_all x1, waiting for transfers between devices: 7.48 us -> 6.81 us  [shards(): mixed = lax.all_to_all(back.reshape(devices, 1, -1), AXES, 0, 0, tiled=True)]
where the time goes in v9:
time: 51.6 us; the launch traced here: 51.3 us
  blocking collectives  18.6 us (36%)
  waiting for transfers between devices  13.5 us (26%)
  starting transfers between devices  11.9 us (23%)
  Pallas kernels  6.38 us (12%)
  between operations  0.77 us (1%)
    all_to_all x1, blocking collectives, shards(): lax.all_to_all(sent.reshape(devices, modes, slots * rows), EXCHANGE, 0, 0...  18.6 us
    ppermute x5, starting transfers between devices, shifted(): return lax.ppermute(value, AXES, pairs)  8.97 us
    all_to_all x1, waiting for transfers between devices, shards(): mixed = lax.all_to_all(back.reshape(devices, 1, -1), AXES, 0, 0, tiled=True)  6.81 us
    ppermute x5, waiting for transfers between devices, shifted(): return lax.ppermute(value, AXES, pairs)  6.69 us
    pallas_call x4, Pallas kernels, call(): pl.pallas_call(kernel, out_shape=outs, in_specs=[vmem] * len(operands), o...  5.28 us
    all_to_all x1, starting transfers between devices, shards(): mixed = lax.all_to_all(back.reshape(devices, 1, -1), AXES, 0, 0, tiled=True)  2.97 us
    pallas_call x1, Pallas kernels, pack(): pl.pallas_call(pack_kernel, grid=(1,), out_shape=[pltpu.VMEM(o, jnp.float...  1.1 us
  transfers between devices with their start and end apart: 6, of which 4 were waited for; matrix products, arithmetic and copies ran while one was open for 0% of the time, Pallas kernels for 1%

profile of v9, /device:TPU:1, one launch (start us, length us, event | category | flops | bytes accessed | tf_op | source)
XLA Modules:
  0.0 51.3 jit_solution(8491169180354889191)
XLA Ops:
  0.6 0.0 copy-start.2
  0.6 0.0 copy-start
  0.6 0.0 copy-start.1
  0.7 1.1 %shard_map.122 = (f32[1,128,256]{2,1,0:T(8,128)S(1)}, f32[1,128,256]{2,1,0:T(8,128)S(1)}, f32[6,8,256]{2,1,0:T(8,128)S(1)}, f32[1,8,256]{2,1,0:T(8,128)S(1)}) custom-call(f32[2,128,256]{2,1,0:T(8,128)} %guess.7, f32[2,128,256]{2,1,0:T(8,128)} %phonon.1, f32[2,128,256]{2,1,0:T(8,128)} %guess.7, f32[2,128,256]{2,1,0:T(8,128)} %phonon.1, s32[2,128,256]{2,1,0:T(8,128)} %bonds.5, ...), custom_call_target="tpu_custom_call" | custom-call | tf_op jit(solution)/shard_map/pallas_call | solution.py:411
  1.8 0.1 collective-permute-start.3
  1.8 2.7 %collective-permute-start.2 = (f32[6,8,256]{2,1,0:T(8,128)S(1)}, f32[6,8,256]{2,1,0:T(8,128)S(1)}, u32[]{:S(2)}, u32[]{:S(2)}) collective-permute-start(f32[6,8,256]{2,1,0:T(8,128)S(1)} %get-tuple-element.10), channel_id=1, source_target_pairs={{1,0},{0,1},{3,2},{2,3},{5,4},{4,5},{7,6},{6,7},{9,8},{8,9},{11,10... | collective-permute-start | bytes 147464 | tf_op jit(solution)/shard_map/ppermute | solution.py:45
  4.5 0.0 copy-start.6
  4.5 0.0 copy-start.7
  4.5 4.4 %collective-permute-start.4 = (f32[1,8,256]{2,1,0:T(8,128)S(1)}, f32[1,8,256]{2,1,0:T(8,128)S(1)}, u32[]{:S(2)}, u32[]{:S(2)}) collective-permute-start(f32[1,8,256]{2,1,0:T(8,128)S(1)} %get-tuple-element.12), channel_id=1, source_target_pairs={{3,0},{2,1},{5,2},{4,3},{7,4},{6,5},{9,6},{8,7},{11,8},{10,9},{13,... | collective-permute-start | bytes 24584 | tf_op jit(solution)/shard_map/ppermute | solution.py:45
  8.9 0.0 copy-done.2
  8.9 0.0 copy-done
  9.0 0.0 copy-done.1
  9.0 0.4 shard_map.123
  9.4 0.4 collective-permute-done.4.after_edge
  9.7 0.0 collective-permute-done.2.edges
  9.7 0.0 collective-permute-done.3.after
  9.7 0.0 copy-done.6
  9.8 0.0 copy-done.7
  9.8 0.0 copy-start.5
  9.8 0.0 copy-start.9
  9.8 0.9 %shard_map.124 = f32[256,384]{1,0:T(8,128)S(1)} custom-call(f32[2,128,256]{2,1,0:T(8,128)S(1)} %copy-done.6, f32[2,128,256]{2,1,0:T(8,128)S(1)} %copy-done, s32[2,128,256]{2,1,0:T(8,128)S(1)} %copy-done.2, f32[6,8,256]{2,1,0:T(8,128)S(1)} %collective-permute-done.2.edges, f32[1,128,256]{2,1,0:T(8,128)S(1)} %collective-permute-done.3.after, ...), custom_call_target="tpu_custom_call" | custom-call | bytes 4194304 | tf_op jit(solution)/shard_map/pallas_call | solution.py:372
  10.7 0.0 copy-start.3
  10.7 0.0 copy-start.4
  10.7 18.6 %all_to_all.10 = f32[32,8,384]{2,1,0:T(8,128)S(1)} all-to-all(f32[32,8,384]{2,1,0:T(8,128)S(1)} %bitcast.6), channel_id=1, replica_groups=mesh['tm'=16,'band'=2] {'band','tm'}, dimensions={0} | all-to-all | bytes 786432 | tf_op jit(solution)/shard_map/all_to_all | solution.py:450
  29.3 0.0 copy-done.5
  29.3 0.0 copy-done.9
  29.3 0.0 copy-done.3
  29.3 0.0 copy-done.4
  29.3 2.1 %shard_map.125 = f32[800,128]{1,0:T(8,128)} custom-call(f32[2,16,8,384]{3,2,1,0:T(8,128)S(1)} %bitcast.5, bf16[2,256,384]{2,1,0:T(8,128)(2,1)S(1)} %copy-done.4, bf16[2,384,256]{2,1,0:T(8,128)(2,1)S(1)} %copy-done.3, bf16[2,256,256]{2,1,0:T(8,128)(2,1)S(1)} %copy-done.9, bf16[2,272,256]{2,1,0:T(8,128)(2,1)S(1)} %copy-done.5), custom_call_target="tpu_custom_call" | custom-call | bytes 4194304 | tf_op jit(solution)/shard_map/pallas_call | solution.py:372
  31.4 3.0 %all-to-all-start.1 = ((f32[32,1,3200]{2,1,0:T(1,128)}), f32[32,1,3200]{2,1,0:T(1,128)S(1)}, u32[]{:S(2)}, u32[]{:S(2)}) async-start(f32[32,1,3200]{2,1,0:T(1,128)} %bitcast.2), calls=%async_computation.1 | async-start | bytes 819200 | tf_op jit(solution)/shard_map/all_to_all | solution.py:457
  34.4 0.0 copy-start.10
  34.4 0.5 collective-permute-start.1
  34.9 0.0 copy-start.8
  34.9 1.3 %collective-permute-start = (f32[1,128,256]{2,1,0:T(8,128)S(1)}, f32[1,128,256]{2,1,0:T(8,128)S(1)}, u32[]{:S(2)}, u32[]{:S(2)}) collective-permute-start(f32[1,128,256]{2,1,0:T(8,128)S(1)} %get-tuple-element.9), channel_id=1, source_target_pairs={{30,0},{31,1},{0,2},{1,3},{2,4},{3,5},{4,6},{5,7},{6,8},{7,9},{8,1... | collective-permute-start | bytes 393224 | tf_op jit(solution)/shard_map/ppermute | solution.py:45
  36.2 5.9 %collective-permute-done.1 = f32[1,128,256]{2,1,0:T(8,128)S(1)} collective-permute-done((f32[1,128,256]{2,1,0:T(8,128)S(1)}, f32[1,128,256]{2,1,0:T(8,128)S(1)}, u32[]{:S(2)}, u32[]{:S(2)}) %collective-permute-start.1) | collective-permute-done | bytes 131104 | tf_op jit(solution)/shard_map/ppermute | solution.py:45
  42.1 0.4 collective-permute-done
  42.5 0.0 copy-done.10
  42.5 0.1 fusion.3.base
  42.6 6.8 %all-to-all-done.1 = f32[32,1,3200]{2,1,0:T(1,128)S(1)} async-done(((f32[32,1,3200]{2,1,0:T(1,128)}), f32[32,1,3200]{2,1,0:T(1,128)S(1)}, u32[]{:S(2)}, u32[]{:S(2)}) %all-to-all-start.1) | async-done | bytes 409632 | tf_op jit(solution)/shard_map/all_to_all | solution.py:457
  49.4 0.0 copy-done.8
  49.4 1.9 %shard_map.126 = (f32[2,128,256]{2,1,0:T(8,128)}, f32[2,128,256]{2,1,0:T(8,128)}) custom-call(f32[2,128,256]{2,1,0:T(8,128)S(1)} %fusion.3.base, f32[2,128,256]{2,1,0:T(8,128)S(1)} %copy-done, s32[2,128,256]{2,1,0:T(8,128)S(1)} %copy-done.2, f32[6,8,256]{2,1,0:T(8,128)S(1)} %collective-permute-done.2.edges, f32[1,128,256]{2,1,0:T(8,128)S(1)} %collective-permute-done.3.after, ...), custom_call_target="tpu_custom_call" | custom-call | bytes 4194304 | tf_op jit(solution)/shard_map/pallas_call | solution.py:372
  (1 shorter events, 0.0 us)
Async XLA Ops:
  0.6 8.3 %copy-start.2 = (s32[2,128,256]{2,1,0:T(8,128)S(1)}, s32[2,128,256]{2,1,0:T(8,128)}, u32[]{:S(2)}) copy-start(s32[2,128,256]{2,1,0:T(8,128)} %bonds.5) | copy-start | bytes 786436
  0.6 8.3 %copy-start = (f32[2,128,256]{2,1,0:T(8,128)S(1)}, f32[2,128,256]{2,1,0:T(8,128)}, u32[]{:S(2)}) copy-start(f32[2,128,256]{2,1,0:T(8,128)} %guess.7) | copy-start | bytes 786436
  0.6 8.3 %copy-start.1 = (f32[2,128,256]{2,1,0:T(8,128)S(1)}, f32[2,128,256]{2,1,0:T(8,128)}, u32[]{:S(2)}) copy-start(f32[2,128,256]{2,1,0:T(8,128)} %phonon.1) | copy-start | bytes 786436
  1.8 8.0 %collective-permute-start.3 = (f32[1,128,256]{2,1,0:T(8,128)S(1)}, f32[1,128,256]{2,1,0:T(8,128)S(1)}, u32[]{:S(2)}, u32[]{:S(2)}) collective-permute-start(f32[1,128,256]{2,1,0:T(8,128)S(1)} %get-tuple-element.11), channel_id=1, source_target_pairs={{2,0},{3,1},{4,2},{5,3},{6,4},{7,5},{8,6},{9,7},{10,8},{11,9},{12,... | collective-permute-start | bytes 393224 | tf_op jit(solution)/shard_map/ppermute | solution.py:45
  1.8 7.9 %collective-permute-start.2 = (f32[6,8,256]{2,1,0:T(8,128)S(1)}, f32[6,8,256]{2,1,0:T(8,128)S(1)}, u32[]{:S(2)}, u32[]{:S(2)}) collective-permute-start(f32[6,8,256]{2,1,0:T(8,128)S(1)} %get-tuple-element.10), channel_id=1, source_target_pairs={{1,0},{0,1},{3,2},{2,3},{5,4},{4,5},{7,6},{6,7},{9,8},{8,9},{11,10... | collective-permute-start | bytes 147464 | tf_op jit(solution)/shard_map/ppermute | solution.py:45
  4.5 5.2 %copy-start.6 = (f32[2,128,256]{2,1,0:T(8,128)S(1)}, f32[2,128,256]{2,1,0:T(8,128)}, u32[]{:S(2)}) copy-start(f32[2,128,256]{2,1,0:T(8,128)} %source.1) | copy-start | bytes 786436
  4.5 5.2 %copy-start.7 = (bf16[2,256,256]{2,1,0:T(8,128)(2,1)S(1)}, bf16[2,256,256]{2,1,0:T(8,128)(2,1)}, u32[]{:S(2)}) copy-start(bf16[2,256,256]{2,1,0:T(8,128)(2,1)} %constant.18.clone.basis) | copy-start | bytes 786436
  4.5 5.2 %collective-permute-start.4 = (f32[1,8,256]{2,1,0:T(8,128)S(1)}, f32[1,8,256]{2,1,0:T(8,128)S(1)}, u32[]{:S(2)}, u32[]{:S(2)}) collective-permute-start(f32[1,8,256]{2,1,0:T(8,128)S(1)} %get-tuple-element.12), channel_id=1, source_target_pairs={{3,0},{2,1},{5,2},{4,3},{7,4},{6,5},{9,6},{8,7},{11,8},{10,9},{13,... | collective-permute-start | bytes 24584 | tf_op jit(solution)/shard_map/ppermute | solution.py:45
  9.8 19.6 %copy-start.5 = (bf16[2,272,256]{2,1,0:T(8,128)(2,1)S(1)}, bf16[2,272,256]{2,1,0:T(8,128)(2,1)}, u32[]{:S(2)}) copy-start(bf16[2,272,256]{2,1,0:T(8,128)(2,1)} %constant.22.clone.rows_out) | copy-start | bytes 835588
  9.8 19.5 %copy-start.9 = (bf16[2,256,256]{2,1,0:T(8,128)(2,1)S(1)}, bf16[2,256,256]{2,1,0:T(8,128)(2,1)}, u32[]{:S(2)}) copy-start(bf16[2,256,256]{2,1,0:T(8,128)(2,1)} %constant.21.clone.rows_in) | copy-start | bytes 786436
  10.7 18.6 %copy-start.3 = (bf16[2,384,256]{2,1,0:T(8,128)(2,1)S(1)}, bf16[2,384,256]{2,1,0:T(8,128)(2,1)}, u32[]{:S(2)}) copy-start(bf16[2,384,256]{2,1,0:T(8,128)(2,1)} %constant.20.clone.slices_out) | copy-start | bytes 1179652
  10.7 18.6 %copy-start.4 = (bf16[2,256,384]{2,1,0:T(8,128)(2,1)S(1)}, bf16[2,256,384]{2,1,0:T(8,128)(2,1)}, u32[]{:S(2)}) copy-start(bf16[2,256,384]{2,1,0:T(8,128)(2,1)} %constant.19.clone.slices_in) | copy-start | bytes 1179652
  31.4 18.0 %all-to-all-start.1 = ((f32[32,1,3200]{2,1,0:T(1,128)}), f32[32,1,3200]{2,1,0:T(1,128)S(1)}, u32[]{:S(2)}, u32[]{:S(2)}) async-start(f32[32,1,3200]{2,1,0:T(1,128)} %bitcast.2), calls=%async_computation.1 | async-start | bytes 819200 | tf_op jit(solution)/shard_map/all_to_all | solution.py:457
  34.4 8.2 %copy-start.10 = (f32[2,128,256]{2,1,0:T(8,128)S(1)}, f32[2,128,256]{2,1,0:T(8,128)}, u32[]{:S(2)}) copy-start(f32[2,128,256]{2,1,0:T(8,128)} %param.12) | copy-start | bytes 786436
  34.4 7.7 %collective-permute-start.1 = (f32[1,128,256]{2,1,0:T(8,128)S(1)}, f32[1,128,256]{2,1,0:T(8,128)S(1)}, u32[]{:S(2)}, u32[]{:S(2)}) collective-permute-start(f32[1,128,256]{2,1,0:T(8,128)S(1)} %slice.12), channel_id=1, source_target_pairs={{2,0},{3,1},{4,2},{5,3},{6,4},{7,5},{8,6},{9,7},{10,8},{11,9},{12,... | collective-permute-start | bytes 393224 | tf_op jit(solution)/shard_map/ppermute | solution.py:45
  34.9 14.6 %copy-start.8 = (bf16[2,256,256]{2,1,0:T(8,128)(2,1)S(1)}, bf16[2,256,256]{2,1,0:T(8,128)(2,1)}, u32[]{:S(2)}) copy-start(bf16[2,256,256]{2,1,0:T(8,128)(2,1)} %constant.23.clone.order) | copy-start | bytes 786436
  34.9 7.7 %collective-permute-start = (f32[1,128,256]{2,1,0:T(8,128)S(1)}, f32[1,128,256]{2,1,0:T(8,128)S(1)}, u32[]{:S(2)}, u32[]{:S(2)}) collective-permute-start(f32[1,128,256]{2,1,0:T(8,128)S(1)} %get-tuple-element.9), channel_id=1, source_target_pairs={{30,0},{31,1},{0,2},{1,3},{2,4},{3,5},{4,6},{5,7},{6,8},{7,9},{8,1... | collective-permute-start | bytes 393224 | tf_op jit(solution)/shard_map/ppermute | solution.py:45

commit v10 on v9

--- a/solution.py
+++ b/solution.py
@@ -250,6 +250,7 @@
 
 def residual_kernel(source, guess, bonds, edges, after, after_edge, expo, tables, inner, basis, out):
     slices, rows, cols = guess.shape
+    edges = unpaired(edges)
     band = Band(bonds, edges, expo, tables, slices)
     field = with_following(guess, edges, after, after_edge)
     pieces = []
@@ -335,6 +336,7 @@
     modes = cols // devices
     slots = slices + 1
     chunk = slots * modes + 1
+    edges = unpaired(edges)
     band = Band(bonds, edges, expo, tables, slices)
 
     rim = mixed[pl.ds(slots * modes, devices, stride=chunk), :]
@@ -384,6 +386,23 @@
     return pltpu.with_memory_space_constraint(value, pltpu.VMEM)
 
 
+def paired(one, two):
+    row = lax.broadcasted_iota(jnp.int32, one.shape, 0)
+    mine = jnp.where(row < EDGE, one, pltpu.roll(one, HALO - NEAR, 0))
+    other = jnp.where(row < EDGE, pltpu.roll(two, NEAR, 0), two)
+    return jnp.where((row & NEAR) == 0, mine, other)
+
+
+def unpaired(edges):
+    row = lax.broadcasted_iota(jnp.int32, edges.shape[1:], 0)
+    tiles = []
+    for i in range(edges.shape[0]):
+        tile = edges[i]
+        tiles.append(jnp.where(row < EDGE, tile, pltpu.roll(tile, NEAR, 0)))
+        tiles.append(jnp.where(row < EDGE, pltpu.roll(tile, HALO - NEAR, 0), tile))
+    return tiles
+
+
 def pack_kernel(guess, *refs):
     last_ph, tops, ends, outs = refs[0], refs[1:4], refs[4:7], refs[7:]
     first, last, rims, rim = outs
@@ -393,10 +412,11 @@
     at = 0
     for top, end in zip(tops, ends):
         both = jnp.where(early, top[...], end[...]).astype(jnp.float32)
-        rims[at : at + top.shape[0]] = both
         if at == 0:
             rim[...] = both[:1]
-        at += top.shape[0]
+        for s in range(0, both.shape[0], 2):
+            rims[at] = paired(both[s], both[s + 1])
+            at += 1
 
 
 def pack(phonon, guess, bonds):
@@ -406,7 +426,7 @@
     whole = lambda shape: pl.BlockSpec(shape, lambda i: (0, 0, 0))
     tops = [whole((v.shape[0], HALO, cols)) for v in fields]
     ends = [pl.BlockSpec((v.shape[0], HALO, cols), lambda i: (0, last, 0)) for v in fields]
-    outs = [(1, rows, cols), (1, rows, cols), (2 * slices + 2, HALO, cols), (1, HALO, cols)]
+    outs = [(1, rows, cols), (1, rows, cols), (slices + 1, HALO, cols), (1, HALO, cols)]
     final = pl.BlockSpec((1, rows, cols), lambda i: (slices - 1, 0, 0))
     return pl.pallas_call(
         pack_kernel,

time: 51.6 us -> 51.5 us (level)
  no operation moved by 1% of the time
where the time goes in v10:
time: 51.5 us; the launch traced here: 51.2 us
  blocking collectives  18.6 us (36%)
  waiting for transfers between devices  13.5 us (26%)
  starting transfers between devices  11.9 us (23%)
  Pallas kernels  6.3 us (12%)
  between operations  0.77 us (1%)
    all_to_all x1, blocking collectives, shards(): lax.all_to_all(sent.reshape(devices, modes, slots * rows), EXCHANGE, 0, 0...  18.6 us
    ppermute x5, starting transfers between devices, shifted(): return lax.ppermute(value, AXES, pairs)  8.97 us
    all_to_all x1, waiting for transfers between devices, shards(): mixed = lax.all_to_all(back.reshape(devices, 1, -1), AXES, 0, 0, tiled=True)  6.81 us
    ppermute x5, waiting for transfers between devices, shifted(): return lax.ppermute(value, AXES, pairs)  6.71 us
    pallas_call x4, Pallas kernels, call(): pl.pallas_call(kernel, out_shape=outs, in_specs=[vmem] * len(operands), o...  5.2 us
    all_to_all x1, starting transfers between devices, shards(): mixed = lax.all_to_all(back.reshape(devices, 1, -1), AXES, 0, 0, tiled=True)  2.96 us
    pallas_call x1, Pallas kernels, pack(): pl.pallas_call(pack_kernel, grid=(1,), out_shape=[pltpu.VMEM(o, jnp.float...  1.1 us
  transfers between devices with their start and end apart: 6, of which 4 were waited for; matrix products, arithmetic and copies ran while one was open for 0% of the time, Pallas kernels for 1%

profile of v10, /device:TPU:1, one launch (start us, length us, event | category | flops | bytes accessed | tf_op | source)
XLA Modules:
  0.0 51.2 jit_solution(12556930264662094845)
XLA Ops:
  0.6 0.0 copy-start.2
  0.6 0.0 copy-start
  0.6 0.0 copy-start.1
  0.7 1.1 %shard_map.122 = (f32[1,128,256]{2,1,0:T(8,128)S(1)}, f32[1,128,256]{2,1,0:T(8,128)S(1)}, f32[3,8,256]{2,1,0:T(8,128)S(1)}, f32[1,8,256]{2,1,0:T(8,128)S(1)}) custom-call(f32[2,128,256]{2,1,0:T(8,128)} %guess.7, f32[2,128,256]{2,1,0:T(8,128)} %phonon.1, f32[2,128,256]{2,1,0:T(8,128)} %guess.7, f32[2,128,256]{2,1,0:T(8,128)} %phonon.1, s32[2,128,256]{2,1,0:T(8,128)} %bonds.5, ...), custom_call_target="tpu_custom_call" | custom-call | tf_op jit(solution)/shard_map/pallas_call | solution.py:431
  1.8 0.1 collective-permute-start.3
  1.8 2.7 %collective-permute-start.2 = (f32[3,8,256]{2,1,0:T(8,128)S(1)}, f32[3,8,256]{2,1,0:T(8,128)S(1)}, u32[]{:S(2)}, u32[]{:S(2)}) collective-permute-start(f32[3,8,256]{2,1,0:T(8,128)S(1)} %get-tuple-element.10), channel_id=1, source_target_pairs={{1,0},{0,1},{3,2},{2,3},{5,4},{4,5},{7,6},{6,7},{9,8},{8,9},{11,10... | collective-permute-start | bytes 73736 | tf_op jit(solution)/shard_map/ppermute | solution.py:45
  4.5 0.0 copy-start.6
  4.5 0.0 copy-start.7
  4.5 4.4 %collective-permute-start.4 = (f32[1,8,256]{2,1,0:T(8,128)S(1)}, f32[1,8,256]{2,1,0:T(8,128)S(1)}, u32[]{:S(2)}, u32[]{:S(2)}) collective-permute-start(f32[1,8,256]{2,1,0:T(8,128)S(1)} %get-tuple-element.12), channel_id=1, source_target_pairs={{3,0},{2,1},{5,2},{4,3},{7,4},{6,5},{9,6},{8,7},{11,8},{10,9},{13,... | collective-permute-start | bytes 24584 | tf_op jit(solution)/shard_map/ppermute | solution.py:45
  8.9 0.0 copy-done.2
  9.0 0.0 copy-done
  9.0 0.0 copy-done.1
  9.0 0.4 shard_map.123
  9.4 0.4 collective-permute-done.4.after_edge
  9.7 0.0 collective-permute-done.2.edges
  9.7 0.0 collective-permute-done.3.after
  9.7 0.0 copy-done.6
  9.8 0.0 copy-done.7
  9.8 0.0 copy-start.5
  9.8 0.0 copy-start.9
  9.8 0.9 %shard_map.124 = f32[256,384]{1,0:T(8,128)S(1)} custom-call(f32[2,128,256]{2,1,0:T(8,128)S(1)} %copy-done.6, f32[2,128,256]{2,1,0:T(8,128)S(1)} %copy-done, s32[2,128,256]{2,1,0:T(8,128)S(1)} %copy-done.2, f32[3,8,256]{2,1,0:T(8,128)S(1)} %collective-permute-done.2.edges, f32[1,128,256]{2,1,0:T(8,128)S(1)} %collective-permute-done.3.after, ...), custom_call_target="tpu_custom_call" | custom-call | bytes 4194304 | tf_op jit(solution)/shard_map/pallas_call | solution.py:374
  10.7 0.0 copy-start.3
  10.7 0.0 copy-start.4
  10.7 18.6 %all_to_all.10 = f32[32,8,384]{2,1,0:T(8,128)S(1)} all-to-all(f32[32,8,384]{2,1,0:T(8,128)S(1)} %bitcast.6), channel_id=1, replica_groups=mesh['tm'=16,'band'=2] {'band','tm'}, dimensions={0} | all-to-all | bytes 786432 | tf_op jit(solution)/shard_map/all_to_all | solution.py:470
  29.3 0.0 copy-done.5
  29.3 0.0 copy-done.9
  29.3 0.0 copy-done.3
  29.3 0.0 copy-done.4
  29.3 2.1 %shard_map.125 = f32[800,128]{1,0:T(8,128)} custom-call(f32[2,16,8,384]{3,2,1,0:T(8,128)S(1)} %bitcast.5, bf16[2,256,384]{2,1,0:T(8,128)(2,1)S(1)} %copy-done.4, bf16[2,384,256]{2,1,0:T(8,128)(2,1)S(1)} %copy-done.3, bf16[2,256,256]{2,1,0:T(8,128)(2,1)S(1)} %copy-done.9, bf16[2,272,256]{2,1,0:T(8,128)(2,1)S(1)} %copy-done.5), custom_call_target="tpu_custom_call" | custom-call | bytes 4194304 | tf_op jit(solution)/shard_map/pallas_call | solution.py:374
  31.4 3.0 %all-to-all-start.1 = ((f32[32,1,3200]{2,1,0:T(1,128)}), f32[32,1,3200]{2,1,0:T(1,128)S(1)}, u32[]{:S(2)}, u32[]{:S(2)}) async-start(f32[32,1,3200]{2,1,0:T(1,128)} %bitcast.2), calls=%async_computation.1 | async-start | bytes 819200 | tf_op jit(solution)/shard_map/all_to_all | solution.py:477
  34.3 0.0 copy-start.10
  34.4 0.5 collective-permute-start.1
  34.8 0.0 copy-start.8
  34.8 1.3 %collective-permute-start = (f32[1,128,256]{2,1,0:T(8,128)S(1)}, f32[1,128,256]{2,1,0:T(8,128)S(1)}, u32[]{:S(2)}, u32[]{:S(2)}) collective-permute-start(f32[1,128,256]{2,1,0:T(8,128)S(1)} %get-tuple-element.9), channel_id=1, source_target_pairs={{30,0},{31,1},{0,2},{1,3},{2,4},{3,5},{4,6},{5,7},{6,8},{7,9},{8,1... | collective-permute-start | bytes 393224 | tf_op jit(solution)/shard_map/ppermute | solution.py:45
  36.2 5.9 %collective-permute-done.1 = f32[1,128,256]{2,1,0:T(8,128)S(1)} collective-permute-done((f32[1,128,256]{2,1,0:T(8,128)S(1)}, f32[1,128,256]{2,1,0:T(8,128)S(1)}, u32[]{:S(2)}, u32[]{:S(2)}) %collective-permute-start.1) | collective-permute-done | bytes 131104 | tf_op jit(solution)/shard_map/ppermute | solution.py:45
  42.1 0.4 collective-permute-done
  42.5 0.0 copy-done.10
  42.5 0.1 fusion.3.base
  42.6 6.8 %all-to-all-done.1 = f32[32,1,3200]{2,1,0:T(1,128)S(1)} async-done(((f32[32,1,3200]{2,1,0:T(1,128)}), f32[32,1,3200]{2,1,0:T(1,128)S(1)}, u32[]{:S(2)}, u32[]{:S(2)}) %all-to-all-start.1) | async-done | bytes 409632 | tf_op jit(solution)/shard_map/all_to_all | solution.py:477
  49.4 0.0 copy-done.8
  49.4 1.9 %shard_map.126 = (f32[2,128,256]{2,1,0:T(8,128)}, f32[2,128,256]{2,1,0:T(8,128)}) custom-call(f32[2,128,256]{2,1,0:T(8,128)S(1)} %fusion.3.base, f32[2,128,256]{2,1,0:T(8,128)S(1)} %copy-done, s32[2,128,256]{2,1,0:T(8,128)S(1)} %copy-done.2, f32[3,8,256]{2,1,0:T(8,128)S(1)} %collective-permute-done.2.edges, f32[1,128,256]{2,1,0:T(8,128)S(1)} %collective-permute-done.3.after, ...), custom_call_target="tpu_custom_call" | custom-call | bytes 4194304 | tf_op jit(solution)/shard_map/pallas_call | solution.py:374
  (1 shorter events, 0.0 us)
Async XLA Ops:
  0.6 8.3 %copy-start.2 = (s32[2,128,256]{2,1,0:T(8,128)S(1)}, s32[2,128,256]{2,1,0:T(8,128)}, u32[]{:S(2)}) copy-start(s32[2,128,256]{2,1,0:T(8,128)} %bonds.5) | copy-start | bytes 786436
  0.6 8.3 %copy-start = (f32[2,128,256]{2,1,0:T(8,128)S(1)}, f32[2,128,256]{2,1,0:T(8,128)}, u32[]{:S(2)}) copy-start(f32[2,128,256]{2,1,0:T(8,128)} %guess.7) | copy-start | bytes 786436
  0.6 8.3 %copy-start.1 = (f32[2,128,256]{2,1,0:T(8,128)S(1)}, f32[2,128,256]{2,1,0:T(8,128)}, u32[]{:S(2)}) copy-start(f32[2,128,256]{2,1,0:T(8,128)} %phonon.1) | copy-start | bytes 786436
  1.8 8.0 %collective-permute-start.3 = (f32[1,128,256]{2,1,0:T(8,128)S(1)}, f32[1,128,256]{2,1,0:T(8,128)S(1)}, u32[]{:S(2)}, u32[]{:S(2)}) collective-permute-start(f32[1,128,256]{2,1,0:T(8,128)S(1)} %get-tuple-element.11), channel_id=1, source_target_pairs={{2,0},{3,1},{4,2},{5,3},{6,4},{7,5},{8,6},{9,7},{10,8},{11,9},{12,... | collective-permute-start | bytes 393224 | tf_op jit(solution)/shard_map/ppermute | solution.py:45
  1.8 7.9 %collective-permute-start.2 = (f32[3,8,256]{2,1,0:T(8,128)S(1)}, f32[3,8,256]{2,1,0:T(8,128)S(1)}, u32[]{:S(2)}, u32[]{:S(2)}) collective-permute-start(f32[3,8,256]{2,1,0:T(8,128)S(1)} %get-tuple-element.10), channel_id=1, source_target_pairs={{1,0},{0,1},{3,2},{2,3},{5,4},{4,5},{7,6},{6,7},{9,8},{8,9},{11,10... | collective-permute-start | bytes 73736 | tf_op jit(solution)/shard_map/ppermute | solution.py:45
  4.5 5.2 %copy-start.6 = (f32[2,128,256]{2,1,0:T(8,128)S(1)}, f32[2,128,256]{2,1,0:T(8,128)}, u32[]{:S(2)}) copy-start(f32[2,128,256]{2,1,0:T(8,128)} %source.1) | copy-start | bytes 786436
  4.5 5.2 %copy-start.7 = (bf16[2,256,256]{2,1,0:T(8,128)(2,1)S(1)}, bf16[2,256,256]{2,1,0:T(8,128)(2,1)}, u32[]{:S(2)}) copy-start(bf16[2,256,256]{2,1,0:T(8,128)(2,1)} %constant.18.clone.basis) | copy-start | bytes 786436
  4.5 5.2 %collective-permute-start.4 = (f32[1,8,256]{2,1,0:T(8,128)S(1)}, f32[1,8,256]{2,1,0:T(8,128)S(1)}, u32[]{:S(2)}, u32[]{:S(2)}) collective-permute-start(f32[1,8,256]{2,1,0:T(8,128)S(1)} %get-tuple-element.12), channel_id=1, source_target_pairs={{3,0},{2,1},{5,2},{4,3},{7,4},{6,5},{9,6},{8,7},{11,8},{10,9},{13,... | collective-permute-start | bytes 24584 | tf_op jit(solution)/shard_map/ppermute | solution.py:45
  9.8 19.5 %copy-start.5 = (bf16[2,272,256]{2,1,0:T(8,128)(2,1)S(1)}, bf16[2,272,256]{2,1,0:T(8,128)(2,1)}, u32[]{:S(2)}) copy-start(bf16[2,272,256]{2,1,0:T(8,128)(2,1)} %constant.22.clone.rows_out) | copy-start | bytes 835588
  9.8 19.5 %copy-start.9 = (bf16[2,256,256]{2,1,0:T(8,128)(2,1)S(1)}, bf16[2,256,256]{2,1,0:T(8,128)(2,1)}, u32[]{:S(2)}) copy-start(bf16[2,256,256]{2,1,0:T(8,128)(2,1)} %constant.21.clone.rows_in) | copy-start | bytes 786436
  10.7 18.6 %copy-start.3 = (bf16[2,384,256]{2,1,0:T(8,128)(2,1)S(1)}, bf16[2,384,256]{2,1,0:T(8,128)(2,1)}, u32[]{:S(2)}) copy-start(bf16[2,384,256]{2,1,0:T(8,128)(2,1)} %constant.20.clone.slices_out) | copy-start | bytes 1179652
  10.7 18.6 %copy-start.4 = (bf16[2,256,384]{2,1,0:T(8,128)(2,1)S(1)}, bf16[2,256,384]{2,1,0:T(8,128)(2,1)}, u32[]{:S(2)}) copy-start(bf16[2,256,384]{2,1,0:T(8,128)(2,1)} %constant.19.clone.slices_in) | copy-start | bytes 1179652
  31.4 18.0 %all-to-all-start.1 = ((f32[32,1,3200]{2,1,0:T(1,128)}), f32[32,1,3200]{2,1,0:T(1,128)S(1)}, u32[]{:S(2)}, u32[]{:S(2)}) async-start(f32[32,1,3200]{2,1,0:T(1,128)} %bitcast.2), calls=%async_computation.1 | async-start | bytes 819200 | tf_op jit(solution)/shard_map/all_to_all | solution.py:477
  34.3 8.2 %copy-start.10 = (f32[2,128,256]{2,1,0:T(8,128)S(1)}, f32[2,128,256]{2,1,0:T(8,128)}, u32[]{:S(2)}) copy-start(f32[2,128,256]{2,1,0:T(8,128)} %param.12) | copy-start | bytes 786436
  34.4 7.7 %collective-permute-start.1 = (f32[1,128,256]{2,1,0:T(8,128)S(1)}, f32[1,128,256]{2,1,0:T(8,128)S(1)}, u32[]{:S(2)}, u32[]{:S(2)}) collective-permute-start(f32[1,128,256]{2,1,0:T(8,128)S(1)} %slice.12), channel_id=1, source_target_pairs={{2,0},{3,1},{4,2},{5,3},{6,4},{7,5},{8,6},{9,7},{10,8},{11,9},{12,... | collective-permute-start | bytes 393224 | tf_op jit(solution)/shard_map/ppermute | solution.py:45
  34.8 14.6 %copy-start.8 = (bf16[2,256,256]{2,1,0:T(8,128)(2,1)S(1)}, bf16[2,256,256]{2,1,0:T(8,128)(2,1)}, u32[]{:S(2)}) copy-start(bf16[2,256,256]{2,1,0:T(8,128)(2,1)} %constant.23.clone.order) | copy-start | bytes 786436
  34.8 7.7 %collective-permute-start = (f32[1,128,256]{2,1,0:T(8,128)S(1)}, f32[1,128,256]{2,1,0:T(8,128)S(1)}, u32[]{:S(2)}, u32[]{:S(2)}) collective-permute-start(f32[1,128,256]{2,1,0:T(8,128)S(1)} %get-tuple-element.9), channel_id=1, source_target_pairs={{30,0},{31,1},{0,2},{1,3},{2,4},{3,5},{4,6},{5,7},{6,8},{7,9},{8,1... | collective-permute-start | bytes 393224 | tf_op jit(solution)/shard_map/ppermute | solution.py:45
